TPU v7x, 32 devices: a whole 2x2x4 slice. The times are simulated.
32 devices in a mesh: img: 16 (over z, y, core), seq: 2 (over x).
Axes of the slice: x: 2, y: 2, z: 4, core: 2. Of those that a mesh axis runs over, the one named last changes fastest.
Arguments:
- tokens: bfloat16 [4096, 768], P(('img', 'seq')), may hold values from -6 to 6
- cotangent: bfloat16 [4096, 768], P(('img', 'seq')), may hold values from -6 to 6
- counts: int32 [16], P('img'), may hold values from 129 to 256, as said below
- widths: int32 [16], P('img'), may hold values from 16 to 32
- norm1_gain: bfloat16 [768], P(('img', 'seq')), may hold values from 0.5 to 1.5
- norm1_shift: bfloat16 [768], P(('img', 'seq')), may hold values from -1.75 to 1.75
- w_qkv: bfloat16 [768, 2304], P(('img', 'seq')), may hold values from -0.3125 to 0.3125
- q_bias: bfloat16 [768], P(('img', 'seq')), may hold values from -1.75 to 1.75
- v_bias: bfloat16 [768], P(('img', 'seq')), may hold values from -1.75 to 1.75
- w_proj: bfloat16 [768, 768], P(('img', 'seq')), may hold values from -0.875 to 0.875
- proj_bias: bfloat16 [768], P(('img', 'seq')), may hold values from -1.75 to 1.75
- gamma1: bfloat16 [768], P(('img', 'seq')), may hold values from 0.5 to 2
- norm2_gain: bfloat16 [768], P(('img', 'seq')), may hold values from 0.5 to 1.5
- norm2_shift: bfloat16 [768], P(('img', 'seq')), may hold values from -1.75 to 1.75
- w_fc1: bfloat16 [768, 3072], P(('img', 'seq')), may hold values from -0.21875 to 0.21875
- fc1_bias: bfloat16 [3072], P(('img', 'seq')), may hold values from -1.75 to 1.75
- w_fc2: bfloat16 [3072, 768], P(('img', 'seq')), may hold values from -0.109375 to 0.109375
- fc2_bias: bfloat16 [768], P(('img', 'seq')), may hold values from -1.75 to 1.75
- gamma2: bfloat16 [768], P(('img', 'seq')), may hold values from 0.5 to 2
- bias_table: bfloat16 [1953, 12], replicated, may hold values from -6 to 6
Outputs:
- output: bfloat16 [4096, 768], P(('img', 'seq'))
- grad_tokens: bfloat16 [4096, 768], P(('img', 'seq'))
- grad_norm1_gain: float32 [768], P(('img', 'seq'))
- grad_norm1_shift: float32 [768], P(('img', 'seq'))
- grad_w_qkv: float32 [768, 2304], P(('img', 'seq'))
- grad_q_bias: float32 [768], P(('img', 'seq'))
- grad_v_bias: float32 [768], P(('img', 'seq'))
- grad_w_proj: float32 [768, 768], P(('img', 'seq'))
- grad_proj_bias: float32 [768], P(('img', 'seq'))
- grad_gamma1: float32 [768], P(('img', 'seq'))
- grad_norm2_gain: float32 [768], P(('img', 'seq'))
- grad_norm2_shift: float32 [768], P(('img', 'seq'))
- grad_w_fc1: float32 [768, 3072], P(('img', 'seq'))
- grad_fc1_bias: float32 [3072], P(('img', 'seq'))
- grad_w_fc2: float32 [3072, 768], P(('img', 'seq'))
- grad_fc2_bias: float32 [768], P(('img', 'seq'))
- grad_gamma2: float32 [768], P(('img', 'seq'))
- grad_bias_table: float32 [1953, 12], replicated
Inputs may be any that keep to these rules, and one draw needn't show every extreme that they name: Image g's patches are positions 0 to counts[g] - 1 of its 256; the rest are padding. Some image has all 256 positions and some exactly 129.
All inputs are finite; a program needn't handle non-finite values.
Results may differ from a plain program's by a relative error of at most 0.014.
The roundings to bfloat16 on the way count: a program that leaves them out, or rounds other values in their place, can miss the bound.
Values may be sent and summed in bfloat16 or wider, within the bound.
A program may use at most 128 MiB of HBM per device.

v0:
```python
from functools import partial

import jax
import jax.numpy as jnp
from jax import lax
from jax.sharding import PartitionSpec as P

HEADS = 12
HEAD_DIM = 64
SIDE = 32


EPSILON = 1e-06
NEG_FILL = -1e30


def layer_norm(values, gain, shift):
    centred = values - jnp.mean(values, axis=-1, keepdims=True)
    inv_std = lax.rsqrt(jnp.mean(centred * centred, axis=-1, keepdims=True) + EPSILON)
    normed = centred * inv_std
    return (normed * gain + shift, normed, inv_std)


def norm_back(grad_out, normed, inv_std, gain):
    scaled = grad_out * gain
    return inv_std * (
        scaled
        - jnp.mean(scaled, axis=-1, keepdims=True)
        - normed * jnp.mean(scaled * normed, axis=-1, keepdims=True)
    )


def pair_probs(query_pair, key_pair, table_pair, rel_index, key_valid):
    product = jnp.einsum("qhd,khd->hqk", query_pair, key_pair, preferred_element_type=jnp.float32)
    scores = product * HEAD_DIM ** (-0.5) + jnp.take(table_pair, rel_index, axis=1)
    scores = jnp.where(key_valid[None, None, :], scores, NEG_FILL)
    top_val = jnp.max(scores, axis=-1, keepdims=True)
    exp_terms = jnp.where(key_valid[None, None, :], jnp.exp(scores - top_val), 0.0)
    return exp_terms / jnp.sum(exp_terms, axis=-1, keepdims=True)


def row_sum(values):
    return jnp.sum(values.astype(jnp.float32), axis=0)


def diagonal_sums(values):
    query_count = values.shape[0]
    key_count = values.shape[1]
    flipped = values[:, ::-1]
    padded = jnp.pad(flipped, ((0, 0), (0, query_count)))
    flat = padded.reshape(-1)[: query_count * (key_count + query_count - 1)]
    return jnp.sum(flat.reshape(query_count, key_count + query_count - 1), axis=0)


def per_device(
    tokens,
    cotangent,
    counts,
    widths,
    norm1_gain,
    norm1_shift,
    w_qkv,
    q_bias,
    v_bias,
    w_proj,
    proj_bias,
    gamma1,
    norm2_gain,
    norm2_shift,
    w_fc1,
    fc1_bias,
    w_fc2,
    fc2_bias,
    gamma2,
    bias_table,
):
    fetched = (
        lax.all_gather(norm1_gain, ("img", "seq"), axis=0, tiled=True),
        lax.all_gather(norm1_shift, ("img", "seq"), axis=0, tiled=True),
        lax.all_gather(w_qkv, ("img", "seq"), axis=0, tiled=True),
        lax.all_gather(q_bias, ("img", "seq"), axis=0, tiled=True),
        lax.all_gather(v_bias, ("img", "seq"), axis=0, tiled=True),
        lax.all_gather(w_proj, ("img", "seq"), axis=0, tiled=True),
        lax.all_gather(proj_bias, ("img", "seq"), axis=0, tiled=True),
        lax.all_gather(gamma1, ("img", "seq"), axis=0, tiled=True),
        lax.all_gather(norm2_gain, ("img", "seq"), axis=0, tiled=True),
        lax.all_gather(norm2_shift, ("img", "seq"), axis=0, tiled=True),
        lax.all_gather(w_fc1, ("img", "seq"), axis=0, tiled=True),
        lax.all_gather(fc1_bias, ("img", "seq"), axis=0, tiled=True),
        lax.all_gather(w_fc2, ("img", "seq"), axis=0, tiled=True),
        lax.all_gather(fc2_bias, ("img", "seq"), axis=0, tiled=True),
        lax.all_gather(gamma2, ("img", "seq"), axis=0, tiled=True),
    )
    (
        gain_one,
        shift_one,
        qkv_weight,
        query_bias,
        value_bias,
        proj_weight,
        proj_shift,
        scale_one,
        gain_two,
        shift_two,
        fc1_weight,
        fc1_shift,
        fc2_weight,
        fc2_shift,
        scale_two,
    ) = fetched
    gain_one = gain_one.astype(jnp.float32)
    shift_one = shift_one.astype(jnp.float32)
    proj_shift = proj_shift.astype(jnp.float32)
    scale_one = scale_one.astype(jnp.float32)
    gain_two = gain_two.astype(jnp.float32)
    shift_two = shift_two.astype(jnp.float32)
    fc1_shift = fc1_shift.astype(jnp.float32)
    fc2_shift = fc2_shift.astype(jnp.float32)
    scale_two = scale_two.astype(jnp.float32)
    local_rows = tokens.shape[0]
    width_model = tokens.shape[1]
    seq_len = local_rows * lax.axis_size("seq")
    offset = lax.axis_index("seq") * local_rows
    image_width = widths[0]
    places = jnp.arange(seq_len, dtype=jnp.int32)
    grid_row = places // image_width
    grid_col = places % image_width
    key_valid = places < counts[0]
    query_row = lax.dynamic_slice_in_dim(grid_row, offset, local_rows)
    query_col = lax.dynamic_slice_in_dim(grid_col, offset, local_rows)
    row_span = (seq_len - 1) // (SIDE // 2) + 1
    rel_index = (query_row[:, None] - grid_row[None, :] + row_span - 1) * (2 * SIDE - 1) + (
        query_col[:, None] - grid_col[None, :] + SIDE - 1
    )
    same_side = (query_col[:, None] >= grid_col[None, :]).astype(jnp.float32)
    table_rows = bias_table.shape[0]
    table_heads = bias_table.astype(jnp.float32).T
    pair_cols = 2 * HEAD_DIM
    pair_count = HEADS // 2
    span_len = seq_len + local_rows - 1
    offsets = jnp.arange(span_len, dtype=jnp.int32) - (seq_len - 1) + offset
    row_left = jnp.floor_divide(offsets, image_width)
    col_left = offsets - row_left * image_width
    row_right = row_left + 1
    col_right = col_left - image_width
    index_left = (row_left + row_span - 1) * (2 * SIDE - 1) + col_left + SIDE - 1
    index_right = (row_right + row_span - 1) * (2 * SIDE - 1) + col_right + SIDE - 1
    fits_left = jnp.abs(row_left) <= row_span - 1
    fits_right = (jnp.abs(row_right) <= row_span - 1) & (col_right > -image_width)
    index_left = jnp.where(fits_left, index_left, table_rows)
    index_right = jnp.where(fits_right, index_right, table_rows)
    diag_index = jnp.concatenate([index_left, index_right])

    def pick_pair(source, start_col, pair_index, row_count):
        columns = lax.dynamic_slice_in_dim(source, start_col + pair_index * pair_cols, pair_cols, 1)
        return columns.reshape(row_count, 2, HEAD_DIM)

    def merge_pairs(stacked, row_count):
        return stacked.transpose(1, 0, 2).reshape(row_count, width_model)

    inputs_f = tokens.astype(jnp.float32)
    normed_full, normed_one, inv_std_one = layer_norm(inputs_f, gain_one, shift_one)
    normed_low = normed_full.astype(jnp.bfloat16)
    qkv_shift = jnp.concatenate(
        [query_bias, jnp.zeros((width_model,), jnp.bfloat16), value_bias]
    ).astype(jnp.float32)
    projected = (
        jnp.dot(normed_low, qkv_weight, preferred_element_type=jnp.float32) + qkv_shift
    ).astype(jnp.bfloat16)
    queries = projected[:, :width_model]
    key_local = projected[:, width_model:]
    keys_all = lax.all_gather(key_local, "seq", axis=0, tiled=True)

    def attend(pair_index):
        query_pair = pick_pair(queries, 0, pair_index, local_rows)
        key_pair = pick_pair(keys_all, 0, pair_index, seq_len)
        value_pair = pick_pair(keys_all, width_model, pair_index, seq_len)
        table_pair = lax.dynamic_slice_in_dim(table_heads, 2 * pair_index, 2, 0)
        probs = pair_probs(query_pair, key_pair, table_pair, rel_index, key_valid)
        mixed = jnp.einsum(
            "hqk,khd->qhd",
            probs.astype(jnp.bfloat16),
            value_pair,
            preferred_element_type=jnp.float32,
        )
        return mixed.reshape(local_rows, pair_cols)

    attn_low = merge_pairs(lax.map(attend, jnp.arange(pair_count)), local_rows).astype(jnp.bfloat16)
    branch_one = jnp.dot(attn_low, proj_weight, preferred_element_type=jnp.float32) + proj_shift
    residual_one = inputs_f + scale_one * branch_one
    normed_full_two, normed_two, inv_std_two = layer_norm(residual_one, gain_two, shift_two)
    normed_low_two = normed_full_two.astype(jnp.bfloat16)
    pre_act = jnp.dot(normed_low_two, fc1_weight, preferred_element_type=jnp.float32) + fc1_shift
    activated, gelu_pull = jax.vjp(partial(jax.nn.gelu, approximate=False), pre_act)
    hidden = activated.astype(jnp.bfloat16)
    branch_two = jnp.dot(hidden, fc2_weight, preferred_element_type=jnp.float32) + fc2_shift
    output = (residual_one + scale_two * branch_two).astype(jnp.bfloat16)
    grad_out = cotangent.astype(jnp.float32)
    grad_scale_two = jnp.sum(grad_out * branch_two, axis=0)
    grad_branch_two = (scale_two * grad_out).astype(jnp.bfloat16)
    grad_fc2_weight = jnp.einsum(
        "tf,td->fd", hidden, grad_branch_two, preferred_element_type=jnp.float32
    )
    grad_fc2_shift = row_sum(grad_branch_two)
    grad_hidden = jnp.einsum(
        "td,fd->tf", grad_branch_two, fc2_weight, preferred_element_type=jnp.float32
    )
    grad_pre = gelu_pull(grad_hidden)[0].astype(jnp.bfloat16)
    grad_fc1_weight = jnp.einsum(
        "td,tf->df", normed_low_two, grad_pre, preferred_element_type=jnp.float32
    )
    grad_fc1_shift = row_sum(grad_pre)
    grad_normed_two = jnp.einsum(
        "tf,df->td", grad_pre, fc1_weight, preferred_element_type=jnp.float32
    )
    grad_gain_two = jnp.sum(grad_normed_two * normed_two, axis=0)
    grad_shift_two = jnp.sum(grad_normed_two, axis=0)
    grad_resid = grad_out + norm_back(grad_normed_two, normed_two, inv_std_two, gain_two)
    grad_scale_one = jnp.sum(grad_resid * branch_one, axis=0)
    grad_branch_one = (scale_one * grad_resid).astype(jnp.bfloat16)
    grad_proj_weight = jnp.einsum(
        "td,te->de", attn_low, grad_branch_one, preferred_element_type=jnp.float32
    )
    grad_proj_shift = row_sum(grad_branch_one)
    grad_attn = jnp.einsum(
        "te,de->td", grad_branch_one, proj_weight, preferred_element_type=jnp.float32
    ).astype(jnp.bfloat16)
    keys_back = lax.all_gather(key_local, "seq", axis=0, tiled=True)

    def table_sum(values):
        left_sums = diagonal_sums(values * same_side)
        right_sums = diagonal_sums(values * (1.0 - same_side))
        return jax.ops.segment_sum(
            jnp.concatenate([left_sums, right_sums]), diag_index, num_segments=table_rows
        )

    def attend_back(pair_index):
        query_pair = pick_pair(queries, 0, pair_index, local_rows)
        key_pair = pick_pair(keys_back, 0, pair_index, seq_len)
        value_pair = pick_pair(keys_back, width_model, pair_index, seq_len)
        table_pair = lax.dynamic_slice_in_dim(table_heads, 2 * pair_index, 2, 0)
        probs = pair_probs(query_pair, key_pair, table_pair, rel_index, key_valid)
        rounded = probs.astype(jnp.bfloat16)
        grad_pair = pick_pair(grad_attn, 0, pair_index, local_rows)
        grad_probs = jnp.einsum(
            "qhd,khd->hqk", grad_pair, value_pair, preferred_element_type=jnp.float32
        )
        grad_scores = probs * (grad_probs - jnp.sum(probs * grad_probs, axis=-1, keepdims=True))
        table_terms = jax.vmap(table_sum)(grad_scores)
        grad_prod = (grad_scores * HEAD_DIM ** (-0.5)).astype(jnp.bfloat16)
        grad_query = jnp.einsum(
            "hqk,khd->qhd", grad_prod, key_pair, preferred_element_type=jnp.float32
        )
        grad_key = jnp.einsum(
            "hqk,qhd->khd", grad_prod, query_pair, preferred_element_type=jnp.float32
        )
        grad_value = jnp.einsum(
            "hqk,qhd->khd", rounded, grad_pair, preferred_element_type=jnp.float32
        )
        return (
            grad_query.reshape(local_rows, pair_cols),
            grad_key.reshape(seq_len, pair_cols),
            grad_value.reshape(seq_len, pair_cols),
            table_terms,
        )

    grad_query_all, grad_key_all, grad_value_all, table_all = lax.map(
        attend_back, jnp.arange(pair_count)
    )
    key_terms = jnp.concatenate(
        [merge_pairs(grad_key_all, seq_len), merge_pairs(grad_value_all, seq_len)], axis=1
    )
    own_terms = lax.psum_scatter(
        key_terms.astype(jnp.bfloat16), "seq", scatter_dimension=0, tiled=True
    ).astype(jnp.float32)
    grad_qkv = jnp.concatenate([merge_pairs(grad_query_all, local_rows), own_terms], axis=1).astype(
        jnp.bfloat16
    )
    table_grad = table_all.reshape(HEADS, table_rows).T
    grad_qkv_weight = jnp.einsum(
        "td,te->de", normed_low, grad_qkv, preferred_element_type=jnp.float32
    )
    grad_query_bias = row_sum(grad_qkv[:, :width_model])
    grad_value_bias = row_sum(grad_qkv[:, 2 * width_model :])
    grad_normed_one = jnp.einsum(
        "te,de->td", grad_qkv, qkv_weight, preferred_element_type=jnp.float32
    )
    grad_gain_one = jnp.sum(grad_normed_one * normed_one, axis=0)
    grad_shift_one = jnp.sum(grad_normed_one, axis=0)
    grad_inputs = (
        grad_resid + norm_back(grad_normed_one, normed_one, inv_std_one, gain_one)
    ).astype(jnp.bfloat16)
    summed = (
        lax.psum_scatter(grad_gain_one, ("img", "seq"), scatter_dimension=0, tiled=True),
        lax.psum_scatter(grad_shift_one, ("img", "seq"), scatter_dimension=0, tiled=True),
        lax.psum_scatter(grad_qkv_weight, ("img", "seq"), scatter_dimension=0, tiled=True),
        lax.psum_scatter(grad_query_bias, ("img", "seq"), scatter_dimension=0, tiled=True),
        lax.psum_scatter(grad_value_bias, ("img", "seq"), scatter_dimension=0, tiled=True),
        lax.psum_scatter(grad_proj_weight, ("img", "seq"), scatter_dimension=0, tiled=True),
        lax.psum_scatter(grad_proj_shift, ("img", "seq"), scatter_dimension=0, tiled=True),
        lax.psum_scatter(grad_scale_one, ("img", "seq"), scatter_dimension=0, tiled=True),
        lax.psum_scatter(grad_gain_two, ("img", "seq"), scatter_dimension=0, tiled=True),
        lax.psum_scatter(grad_shift_two, ("img", "seq"), scatter_dimension=0, tiled=True),
        lax.psum_scatter(grad_fc1_weight, ("img", "seq"), scatter_dimension=0, tiled=True),
        lax.psum_scatter(grad_fc1_shift, ("img", "seq"), scatter_dimension=0, tiled=True),
        lax.psum_scatter(grad_fc2_weight, ("img", "seq"), scatter_dimension=0, tiled=True),
        lax.psum_scatter(grad_fc2_shift, ("img", "seq"), scatter_dimension=0, tiled=True),
        lax.psum_scatter(grad_scale_two, ("img", "seq"), scatter_dimension=0, tiled=True),
    )
    table_total = lax.psum(table_grad, ("img", "seq"))
    return (output, grad_inputs) + tuple(summed) + (table_total,)


def solution(mesh):
    return jax.shard_map(
        per_device,
        mesh=mesh,
        in_specs=(
            P(("img", "seq"), None),
            P(("img", "seq"), None),
            P("img"),
            P("img"),
            P(("img", "seq")),
            P(("img", "seq")),
            P(("img", "seq"), None),
            P(("img", "seq")),
            P(("img", "seq")),
            P(("img", "seq"), None),
            P(("img", "seq")),
            P(("img", "seq")),
            P(("img", "seq")),
            P(("img", "seq")),
            P(("img", "seq"), None),
            P(("img", "seq")),
            P(("img", "seq"), None),
            P(("img", "seq")),
            P(("img", "seq")),
            P(),
        ),
        out_specs=(
            P(("img", "seq"), None),
            P(("img", "seq"), None),
            P(("img", "seq")),
            P(("img", "seq")),
            P(("img", "seq"), None),
            P(("img", "seq")),
            P(("img", "seq")),
            P(("img", "seq"), None),
            P(("img", "seq")),
            P(("img", "seq")),
            P(("img", "seq")),
            P(("img", "seq")),
            P(("img", "seq"), None),
            P(("img", "seq")),
            P(("img", "seq"), None),
            P(("img", "seq")),
            P(("img", "seq")),
            P(),
        ),
        check_vma=False,
    )
```

profile of v0, /device:TPU:0, one launch (start us, length us, event | category | flops | bytes accessed | tf_op | source)
XLA Modules:
  0.0 2372.6 jit_solution(14542166419529436356)
XLA Ops:
  19.3 42.8 %all-reduce.25 = (bf16[768]{0:T(1024)(128)(2,1)S(1)}, bf16[768]{0:T(1024)(128)(2,1)S(1)}, bf16[768]{0:T(1024)(128)(2,1)S(1)}, bf16[768]{0:T(1024)(128)(2,1)S(1)}...) all-reduce(bf16[768]{0:T(1024)(128)(2,1)S(1)} %dynamic-update-slice, ...), channel_id=1, replica_groups=mesh['img'=16,'seq'=2] {'img','seq'}, use_global_device_ids=true, to_apply=%add.6 | all-reduce | flops 10752 | bytes 43008
  67.3 7.1 all-gather.5.cloned.1.call-done
  77.2 12.4 all_gather.55
  91.6 745.2 %while.33 = (s32[]{:T(128)}, bf16[6,128,128]{1,2,0:T(8,128)(2,1)S(1)}, s32[6]{0:T(128)S(1)}, bf16[256,1536]{0,1:T(8,128)(2,1)}, bf16[128,768]{0,1:T(8,128)(2,1)}...) while((s32[]{:T(128)}, ...), condition=%wide.region_5.7_spmd.clone, body=%wide.region_2.6_spmd.clone.sunk | while | flops 18220044 | bytes 3579776 | solution.py:188
  95.7 108.2 %gather_fusion = f32[32768,2]{1,0:T(8,128)} fusion(f32[2,1953]{0,1:T(8,128)S(1)} %constant_dynamic-slice_fusion.18, s32[32768]{0:T(1024)S(1)} %broadcast_clamp_fusion.4), kind=kCustom, calls=%fused_computation.clone.clone.1 | custom fusion | bytes 655360 | tf_op jit(solution)/shard_map/while/body/eval_jaxpr/jit(_take)/gather | solution.py:35
  203.9 10.0 copy.106
  220.0 108.2 %gather_fusion = f32[32768,2]{1,0:T(8,128)} fusion(f32[2,1953]{0,1:T(8,128)S(1)} %constant_dynamic-slice_fusion.18, s32[32768]{0:T(1024)S(1)} %broadcast_clamp_fusion.4), kind=kCustom, calls=%fused_computation.clone.clone.1 | custom fusion | bytes 655360 | tf_op jit(solution)/shard_map/while/body/eval_jaxpr/jit(_take)/gather | solution.py:35
  328.2 10.0 copy.106
  344.2 108.2 %gather_fusion = f32[32768,2]{1,0:T(8,128)} fusion(f32[2,1953]{0,1:T(8,128)S(1)} %constant_dynamic-slice_fusion.18, s32[32768]{0:T(1024)S(1)} %broadcast_clamp_fusion.4), kind=kCustom, calls=%fused_computation.clone.clone.1 | custom fusion | bytes 655360 | tf_op jit(solution)/shard_map/while/body/eval_jaxpr/jit(_take)/gather | solution.py:35
  452.4 10.0 copy.106
  468.4 108.2 %gather_fusion = f32[32768,2]{1,0:T(8,128)} fusion(f32[2,1953]{0,1:T(8,128)S(1)} %constant_dynamic-slice_fusion.18, s32[32768]{0:T(1024)S(1)} %broadcast_clamp_fusion.4), kind=kCustom, calls=%fused_computation.clone.clone.1 | custom fusion | bytes 655360 | tf_op jit(solution)/shard_map/while/body/eval_jaxpr/jit(_take)/gather | solution.py:35
  576.6 10.0 copy.106
  592.5 108.2 %gather_fusion = f32[32768,2]{1,0:T(8,128)} fusion(f32[2,1953]{0,1:T(8,128)S(1)} %constant_dynamic-slice_fusion.18, s32[32768]{0:T(1024)S(1)} %broadcast_clamp_fusion.4), kind=kCustom, calls=%fused_computation.clone.clone.1 | custom fusion | bytes 655360 | tf_op jit(solution)/shard_map/while/body/eval_jaxpr/jit(_take)/gather | solution.py:35
  700.8 10.0 copy.106
  716.7 108.2 %gather_fusion = f32[32768,2]{1,0:T(8,128)} fusion(f32[2,1953]{0,1:T(8,128)S(1)} %constant_dynamic-slice_fusion.18, s32[32768]{0:T(1024)S(1)} %broadcast_clamp_fusion.4), kind=kCustom, calls=%fused_computation.clone.clone.1 | custom fusion | bytes 655360 | tf_op jit(solution)/shard_map/while/body/eval_jaxpr/jit(_take)/gather | solution.py:35
  824.9 10.0 copy.106
  839.5 8.4 multiply_convert_fusion.3
  848.0 5.9 convert_reduce_fusion
  861.9 841.8 %while.34 = (s32[]{:T(128)}, bf16[6,128,128]{1,2,0:T(8,128)(2,1)}, bf16[6,256,128]{1,2,0:T(8,128)(2,1)}, bf16[6,256,128]{1,2,0:T(8,128)(2,1)}, f32[6,2,1953]{2,1...) while((s32[]{:T(128)}, bf16[6,128,128]{1,2,0:T(8,128)(2,1)}, ...), condition=%wide.region_17.19_spmd.clone.clone, body=%wide.region_10.18_spmd.clone.clone.sunk | while | flops 61902344 | bytes 15489084 | solution.py:267
  867.8 108.2 %gather_fusion.1 = f32[32768,2]{1,0:T(8,128)} fusion(f32[2,1953]{0,1:T(8,128)S(1)} %constant_dynamic-slice_fusion.22, s32[32768]{0:T(1024)S(1)} %broadcast_clamp_fusion.5), kind=kCustom, calls=%fused_computation.1.clone.clone.1 | custom fusion | bytes 655360 | tf_op jit(solution)/shard_map/while/body/eval_jaxpr/jit(_take)/gather | solution.py:35
  976.0 10.0 copy.109
  994.8 6.4 scatter_custom_fusion.7
  1008.1 108.2 %gather_fusion.1 = f32[32768,2]{1,0:T(8,128)} fusion(f32[2,1953]{0,1:T(8,128)S(1)} %constant_dynamic-slice_fusion.22, s32[32768]{0:T(1024)S(1)} %broadcast_clamp_fusion.5), kind=kCustom, calls=%fused_computation.1.clone.clone.1 | custom fusion | bytes 655360 | tf_op jit(solution)/shard_map/while/body/eval_jaxpr/jit(_take)/gather | solution.py:35
  1116.3 10.0 copy.109
  1135.1 6.4 scatter_custom_fusion.7
  1148.4 108.2 %gather_fusion.1 = f32[32768,2]{1,0:T(8,128)} fusion(f32[2,1953]{0,1:T(8,128)S(1)} %constant_dynamic-slice_fusion.22, s32[32768]{0:T(1024)S(1)} %broadcast_clamp_fusion.5), kind=kCustom, calls=%fused_computation.1.clone.clone.1 | custom fusion | bytes 655360 | tf_op jit(solution)/shard_map/while/body/eval_jaxpr/jit(_take)/gather | solution.py:35
  1256.6 10.0 copy.109
  1275.5 6.4 scatter_custom_fusion.7
  1288.7 108.2 %gather_fusion.1 = f32[32768,2]{1,0:T(8,128)} fusion(f32[2,1953]{0,1:T(8,128)S(1)} %constant_dynamic-slice_fusion.22, s32[32768]{0:T(1024)S(1)} %broadcast_clamp_fusion.5), kind=kCustom, calls=%fused_computation.1.clone.clone.1 | custom fusion | bytes 655360 | tf_op jit(solution)/shard_map/while/body/eval_jaxpr/jit(_take)/gather | solution.py:35
  1397.0 10.0 copy.109
  1415.8 6.4 scatter_custom_fusion.7
  1429.0 108.2 %gather_fusion.1 = f32[32768,2]{1,0:T(8,128)} fusion(f32[2,1953]{0,1:T(8,128)S(1)} %constant_dynamic-slice_fusion.22, s32[32768]{0:T(1024)S(1)} %broadcast_clamp_fusion.5), kind=kCustom, calls=%fused_computation.1.clone.clone.1 | custom fusion | bytes 655360 | tf_op jit(solution)/shard_map/while/body/eval_jaxpr/jit(_take)/gather | solution.py:35
  1537.3 10.0 copy.109
  1556.0 6.4 scatter_custom_fusion.7
  1569.3 108.2 %gather_fusion.1 = f32[32768,2]{1,0:T(8,128)} fusion(f32[2,1953]{0,1:T(8,128)S(1)} %constant_dynamic-slice_fusion.22, s32[32768]{0:T(1024)S(1)} %broadcast_clamp_fusion.5), kind=kCustom, calls=%fused_computation.1.clone.clone.1 | custom fusion | bytes 655360 | tf_op jit(solution)/shard_map/while/body/eval_jaxpr/jit(_take)/gather | solution.py:35
  1677.6 10.0 copy.109
  1696.4 6.4 scatter_custom_fusion.7
  1708.9 13.4 reduce-scatter.16.cloned.1.call-done
  1723.6 4.1 fusion.75
  1728.8 5.1 fusion.90
  1735.2 5.1 fusion.77
  1740.6 3.4 fusion.71
  1744.1 40.5 %all-reduce.24 = (f32[768]{0:T(1024)S(1)}, f32[768]{0:T(1024)S(1)}, f32[768]{0:T(1024)S(1)}, f32[768]{0:T(1024)S(1)}, f32[768]{0:T(1024)S(1)}, /*index=5*/f32[76...) all-reduce(f32[768]{0:T(1024)S(1)} %get-tuple-element.502, ...), channel_id=3, replica_groups=mesh['img'=16,'seq'=2] {'img','seq'}, use_global_device_ids=true, to_apply=%region_22.24.clone | all-reduce | flops 10752 | bytes 86016
  1791.9 59.8 %all-reduce.28.cloned.1.call-done = f32[1953,12]{0,1:T(8,128)} async-done(((f32[1953,12]{0,1:T(8,128)}), f32[1953,12]{0,1:T(8,128)}) %all-reduce.28.cloned.1.call-update) | async-done | bytes 93760 | tf_op jit(solution)/shard_map/psum | solution.py:310
  1851.7 104.8 %reduce-scatter.10.cloned.1.call-done = f32[24,768]{1,0:T(8,128)} async-done(((f32[768,768]{1,0:T(8,128)}), f32[24,768]{1,0:T(8,128)}) %reduce-scatter.10.cloned.1.call-update) | async-done | bytes 73744 | tf_op jit(solution)/shard_map/reduce_scatter | solution.py:299
  1956.5 124.4 %reduce-scatter.8.cloned.1.call-done = f32[24,2304]{1,0:T(8,128)} async-done(((f32[768,2304]{1,0:T(8,128)}), f32[24,2304]{1,0:T(8,128)}) %reduce-scatter.8.cloned.1.call-update) | async-done | bytes 221200 | tf_op jit(solution)/shard_map/reduce_scatter | solution.py:296
  2080.9 142.4 %reduce-scatter.12.cloned.1.call-done = f32[24,3072]{1,0:T(8,128)} async-done(((f32[768,3072]{1,0:T(8,128)}), f32[24,3072]{1,0:T(8,128)}) %reduce-scatter.12.cloned.1.call-update) | async-done | bytes 294928 | tf_op jit(solution)/shard_map/reduce_scatter | solution.py:304
  2223.3 140.9 %reduce-scatter.14.cloned.1.call-done = f32[96,768]{1,0:T(8,128)} async-done(((f32[3072,768]{1,0:T(8,128)}), f32[96,768]{1,0:T(8,128)}) %reduce-scatter.14.cloned.1.call-update) | async-done | bytes 294928 | tf_op jit(solution)/shard_map/reduce_scatter | solution.py:306
  (566 shorter events, 162.2 us)
Async XLA Ops:
  7.2 67.2 %copy-start = (bf16[128,768]{1,0:T(8,128)(2,1)S(1)}, bf16[128,768]{1,0:T(8,128)(2,1)}, u32[]{:S(2)}) copy-start(bf16[128,768]{1,0:T(8,128)(2,1)} %param.26) | copy-start | bytes 589828
  7.2 67.2 %all-gather.5.cloned.1.call-start = ((), (), s32[]{:S(2)}) async-start(), calls=%async_computation.5 | async-start | bytes 3649536 | tf_op jit(solution)/shard_map/all_gather | solution.py:80
  7.9 828.9 %all-gather.7.cloned.1.call-start = ((), (), s32[]{:S(2)}) async-start(), calls=%async_computation.6 | async-start | bytes 1216512 | tf_op jit(solution)/shard_map/all_gather | solution.py:83
  8.7 830.8 %all-gather.9.cloned.1.call-start = ((), (), s32[]{:S(2)}) async-start(), calls=%async_computation.7 | async-start | bytes 4866048 | tf_op jit(solution)/shard_map/all_gather | solution.py:88
  9.4 838.5 %all-gather.11.cloned.1.call-start = ((), (), s32[]{:S(2)}) async-start(), calls=%async_computation.8 | async-start | bytes 4866048 | tf_op jit(solution)/shard_map/all_gather | solution.py:90
  10.0 1712.3 %reduce-scatter.16.cloned.1.call-start = ((), (), s32[]{:S(2)}) async-start(), calls=%async_computation.14 | async-start | bytes 1179648
  62.1 794.2 %copy-start.31 = (f32[768]{0:T(1024)}, f32[768]{0:T(1024)S(1)}, u32[]{:S(2)}) copy-start(f32[768]{0:T(1024)S(1)} %convert_element_type.135) | copy-start | bytes 9220
  62.1 15.0 copy-start.26
  62.1 15.0 copy-start.24
  63.2 13.9 copy-start.41
  64.4 12.8 copy-start.46
  66.4 789.9 %copy-start.22 = (f32[768]{0:T(1024)}, f32[768]{0:T(1024)S(1)}, u32[]{:S(2)}) copy-start(f32[768]{0:T(1024)S(1)} %convert_element_type.136) | copy-start | bytes 9220
  66.4 773.1 %copy-start.28 = (f32[768]{0:T(1024)}, f32[768]{0:T(1024)S(1)}, u32[]{:S(2)}) copy-start(f32[768]{0:T(1024)S(1)} %convert_element_type.137) | copy-start | bytes 9220
  836.8 11.2 copy-start.13
  839.3 17.0 copy-start.39
  839.5 16.8 copy-start.44
  839.5 8.5 copy-start.16
  847.9 8.3 copy-start.4
  848.0 5.9 copy-start.2
  861.9 5.9 copy-start.20
  976.0 10.0 copy-start.19
  976.0 10.0 copy-start.21
  1002.2 5.9 copy-start.18
  1002.2 5.9 copy-start.20
  1116.3 10.0 copy-start.19
  1116.3 10.0 copy-start.21
  1142.5 5.9 copy-start.20
  1256.6 10.0 copy-start.19
  1256.6 10.0 copy-start.21
  1282.8 5.9 copy-start.20
  1397.0 10.0 copy-start.19
  1397.0 10.0 copy-start.21
  1423.1 5.9 copy-start.20
  1537.3 10.0 copy-start.19
  1537.3 10.0 copy-start.21
  1563.4 5.9 copy-start.20
  1677.6 10.0 copy-start.19
  1677.6 10.0 copy-start.21
  1706.1 145.6 %all-reduce.28.cloned.1.call-start = ((), (), s32[]{:S(2)}) async-start(), calls=%async_computation.13 | async-start | bytes 262144 | tf_op jit(solution)/shard_map/psum | solution.py:310
  1706.9 249.6 %reduce-scatter.10.cloned.1.call-start = ((), (), s32[]{:S(2)}) async-start(), calls=%async_computation.10 | async-start | bytes 2433024 | tf_op jit(solution)/shard_map/reduce_scatter | solution.py:299
  1708.8 14.7 copy-start.12
  1708.8 14.7 copy-start.25
  1708.8 14.7 copy-start.27
  1708.8 14.7 copy-start.42
  1708.8 14.7 copy-start.47
  1708.9 372.0 %reduce-scatter.8.cloned.1.call-start = ((), (), s32[]{:S(2)}) async-start(), calls=%async_computation.9 | async-start | bytes 7299072 | tf_op jit(solution)/shard_map/reduce_scatter | solution.py:296
  1727.7 495.5 %reduce-scatter.12.cloned.1.call-start = ((), (), s32[]{:S(2)}) async-start(), calls=%async_computation.11 | async-start | bytes 9732096 | tf_op jit(solution)/shard_map/reduce_scatter | solution.py:304
  1734.0 630.2 %reduce-scatter.14.cloned.1.call-start = ((), (), s32[]{:S(2)}) async-start(), calls=%async_computation.12 | async-start | bytes 9732096 | tf_op jit(solution)/shard_map/reduce_scatter | solution.py:306
  (40 other events, 109.6 us)
Sparse Core Ops, SparseCore 0:
  11.0 63.3 all-gather.4
  77.3 52.8 all-gather.6
  133.1 62.5 all-gather.8
  198.5 62.4 all-gather.10
  1706.2 16.0 reduce-scatter.15
  1729.2 122.4 all-reduce.27
  1858.4 98.0 reduce-scatter.9
  1962.8 118.0 reduce-scatter.7
  2088.3 134.8 reduce-scatter.11
  2229.6 134.5 reduce-scatter.13
where the time goes:
time: 2380 us; the launch traced here: 2370 us
  local copies, waits for them, and re-layouts  1520 us (64%)
  waiting for transfers between devices  596 us (25%)
  blocking collectives  95.6 us (4%)
  matrix products  71.2 us (3%)
  other arithmetic  59.8 us (3%)
    gather x24, local copies, waits for them, and re-layouts, pair_probs(): jnp.take(table_pair, rel_index, axis=1)  1420 us
    reduce_scatter x1, waiting for transfers between devices, per_device(): lax.psum_scatter(grad_fc1_weight, ('img', 'seq'), scatter_dimension=0, ti...  142 us
    reduce_scatter x1, waiting for transfers between devices, per_device(): lax.psum_scatter(grad_fc2_weight, ('img', 'seq'), scatter_dimension=0, ti...  141 us
    reduce_scatter x1, waiting for transfers between devices, per_device(): lax.psum_scatter(grad_qkv_weight, ('img', 'seq'), scatter_dimension=0, ti...  124 us
    reduce_scatter x1, waiting for transfers between devices, per_device(): lax.psum_scatter(grad_proj_weight, ('img', 'seq'), scatter_dimension=0, t...  105 us
    unnamed x2, blocking collectives  83.2 us
    psum x1, waiting for transfers between devices, per_device(): table_total = lax.psum(table_grad, ('img', 'seq'))  59.8 us
  transfers between devices with their start and end apart: 10, of which 7 were waited for; matrix products, arithmetic and copies ran while one was open for 34% of the time, Pallas kernels for 0%

commit v1 on v0

--- a/solution.py
+++ b/solution.py
@@ -3,15 +3,223 @@
 import jax
 import jax.numpy as jnp
 from jax import lax
+from jax.experimental import pallas as pl
+from jax.experimental.pallas import tpu as pltpu
 from jax.sharding import PartitionSpec as P
 
 HEADS = 12
 HEAD_DIM = 64
 SIDE = 32
+PAIR = 2 * HEAD_DIM
+PAIRS = HEADS // 2
+HEAD_ROWS = 16
+LANES = 128
+F32 = jnp.float32
+BF16 = jnp.bfloat16
+NT = (((1,), (1,)), ((), ()))
+TN = (((0,), (0,)), ((), ()))
 
 
 EPSILON = 1e-06
 NEG_FILL = -1e30
+
+
+def dot(left, right, dims=(((1,), (0,)), ((), ()))):
+    return lax.dot_general(left, right, dims, preferred_element_type=F32)
+
+
+def iota(shape, dim):
+    return lax.broadcasted_iota(jnp.int32, shape, dim)
+
+
+def floor_div(values, width):
+    return jnp.floor((values.astype(F32) + 0.5) / width.astype(F32)).astype(jnp.int32)
+
+
+def table_index(place, span, rows, row_span, width, offset):
+    right = place >= span
+    diagonal = offset + rows - 1 - jnp.where(right, place - span, place)
+    row = floor_div(diagonal, width)
+    col = diagonal - row * width
+    row = jnp.where(right, row + 1, row)
+    col = jnp.where(right, col - width, col)
+    return (row + row_span - 1) * (2 * SIDE - 1) + col + SIDE - 1
+
+
+def same_side(rows, keys, width, offset):
+    query = iota((rows, keys), 0) + offset
+    key = iota((rows, keys), 1)
+    return (query - floor_div(query, width) * width) >= (key - floor_div(key, width) * width)
+
+
+def fill_diagonals(table_ref, diag_ref, rows, keys, row_span, width, offset):
+    span = rows + keys
+    entries = table_ref.shape[1]
+    step = 2 * LANES
+    index = table_index(iota((step, 2 * span), 1), span, rows, row_span, width, offset)
+    entry = iota((step, 2 * span), 0)
+    diag_ref[...] = jnp.zeros_like(diag_ref)
+
+    def add(chunk, carry):
+        start = pl.multiple_of(chunk * step, step)
+        chosen = jnp.where(entry + start == index, 1.0, 0.0).astype(BF16)
+        diag_ref[...] += dot(table_ref[:, pl.ds(start, step)], chosen)
+        return carry
+
+    lax.fori_loop(0, entries // step, add, 0)
+
+
+def half_mask(shape, half):
+    lane = iota(shape, 1)
+    return lane < HEAD_DIM if half == 0 else lane >= HEAD_DIM
+
+
+def pick(values, half):
+    return jnp.where(half_mask(values.shape, half), values, jnp.zeros_like(values))
+
+
+def attend(query_ref, kv_ref, diag_ref, probs_ref, mixed_ref, width, count, offset):
+    rows, model = query_ref.shape
+    keys = kv_ref.shape[0]
+    span = rows + keys
+    same = same_side(rows, keys, width, offset)
+    valid = iota((rows, keys), 1) < count
+
+    def one_pair(pair, carry):
+        cols = pl.ds(pl.multiple_of(pair * PAIR, PAIR), PAIR)
+        value_cols = pl.ds(pl.multiple_of(model + pair * PAIR, PAIR), PAIR)
+        query_pair = query_ref[:, cols]
+        key_pair = kv_ref[:, cols]
+        value_pair = kv_ref[:, value_cols]
+        mixed = jnp.zeros((rows, PAIR), F32)
+        for half in range(2):
+            head = pair * 2 + half
+            product = dot(pick(query_pair, half), key_pair, NT)
+            shifted = []
+            for side in range(2):
+                line = diag_ref[pl.ds(head, 1), side * span : (side + 1) * span]
+                line = jnp.broadcast_to(line, (rows, span))
+                line = pltpu.roll(line, keys + 1, 1, stride=1, stride_axis=0)
+                shifted.append(line[:, :keys])
+            scores = product * HEAD_DIM**-0.5 + jnp.where(same, shifted[0], shifted[1])
+            scores = jnp.where(valid, scores, NEG_FILL)
+            terms = jnp.exp(scores - jnp.max(scores, axis=1, keepdims=True))
+            terms = jnp.where(valid, terms, 0.0)
+            probs = terms / jnp.sum(terms, axis=1, keepdims=True)
+            probs_ref[head] = probs
+            mixed = mixed + dot(probs.astype(BF16), pick(value_pair, half))
+        mixed_ref[:, cols] = mixed.astype(BF16)
+        return carry
+
+    lax.fori_loop(0, PAIRS, one_pair, 0)
+
+
+def fold_rows(values):
+    while values.shape[0] > 8:
+        half = values.shape[0] // 2
+        values = values[half:] + pltpu.roll(values[:half], half, 1)
+    return values
+
+
+def attend_back(
+    query_ref, kv_ref, probs_ref, grad_ref, grad_query_ref, grad_kv_ref, fold_ref, width, offset
+):
+    rows, model = query_ref.shape
+    keys = kv_ref.shape[0]
+    same = same_side(rows, keys, width, offset)
+    fold_ref[...] = jnp.zeros_like(fold_ref)
+
+    def one_pair(pair, carry):
+        cols = pl.ds(pl.multiple_of(pair * PAIR, PAIR), PAIR)
+        value_cols = pl.ds(pl.multiple_of(model + pair * PAIR, PAIR), PAIR)
+        query_pair = query_ref[:, cols]
+        key_pair = kv_ref[:, cols]
+        value_pair = kv_ref[:, value_cols]
+        grad_pair = grad_ref[:, cols]
+        grad_query = jnp.zeros((rows, PAIR), F32)
+        grad_key = jnp.zeros((keys, PAIR), F32)
+        grad_value = jnp.zeros((keys, PAIR), F32)
+        for half in range(2):
+            head = pair * 2 + half
+            probs = probs_ref[head]
+            grad_half = pick(grad_pair, half)
+            grad_probs = dot(grad_half, value_pair, NT)
+            grad_scores = probs * (
+                grad_probs - jnp.sum(probs * grad_probs, axis=1, keepdims=True)
+            )
+            blank = jnp.zeros((rows, rows), F32)
+            left = jnp.where(same, grad_scores, 0.0)
+            right = jnp.where(same, 0.0, grad_scores)
+            for side, part in enumerate((left, right)):
+                place = pl.multiple_of((side * HEAD_ROWS + head) * 8, 8)
+                folded = fold_rows(jnp.concatenate([part, blank], axis=1))
+                for block in range((rows + keys) // LANES):
+                    fold_ref[block, pl.ds(place, 8), :] = folded[:, block * LANES : (block + 1) * LANES]
+            grad_prod = (grad_scores * HEAD_DIM**-0.5).astype(BF16)
+            grad_query = grad_query + dot(grad_prod, pick(key_pair, half))
+            grad_key = grad_key + dot(grad_prod, pick(query_pair, half), TN)
+            grad_value = grad_value + dot(probs.astype(BF16), grad_half, TN)
+        grad_query_ref[:, cols] = grad_query.astype(BF16)
+        grad_kv_ref[:, cols] = grad_key.astype(BF16)
+        grad_kv_ref[:, value_cols] = grad_value.astype(BF16)
+        return carry
+
+    lax.fori_loop(0, PAIRS, one_pair, 0)
+
+
+def table_gradient(fold_ref, out_ref, rows, keys, row_span, width, offset):
+    span = rows + keys
+    lines = 2 * HEAD_ROWS
+    total = jnp.zeros((lines, span), F32)
+    for row in range(8):
+        blocks = [fold_ref[block, pl.ds(row, lines, stride=8), :] for block in range(span // LANES)]
+        moved = jnp.concatenate(blocks, axis=1)
+        total = total + (pltpu.roll(moved, 7 - row, 1) if row < 7 else moved)
+    parts = []
+    for side in range(2):
+        rest = total[side * HEAD_ROWS : (side + 1) * HEAD_ROWS]
+        pieces = []
+        for _ in range(3):
+            piece = rest.astype(BF16)
+            rest = rest - piece.astype(F32)
+            pieces.append(piece)
+        parts.append(jnp.concatenate(pieces, axis=0))
+    place = iota((span, LANES), 0)
+    index = [
+        table_index(place + side * span, span, rows, row_span, width, offset) for side in range(2)
+    ]
+    entry = iota((span, LANES), 1)
+
+    def put(chunk, carry):
+        start = pl.multiple_of(chunk * LANES, LANES)
+        sums = jnp.zeros((3 * HEAD_ROWS, LANES), F32)
+        for side in range(2):
+            chosen = jnp.where(entry + start == index[side], 1.0, 0.0).astype(BF16)
+            sums = sums + dot(parts[side], chosen)
+        out_ref[:, pl.ds(start, LANES)] = (
+            sums[:HEAD_ROWS] + sums[HEAD_ROWS : 2 * HEAD_ROWS] + sums[2 * HEAD_ROWS :]
+        )
+        return carry
+
+    lax.fori_loop(0, out_ref.shape[1] // LANES, put, 0)
+
+
+def attend_kernel(row_span, scal_ref, query_ref, kv_ref, table_ref, mixed_ref, probs_ref, diag_ref):
+    rows, keys = query_ref.shape[0], kv_ref.shape[0]
+    width, count, offset = scal_ref[0], scal_ref[1], scal_ref[2]
+    fill_diagonals(table_ref, diag_ref, rows, keys, row_span, width, offset)
+    attend(query_ref, kv_ref, diag_ref, probs_ref, mixed_ref, width, count, offset)
+
+
+def attend_back_kernel(
+    row_span, scal_ref, query_ref, kv_ref, probs_ref, grad_ref, grad_query_ref, grad_kv_ref, table_ref, fold_ref
+):
+    rows, keys = query_ref.shape[0], kv_ref.shape[0]
+    width, offset = scal_ref[0], scal_ref[2]
+    attend_back(
+        query_ref, kv_ref, probs_ref, grad_ref, grad_query_ref, grad_kv_ref, fold_ref, width, offset
+    )
+    table_gradient(fold_ref, table_ref, rows, keys, row_span, width, offset)
 
 
 def layer_norm(values, gain, shift):
@@ -30,26 +238,8 @@
     )
 
 
-def pair_probs(query_pair, key_pair, table_pair, rel_index, key_valid):
-    product = jnp.einsum("qhd,khd->hqk", query_pair, key_pair, preferred_element_type=jnp.float32)
-    scores = product * HEAD_DIM ** (-0.5) + jnp.take(table_pair, rel_index, axis=1)
-    scores = jnp.where(key_valid[None, None, :], scores, NEG_FILL)
-    top_val = jnp.max(scores, axis=-1, keepdims=True)
-    exp_terms = jnp.where(key_valid[None, None, :], jnp.exp(scores - top_val), 0.0)
-    return exp_terms / jnp.sum(exp_terms, axis=-1, keepdims=True)
-
-
 def row_sum(values):
     return jnp.sum(values.astype(jnp.float32), axis=0)
-
-
-def diagonal_sums(values):
-    query_count = values.shape[0]
-    key_count = values.shape[1]
-    flipped = values[:, ::-1]
-    padded = jnp.pad(flipped, ((0, 0), (0, query_count)))
-    flat = padded.reshape(-1)[: query_count * (key_count + query_count - 1)]
-    return jnp.sum(flat.reshape(query_count, key_count + query_count - 1), axis=0)
 
 
 def per_device(
@@ -121,42 +311,16 @@
     width_model = tokens.shape[1]
     seq_len = local_rows * lax.axis_size("seq")
     offset = lax.axis_index("seq") * local_rows
-    image_width = widths[0]
-    places = jnp.arange(seq_len, dtype=jnp.int32)
-    grid_row = places // image_width
-    grid_col = places % image_width
-    key_valid = places < counts[0]
-    query_row = lax.dynamic_slice_in_dim(grid_row, offset, local_rows)
-    query_col = lax.dynamic_slice_in_dim(grid_col, offset, local_rows)
     row_span = (seq_len - 1) // (SIDE // 2) + 1
-    rel_index = (query_row[:, None] - grid_row[None, :] + row_span - 1) * (2 * SIDE - 1) + (
-        query_col[:, None] - grid_col[None, :] + SIDE - 1
-    )
-    same_side = (query_col[:, None] >= grid_col[None, :]).astype(jnp.float32)
     table_rows = bias_table.shape[0]
-    table_heads = bias_table.astype(jnp.float32).T
-    pair_cols = 2 * HEAD_DIM
-    pair_count = HEADS // 2
-    span_len = seq_len + local_rows - 1
-    offsets = jnp.arange(span_len, dtype=jnp.int32) - (seq_len - 1) + offset
-    row_left = jnp.floor_divide(offsets, image_width)
-    col_left = offsets - row_left * image_width
-    row_right = row_left + 1
-    col_right = col_left - image_width
-    index_left = (row_left + row_span - 1) * (2 * SIDE - 1) + col_left + SIDE - 1
-    index_right = (row_right + row_span - 1) * (2 * SIDE - 1) + col_right + SIDE - 1
-    fits_left = jnp.abs(row_left) <= row_span - 1
-    fits_right = (jnp.abs(row_right) <= row_span - 1) & (col_right > -image_width)
-    index_left = jnp.where(fits_left, index_left, table_rows)
-    index_right = jnp.where(fits_right, index_right, table_rows)
-    diag_index = jnp.concatenate([index_left, index_right])
-
-    def pick_pair(source, start_col, pair_index, row_count):
-        columns = lax.dynamic_slice_in_dim(source, start_col + pair_index * pair_cols, pair_cols, 1)
-        return columns.reshape(row_count, 2, HEAD_DIM)
-
-    def merge_pairs(stacked, row_count):
-        return stacked.transpose(1, 0, 2).reshape(row_count, width_model)
+    entries = -(-table_rows // (2 * LANES)) * 2 * LANES
+    table_lines = jnp.pad(
+        bias_table.T, ((0, HEAD_ROWS - HEADS), (0, entries - table_rows))
+    )
+    scalars = jnp.stack([widths[0], counts[0], offset.astype(jnp.int32)])
+    smem = pl.BlockSpec(memory_space=pltpu.SMEM)
+    vmem = pl.BlockSpec(memory_space=pltpu.VMEM)
+    params = pltpu.CompilerParams(vmem_limit_bytes=40 << 20)
 
     inputs_f = tokens.astype(jnp.float32)
     normed_full, normed_one, inv_std_one = layer_norm(inputs_f, gain_one, shift_one)
@@ -171,21 +335,17 @@
     key_local = projected[:, width_model:]
     keys_all = lax.all_gather(key_local, "seq", axis=0, tiled=True)
 
-    def attend(pair_index):
-        query_pair = pick_pair(queries, 0, pair_index, local_rows)
-        key_pair = pick_pair(keys_all, 0, pair_index, seq_len)
-        value_pair = pick_pair(keys_all, width_model, pair_index, seq_len)
-        table_pair = lax.dynamic_slice_in_dim(table_heads, 2 * pair_index, 2, 0)
-        probs = pair_probs(query_pair, key_pair, table_pair, rel_index, key_valid)
-        mixed = jnp.einsum(
-            "hqk,khd->qhd",
-            probs.astype(jnp.bfloat16),
-            value_pair,
-            preferred_element_type=jnp.float32,
-        )
-        return mixed.reshape(local_rows, pair_cols)
-
-    attn_low = merge_pairs(lax.map(attend, jnp.arange(pair_count)), local_rows).astype(jnp.bfloat16)
+    attn_low, probs = pl.pallas_call(
+        partial(attend_kernel, row_span),
+        out_shape=(
+            jax.ShapeDtypeStruct((local_rows, width_model), BF16),
+            jax.ShapeDtypeStruct((HEADS, local_rows, seq_len), F32),
+        ),
+        in_specs=[smem, vmem, vmem, vmem],
+        out_specs=(vmem, vmem),
+        scratch_shapes=[pltpu.VMEM((HEAD_ROWS, 2 * (local_rows + seq_len)), F32)],
+        compiler_params=params,
+    )(scalars, queries, keys_all, table_lines)
     branch_one = jnp.dot(attn_low, proj_weight, preferred_element_type=jnp.float32) + proj_shift
     residual_one = inputs_f + scale_one * branch_one
     normed_full_two, normed_two, inv_std_two = layer_norm(residual_one, gain_two, shift_two)
@@ -225,58 +385,22 @@
     grad_attn = jnp.einsum(
         "te,de->td", grad_branch_one, proj_weight, preferred_element_type=jnp.float32
     ).astype(jnp.bfloat16)
-    keys_back = lax.all_gather(key_local, "seq", axis=0, tiled=True)
-
-    def table_sum(values):
-        left_sums = diagonal_sums(values * same_side)
-        right_sums = diagonal_sums(values * (1.0 - same_side))
-        return jax.ops.segment_sum(
-            jnp.concatenate([left_sums, right_sums]), diag_index, num_segments=table_rows
-        )
-
-    def attend_back(pair_index):
-        query_pair = pick_pair(queries, 0, pair_index, local_rows)
-        key_pair = pick_pair(keys_back, 0, pair_index, seq_len)
-        value_pair = pick_pair(keys_back, width_model, pair_index, seq_len)
-        table_pair = lax.dynamic_slice_in_dim(table_heads, 2 * pair_index, 2, 0)
-        probs = pair_probs(query_pair, key_pair, table_pair, rel_index, key_valid)
-        rounded = probs.astype(jnp.bfloat16)
-        grad_pair = pick_pair(grad_attn, 0, pair_index, local_rows)
-        grad_probs = jnp.einsum(
-            "qhd,khd->hqk", grad_pair, value_pair, preferred_element_type=jnp.float32
-        )
-        grad_scores = probs * (grad_probs - jnp.sum(probs * grad_probs, axis=-1, keepdims=True))
-        table_terms = jax.vmap(table_sum)(grad_scores)
-        grad_prod = (grad_scores * HEAD_DIM ** (-0.5)).astype(jnp.bfloat16)
-        grad_query = jnp.einsum(
-            "hqk,khd->qhd", grad_prod, key_pair, preferred_element_type=jnp.float32
-        )
-        grad_key = jnp.einsum(
-            "hqk,qhd->khd", grad_prod, query_pair, preferred_element_type=jnp.float32
-        )
-        grad_value = jnp.einsum(
-            "hqk,qhd->khd", rounded, grad_pair, preferred_element_type=jnp.float32
-        )
-        return (
-            grad_query.reshape(local_rows, pair_cols),
-            grad_key.reshape(seq_len, pair_cols),
-            grad_value.reshape(seq_len, pair_cols),
-            table_terms,
-        )
-
-    grad_query_all, grad_key_all, grad_value_all, table_all = lax.map(
-        attend_back, jnp.arange(pair_count)
-    )
-    key_terms = jnp.concatenate(
-        [merge_pairs(grad_key_all, seq_len), merge_pairs(grad_value_all, seq_len)], axis=1
-    )
-    own_terms = lax.psum_scatter(
-        key_terms.astype(jnp.bfloat16), "seq", scatter_dimension=0, tiled=True
-    ).astype(jnp.float32)
-    grad_qkv = jnp.concatenate([merge_pairs(grad_query_all, local_rows), own_terms], axis=1).astype(
-        jnp.bfloat16
-    )
-    table_grad = table_all.reshape(HEADS, table_rows).T
+    grad_query, key_terms, table_grad = pl.pallas_call(
+        partial(attend_back_kernel, row_span),
+        out_shape=(
+            jax.ShapeDtypeStruct((local_rows, width_model), BF16),
+            jax.ShapeDtypeStruct((seq_len, 2 * width_model), BF16),
+            jax.ShapeDtypeStruct((HEAD_ROWS, entries), F32),
+        ),
+        in_specs=[smem, vmem, vmem, vmem, vmem],
+        out_specs=(vmem, vmem, vmem),
+        scratch_shapes=[
+            pltpu.VMEM(((local_rows + seq_len) // LANES, 2 * HEAD_ROWS * 8, LANES), F32)
+        ],
+        compiler_params=params,
+    )(scalars, queries, keys_all, probs, grad_attn)
+    own_terms = lax.psum_scatter(key_terms, "seq", scatter_dimension=0, tiled=True)
+    grad_qkv = jnp.concatenate([grad_query, own_terms], axis=1)
     grad_qkv_weight = jnp.einsum(
         "td,te->de", normed_low, grad_qkv, preferred_element_type=jnp.float32
     )
@@ -307,7 +431,7 @@
         lax.psum_scatter(grad_fc2_shift, ("img", "seq"), scatter_dimension=0, tiled=True),
         lax.psum_scatter(grad_scale_two, ("img", "seq"), scatter_dimension=0, tiled=True),
     )
-    table_total = lax.psum(table_grad, ("img", "seq"))
+    table_total = lax.psum(table_grad, ("img", "seq"))[:HEADS, :table_rows].T
     return (output, grad_inputs) + tuple(summed) + (table_total,)
 
 

time: 2380 us -> 947 us (0.40)
  local copies, waits for them, and re-layouts: 1520 us -> 22.2 us
  waiting for transfers between devices: 596 us -> 745 us
  other arithmetic: 59.8 us -> 8.23 us
  matrix products: 71.2 us -> 45.2 us
    gather x24 -> x0, local copies, waits for them, and re-layouts: 1420 us -> none  [pair_probs(): jnp.take(table_pair, rel_index, axis=1)]
    all_gather x1, waiting for transfers between devices: 0.02 us -> 62.1 us  [per_device(): lax.all_gather(w_fc1, ('img', 'seq'), axis=0, tiled=True)]
    all_gather x1, waiting for transfers between devices: 0.01 us -> 56.6 us  [per_device(): lax.all_gather(w_fc2, ('img', 'seq'), axis=0, tiled=True)]
    reduce_scatter x1, waiting for transfers between devices: 105 us -> 51.9 us  [per_device(): lax.psum_scatter(grad_proj_weight, ('img', 'seq'), scatter_dimension=0, t...]
    psum x1, waiting for transfers between devices: 59.8 us -> 112 us  [per_device(): table_total = lax.psum(table_grad, ('img', 'seq'))[:HEADS, :table_rows].T]
    dynamic_slice x62 -> x0, local copies, waits for them, and re-layouts: 40.1 us -> none  [the longest x36 25.1 us: pick_pair(): lax.dynamic_slice_in_dim(source, start_col + pair_index * pair_cols, pair...]
    scatter-add x6 -> x0, other arithmetic: 38.3 us -> none  [table_sum(): jax.ops.segment_sum(jnp.concatenate([left_sums, right_sums]), diag_index,...]
    all_gather x1, waiting for transfers between devices: 0.02 us -> 34.6 us  [per_device(): lax.all_gather(w_proj, ('img', 'seq'), axis=0, tiled=True)]
  transfers between devices with their start and end apart: 10 -> 10, of which waited for: 7 -> 10; matrix products, arithmetic and copies ran while one was open for 34% -> 6% of each run, Pallas kernels for 0% -> 1%
where the time goes in v1:
time: 947 us
  waiting for transfers between devices  745 us (79%)
  blocking collectives  95.6 us (10%)
  matrix products  45.2 us (5%)
  local copies, waits for them, and re-layouts  22.2 us (2%)
  between operations  15.9 us (2%)
  Pallas kernels  14.2 us (1%)
    reduce_scatter x1, waiting for transfers between devices, per_device(): lax.psum_scatter(grad_fc1_weight, ('img', 'seq'), scatter_dimension=0, ti...  142 us
    reduce_scatter x1, waiting for transfers between devices, per_device(): lax.psum_scatter(grad_fc2_weight, ('img', 'seq'), scatter_dimension=0, ti...  141 us
    reduce_scatter x1, waiting for transfers between devices, per_device(): lax.psum_scatter(grad_qkv_weight, ('img', 'seq'), scatter_dimension=0, ti...  124 us
    psum x1, waiting for transfers between devices, per_device(): table_total = lax.psum(table_grad, ('img', 'seq'))[:HEADS, :table_rows].T  112 us
    unnamed x2, blocking collectives  83.1 us
    all_gather x1, waiting for transfers between devices, per_device(): lax.all_gather(w_fc1, ('img', 'seq'), axis=0, tiled=True)  62.1 us
    all_gather x1, waiting for transfers between devices, per_device(): lax.all_gather(w_fc2, ('img', 'seq'), axis=0, tiled=True)  56.6 us
    reduce_scatter x1, waiting for transfers between devices, per_device(): lax.psum_scatter(grad_proj_weight, ('img', 'seq'), scatter_dimension=0, t...  51.9 us
  transfers between devices with their start and end apart: 10, of which 10 were waited for; matrix products, arithmetic and copies ran while one was open for 6% of the time, Pallas kernels for 1%

profile of v1, /device:TPU:0, one launch (start us, length us, event | category | flops | bytes accessed | tf_op | source)
XLA Modules:
  0.0 946.6 jit_solution(10664149139326114602)
XLA Ops:
  8.0 0.7 all-gather.7.cloned.1.call-update
  8.7 0.7 all-gather.9.cloned.1.call-update
  10.0 0.8 dynamic-update-slice.4
  10.9 0.8 dynamic-update-slice.3
  11.7 0.8 dynamic-update-slice.2
  12.6 0.8 dynamic-update-slice.1
  13.4 0.8 dynamic-update-slice.5
  14.2 0.8 dynamic-update-slice
  15.1 0.8 dynamic-update-slice.8
  15.9 0.8 dynamic-update-slice.7
  16.7 0.8 dynamic-update-slice.10
  17.6 0.8 dynamic-update-slice.6
  18.4 0.8 dynamic-update-slice.9
  19.3 42.8 %all-reduce.24 = (bf16[768]{0:T(1024)(128)(2,1)S(1)}, bf16[768]{0:T(1024)(128)(2,1)S(1)}, bf16[768]{0:T(1024)(128)(2,1)S(1)}, bf16[768]{0:T(1024)(128)(2,1)S(1)}...) all-reduce(bf16[768]{0:T(1024)(128)(2,1)S(1)} %dynamic-update-slice, ...), channel_id=1, replica_groups=mesh['img'=16,'seq'=2] {'img','seq'}, use_global_device_ids=true, to_apply=%add.5 | all-reduce | flops 10752 | bytes 43008
  66.9 0.8 pad.4.table_ref
  67.9 1.0 convert_reduce_fusion.1
  68.9 1.1 fusion.21
  70.1 4.2 all-gather.5.cloned.1.call-done
  74.3 2.8 fusion
  77.3 12.5 %all_gather.54.kv_ref = bf16[256,1536]{1,0:T(8,128)(2,1)S(1)} all-gather(bf16[128,1536]{1,0:T(8,128)(2,1)S(1)} %slice.17), channel_id=1, replica_groups=mesh['img'=16,'seq'=2] {'seq'}, dimensions={0}, use_global_device_ids=true | all-gather | bytes 1179648 | tf_op jit(solution)/shard_map/all_gather | solution.py:336
  89.8 5.7 shard_map.331
  95.5 34.6 %all-gather.7.cloned.1.call-done = bf16[768,768]{1,0:T(8,128)(2,1)} async-done(((bf16[24,768]{1,0:T(8,128)(2,1)}), bf16[768,768]{1,0:T(8,128)(2,1)}) %all-gather.7.cloned.1.call-update) | async-done | bytes 1179664 | tf_op jit(solution)/shard_map/all_gather | solution.py:273
  130.2 2.4 fusion.35
  133.6 62.1 %all-gather.9.cloned.1.call-done = bf16[768,3072]{1,0:T(8,128)(2,1)} async-done(((bf16[24,3072]{1,0:T(8,128)(2,1)}), bf16[768,3072]{1,0:T(8,128)(2,1)}) %all-gather.9.cloned.1.call-update) | async-done | bytes 4718608 | tf_op jit(solution)/shard_map/all_gather | solution.py:278
  195.7 8.6 multiply_convert_fusion
  204.3 56.6 %all-gather.11.cloned.1.call-done = bf16[3072,768]{1,0:T(8,128)(2,1)} async-done(((bf16[96,768]{1,0:T(8,128)(2,1)}), bf16[3072,768]{1,0:T(8,128)(2,1)}) %all-gather.11.cloned.1.call-update) | async-done | bytes 4718608 | tf_op jit(solution)/shard_map/all_gather | solution.py:280
  260.9 5.8 convert_reduce_fusion
  266.8 2.3 multiply_reduce_fusion
  269.7 2.2 fusion.23
  271.8 0.7 convert_reduce_fusion.3
  273.2 8.4 shard_map.332
  282.3 2.8 fusion.36
  285.2 12.8 %reduce-scatter.6.cloned.1.call-done = bf16[128,1536]{1,0:T(8,128)(2,1)} async-done(((bf16[256,1536]{1,0:T(8,128)(2,1)}), bf16[128,1536]{1,0:T(8,128)(2,1)}) %reduce-scatter.6.cloned.1.call-update) | async-done | bytes 393232 | tf_op jit(solution)/shard_map/reduce_scatter | solution.py:402
  298.1 1.0 constant_dynamic-update-slice_fusion
  299.1 4.1 fusion.30
  303.3 1.0 copy-done.9
  304.4 5.1 fusion.33
  309.8 0.8 copy-done.5
  310.7 5.1 fusion.24
  315.8 111.6 %all-reduce.27.cloned.1.call-done = f32[16,2048]{1,0:T(8,128)} async-done(((f32[16,2048]{1,0:T(8,128)}), f32[16,2048]{1,0:T(8,128)}) %all-reduce.27.cloned.1.call-update) | async-done | bytes 131088 | tf_op jit(solution)/shard_map/psum | solution.py:434
  427.4 1.6 slice_bitcast_fusion
  429.1 3.5 fusion.20
  432.6 40.3 %all-reduce.23 = (f32[768]{0:T(1024)S(1)}, f32[768]{0:T(1024)S(1)}, f32[768]{0:T(1024)S(1)}, f32[768]{0:T(1024)S(1)}, f32[768]{0:T(1024)S(1)}, /*index=5*/f32[76...) all-reduce(f32[768]{0:T(1024)S(1)} %get-tuple-element.30, ...), channel_id=3, replica_groups=mesh['img'=16,'seq'=2] {'img','seq'}, use_global_device_ids=true, to_apply=%region_10.11.clone | all-reduce | flops 10752 | bytes 86016
  479.4 0.9 fusion.19
  480.3 51.9 %reduce-scatter.10.cloned.1.call-done = f32[24,768]{1,0:T(8,128)} async-done(((f32[768,768]{1,0:T(8,128)}), f32[24,768]{1,0:T(8,128)}) %reduce-scatter.10.cloned.1.call-update) | async-done | bytes 73744 | tf_op jit(solution)/shard_map/reduce_scatter | solution.py:423
  532.2 124.4 %reduce-scatter.8.cloned.1.call-done = f32[24,2304]{1,0:T(8,128)} async-done(((f32[768,2304]{1,0:T(8,128)}), f32[24,2304]{1,0:T(8,128)}) %reduce-scatter.8.cloned.1.call-update) | async-done | bytes 221200 | tf_op jit(solution)/shard_map/reduce_scatter | solution.py:420
  656.6 142.3 %reduce-scatter.12.cloned.1.call-done = f32[24,3072]{1,0:T(8,128)} async-done(((f32[768,3072]{1,0:T(8,128)}), f32[24,3072]{1,0:T(8,128)}) %reduce-scatter.12.cloned.1.call-update) | async-done | bytes 294928 | tf_op jit(solution)/shard_map/reduce_scatter | solution.py:428
  798.9 140.9 %reduce-scatter.14.cloned.1.call-done = f32[96,768]{1,0:T(8,128)} async-done(((f32[3072,768]{1,0:T(8,128)}), f32[96,768]{1,0:T(8,128)}) %reduce-scatter.14.cloned.1.call-update) | async-done | bytes 294928 | tf_op jit(solution)/shard_map/reduce_scatter | solution.py:430
  (140 shorter events, 15.1 us)
Async XLA Ops:
  7.2 67.1 %all-gather.5.cloned.1.call-start = ((), (), s32[]{:S(2)}) async-start(), calls=%async_computation.5 | async-start | bytes 3649536 | tf_op jit(solution)/shard_map/all_gather | solution.py:270
  7.9 122.2 %all-gather.7.cloned.1.call-start = ((), (), s32[]{:S(2)}) async-start(), calls=%async_computation.6 | async-start | bytes 1216512 | tf_op jit(solution)/shard_map/all_gather | solution.py:273
  8.7 187.0 %all-gather.9.cloned.1.call-start = ((), (), s32[]{:S(2)}) async-start(), calls=%async_computation.7 | async-start | bytes 4866048 | tf_op jit(solution)/shard_map/all_gather | solution.py:278
  9.4 251.5 %all-gather.11.cloned.1.call-start = ((), (), s32[]{:S(2)}) async-start(), calls=%async_computation.8 | async-start | bytes 4866048 | tf_op jit(solution)/shard_map/all_gather | solution.py:280
  10.0 288.1 %reduce-scatter.6.cloned.1.call-start = ((), (), s32[]{:S(2)}) async-start(), calls=%async_computation.9 | async-start | bytes 1179648 | tf_op jit(solution)/shard_map/reduce_scatter | solution.py:402
  68.9 8.2 copy-start.20
  70.1 7.1 copy-start.30
  77.2 53.0 %copy-start = (bf16[128,768]{1,0:T(8,128)(2,1)S(1)}, bf16[128,768]{1,0:T(8,128)(2,1)}, u32[]{:S(2)}) copy-start(bf16[128,768]{1,0:T(8,128)(2,1)} %param.20) | copy-start | bytes 589828
  77.2 52.9 %copy-start.18 = (f32[768]{0:T(1024)S(1)}, f32[768]{0:T(1024)}, u32[]{:S(2)}) copy-start(f32[768]{0:T(1024)} %convert_element_type.88) | copy-start | bytes 9220
  77.2 52.9 %copy-start.26 = (f32[768]{0:T(1024)S(1)}, f32[768]{0:T(1024)}, u32[]{:S(2)}) copy-start(f32[768]{0:T(1024)} %convert_element_type.94) | copy-start | bytes 9220
  132.5 0.5 copy-start.32
  133.6 127.3 %copy-start.13 = (bf16[128,768]{1,0:T(8,128)(2,1)S(1)}, bf16[128,768]{1,0:T(8,128)(2,1)}, u32[]{:S(2)}) copy-start(bf16[128,768]{1,0:T(8,128)(2,1)} %param.21) | copy-start | bytes 589828
  260.9 5.8 copy-start.2
  260.9 5.8 copy-start.33
  260.9 5.8 copy-start.36
  266.7 2.4 copy-start.8
  266.7 2.6 copy-start.1
  266.7 2.8 copy-start.4
  266.7 2.9 copy-start.11
  266.7 2.9 copy-start.16
  266.7 2.9 copy-start.22
  269.6 2.2 copy-start.19
  269.7 2.9 copy-start.3
  271.8 1.3 copy-start.6
  272.5 0.7 copy-start.10
  281.7 145.8 %all-reduce.27.cloned.1.call-start = ((), (), s32[]{:S(2)}) async-start(), calls=%async_computation.14 | async-start | bytes 262144 | tf_op jit(solution)/shard_map/psum | solution.py:434
  282.2 250.0 %reduce-scatter.10.cloned.1.call-start = ((), (), s32[]{:S(2)}) async-start(), calls=%async_computation.11 | async-start | bytes 2433024 | tf_op jit(solution)/shard_map/reduce_scatter | solution.py:423
  285.1 14.0 %copy-start.21 = (f32[128]{0:T(128)S(1)}, f32[128]{0:T(128)}, u32[]{:S(2)}) copy-start(f32[128]{0:T(128)} %copy-done.20) | copy-start | bytes 1540
  285.1 14.0 %copy-start.31 = (f32[128]{0:T(128)S(1)}, f32[128]{0:T(128)}, u32[]{:S(2)}) copy-start(f32[128]{0:T(128)} %copy-done.30) | copy-start | bytes 1540
  285.2 371.4 %reduce-scatter.8.cloned.1.call-start = ((), (), s32[]{:S(2)}) async-start(), calls=%async_computation.10 | async-start | bytes 7299072 | tf_op jit(solution)/shard_map/reduce_scatter | solution.py:420
  303.2 1.1 copy-start.9
  303.2 1.1 copy-start.15
  303.2 1.1 copy-start.34
  303.2 1.1 copy-start.37
  303.2 495.6 %reduce-scatter.12.cloned.1.call-start = ((), (), s32[]{:S(2)}) async-start(), calls=%async_computation.12 | async-start | bytes 9732096 | tf_op jit(solution)/shard_map/reduce_scatter | solution.py:428
  309.5 1.1 copy-start.5
  309.5 1.2 copy-start.14
  309.5 1.2 copy-start.17
  309.5 630.3 %reduce-scatter.14.cloned.1.call-start = ((), (), s32[]{:S(2)}) async-start(), calls=%async_computation.13 | async-start | bytes 9732096 | tf_op jit(solution)/shard_map/reduce_scatter | solution.py:430
  315.7 113.3 %copy-start.12 = (bf16[128,1536]{1,0:T(8,128)(2,1)S(1)}, bf16[128,1536]{1,0:T(8,128)(2,1)}, u32[]{:S(2)}) copy-start(bf16[128,1536]{1,0:T(8,128)(2,1)} %reduce-scatter.6.cloned.1.call-done) | copy-start | bytes 1179652
  429.0 3.5 copy-start.23
  429.0 3.5 copy-start.24
  429.1 3.5 copy-start.25
  429.1 3.5 copy-start.27
  429.1 3.5 copy-start.28
  429.1 3.5 copy-start.29
  429.1 3.5 copy-start.35
  429.1 50.3 %copy-start.7 = (f32[128,768]{1,0:T(8,128)S(1)}, f32[128,768]{1,0:T(8,128)}, u32[]{:S(2)}) copy-start(f32[128,768]{1,0:T(8,128)} %copy-done.6) | copy-start | bytes 1179652
Sparse Core Ops, SparseCore 0:
  10.9 63.3 all-gather.4
  77.2 52.8 all-gather.6
  133.1 62.5 all-gather.8
  198.5 62.3 all-gather.10
  281.8 16.2 reduce-scatter.5
  304.9 122.4 all-reduce.26
  434.1 98.0 reduce-scatter.9
  538.5 118.0 reduce-scatter.7
  664.1 134.7 reduce-scatter.11
  805.2 134.5 reduce-scatter.13

commit v2 on v1

--- a/solution.py
+++ b/solution.py
@@ -222,6 +222,358 @@
     table_gradient(fold_ref, table_ref, rows, keys, row_span, width, offset)
 
 
+MESH = pl.DeviceIdType.MESH
+Z_SIZE = 4
+
+
+class Place:
+    def __init__(self):
+        img = lax.axis_index("img")
+        self.x = lax.axis_index("seq")
+        self.c = lax.rem(img, 2)
+        self.y = lax.rem(img // 2, 2)
+        self.z = img // 4
+
+    def at(self, z=None, y=None, c=None, x=None):
+        z = self.z if z is None else z
+        y = self.y if y is None else y
+        c = self.c if c is None else c
+        x = self.x if x is None else x
+        return {"img": (z * 2 + y) * 2 + c, "seq": x}
+
+    def sibling(self):
+        return self.at(c=1 - self.c)
+
+    def over_x(self):
+        return self.at(x=1 - self.x)
+
+    def over_y(self):
+        return self.at(y=1 - self.y)
+
+    def z_of(self, step):
+        return lax.rem(self.z + step, Z_SIZE)
+
+    def partners(self):
+        return [self.sibling(), self.over_x(), self.over_y()] + [
+            self.at(z=self.z_of(step)) for step in range(1, Z_SIZE)
+        ]
+
+
+def meet(place):
+    barrier = pltpu.get_barrier_semaphore()
+    partners = place.partners()
+    for partner in partners:
+        pl.semaphore_signal(barrier, inc=1, device_id=partner, device_id_type=MESH)
+    pl.semaphore_wait(barrier, len(partners))
+
+
+class Sems:
+    def __init__(self, send, recv):
+        self.send, self.recv, self.used = send, recv, 0
+
+    def copy(self, src, dst, device):
+        index = self.used
+        self.used += 1
+        return pltpu.make_async_remote_copy(
+            src_ref=src,
+            dst_ref=dst,
+            send_sem=self.send.at[index],
+            recv_sem=self.recv.at[index],
+            device_id=device,
+            device_id_type=MESH,
+        )
+
+
+GATHER_COPIES = 10
+
+
+class Gather:
+    def __init__(self, place, src, slots, cols, x_last, sems, local_sem):
+        z, y, c, x = place.z, place.y, place.c, place.x
+        every = slice(None)
+
+        def part(a, b, d, e):
+            return slots.at[a, b, d, e, :, cols]
+
+        own = part(z, y, c, x)
+        self.local = pltpu.make_async_copy(src.at[:, cols], own, local_sem)
+        self.along_z = [
+            sems.copy(src.at[:, cols], own, place.at(z=place.z_of(step)))
+            for step in range(1, Z_SIZE)
+        ]
+        line = part(every, y, c, x)
+        mid_line = part(every, 1 - y, c, x) if x_last else part(every, y, c, 1 - x)
+        mid, last = place.over_y(), place.over_x()
+        if not x_last:
+            mid, last = last, mid
+        sibling = place.sibling()
+        far_line = part(every, y, c, 1 - x) if x_last else part(every, 1 - y, c, x)
+        cross_line = part(every, 1 - y, c, 1 - x)
+        self.line_mid = sems.copy(line, line, mid)
+        self.line_last = sems.copy(line, line, last)
+        self.line_core = sems.copy(line, line, sibling)
+        self.mid_last = sems.copy(mid_line, mid_line, last)
+        self.mid_core = sems.copy(mid_line, mid_line, sibling)
+        self.far_core = sems.copy(far_line, far_line, sibling)
+        self.cross_core = sems.copy(cross_line, cross_line, sibling)
+
+    def begin(self):
+        self.local.start()
+        for copy in self.along_z:
+            copy.start()
+
+    def second(self):
+        self.local.wait()
+        for copy in self.along_z:
+            copy.wait_recv()
+        self.line_mid.start()
+        self.line_last.start()
+        self.line_core.start()
+
+    def third(self):
+        self.line_mid.wait_recv()
+        self.mid_last.start()
+        self.mid_core.start()
+
+    def fourth(self):
+        self.line_last.wait_recv()
+        self.far_core.start()
+        self.mid_last.wait_recv()
+        self.cross_core.start()
+
+    def arrive(self):
+        for copy in (self.line_core, self.mid_core, self.far_core, self.cross_core):
+            copy.wait_recv()
+
+    def settle(self):
+        for copy in self.along_z + [
+            self.line_mid,
+            self.line_last,
+            self.line_core,
+            self.mid_last,
+            self.mid_core,
+            self.far_core,
+            self.cross_core,
+        ]:
+            copy.wait_send()
+
+
+def halves(width):
+    middle = width // 2 // LANES * LANES
+    return [(0, middle), (middle, width - middle)]
+
+
+def gather_kernel(count, *refs):
+    sources, slots = refs[:count], refs[count : 2 * count]
+    send, recv, local = refs[2 * count :]
+    place = Place()
+    meet(place)
+    sems = Sems(send, recv)
+    chunks = []
+    for src, slot in zip(sources, slots):
+        width = src.shape[1]
+        cuts = [(0, width)] if width <= LANES else halves(width)
+        for half, (start, size) in enumerate(cuts):
+            chunks.append(
+                Gather(place, src, slot, pl.ds(start, size), half == 0, sems, local.at[len(chunks)])
+            )
+    for chunk in chunks:
+        chunk.begin()
+    steps = []
+    for number, chunk in enumerate(chunks):
+        for lag, step in enumerate((chunk.second, chunk.third, chunk.fourth, chunk.arrive)):
+            steps.append((number // 2 + lag, lag, number, step))
+    for _, _, _, step in sorted(steps, key=lambda entry: entry[:3]):
+        step()
+    for chunk in chunks:
+        chunk.settle()
+
+
+def gather_all(sources):
+    count = len(sources)
+    chunks = sum(1 if source.shape[1] <= LANES else 2 for source in sources)
+    anywhere = pl.BlockSpec(memory_space=pl.ANY)
+    shapes = [(Z_SIZE, 2, 2, 2) + source.shape for source in sources]
+    return pl.pallas_call(
+        partial(gather_kernel, count),
+        out_shape=tuple(
+            jax.ShapeDtypeStruct(shape, source.dtype) for shape, source in zip(shapes, sources)
+        ),
+        in_specs=[anywhere] * count,
+        out_specs=(anywhere,) * count,
+        scratch_shapes=[
+            pltpu.SemaphoreType.DMA((GATHER_COPIES * chunks,)),
+            pltpu.SemaphoreType.DMA((GATHER_COPIES * chunks,)),
+            pltpu.SemaphoreType.DMA((chunks,)),
+        ],
+        compiler_params=pltpu.CompilerParams(collective_id=0, has_side_effects=True),
+    )(*sources)
+
+
+REDUCE_COPIES = 6
+
+
+class Reduce:
+    def __init__(self, place, grad, own, first, second, third, out, start, size, x_first, sems):
+        self.place, self.grad, self.own, self.first = place, grad, own, first
+        self.second, self.third, self.out = second, third, out
+        self.start, self.size, self.x_first = start, size, x_first
+        z, y, c, x = place.z, place.y, place.c, place.x
+        every = slice(None)
+        cols = pl.ds(start, size)
+        self.cols = cols
+        self.to_core = sems.copy(
+            grad.at[:, :, 1 - c, :, :, cols], own.at[:, :, :, :, cols], place.sibling()
+        )
+        over_first, over_second = place.over_x(), place.over_y()
+        if x_first:
+            leaving, other = own.at[:, :, 1 - x, :, cols], 1 - y
+        else:
+            over_first, over_second = over_second, over_first
+            leaving, other = own.at[:, 1 - y, :, :, cols], 1 - x
+        self.kept = y if x_first else x
+        self.over_first = sems.copy(leaving, first, over_first)
+        self.over_second = sems.copy(first.at[:, other], second, over_second)
+        self.along_z = []
+        for step in range(1, Z_SIZE):
+            target = place.z_of(step)
+            self.along_z.append(
+                sems.copy(second.at[target], third.at[step - 1], place.at(z=target))
+            )
+
+    def begin(self):
+        self.to_core.start()
+
+    def add_core(self):
+        self.to_core.wait_recv()
+        place = self.place
+
+        def add(zy, carry):
+            z, y = zy // 2, lax.rem(zy, 2)
+            for x in range(2):
+                mine = self.grad[z, y, place.c, x, :, self.cols].astype(F32)
+                theirs = self.own[z, y, x, :, self.cols].astype(F32)
+                self.own[z, y, x, :, self.cols] = (mine + theirs).astype(self.own.dtype)
+            return carry
+
+        lax.fori_loop(0, 2 * Z_SIZE, add, 0)
+        self.over_first.start()
+
+    def add_first(self):
+        self.over_first.wait_recv()
+        place = self.place
+
+        def add(z, carry):
+            for other in range(2):
+                if self.x_first:
+                    mine = self.own[z, other, place.x, :, self.cols].astype(F32)
+                else:
+                    mine = self.own[z, place.y, other, :, self.cols].astype(F32)
+                theirs = self.first[z, other].astype(F32)
+                self.first[z, other] = (mine + theirs).astype(self.first.dtype)
+            return carry
+
+        lax.fori_loop(0, Z_SIZE, add, 0)
+        self.over_second.start()
+
+    def add_second(self):
+        self.over_second.wait_recv()
+
+        def add(z, carry):
+            mine = self.first[z, self.kept].astype(F32)
+            theirs = self.second[z].astype(F32)
+            self.second[z] = (mine + theirs).astype(self.second.dtype)
+            return carry
+
+        lax.fori_loop(0, Z_SIZE, add, 0)
+        for copy in self.along_z:
+            copy.start()
+
+    def finish(self):
+        total = self.second[self.place.z].astype(F32)
+        for step, copy in enumerate(self.along_z):
+            copy.wait_recv()
+            total = total + self.third[step].astype(F32)
+        self.out[:, self.cols] = total
+
+    def settle(self):
+        for copy in [self.to_core, self.over_first, self.over_second] + self.along_z:
+            copy.wait_send()
+
+
+def reduce_buffers(rows, width, dtype):
+    cuts = [(0, width)] if width <= LANES else halves(width)
+    shapes = [pltpu.VMEM((Z_SIZE, 2, 2, rows, width), dtype)]
+    for _, size in cuts:
+        shapes.append(pltpu.VMEM((Z_SIZE, 2, rows, size), dtype))
+        shapes.append(pltpu.VMEM((Z_SIZE, rows, size), dtype))
+        shapes.append(pltpu.VMEM((Z_SIZE - 1, rows, size), dtype))
+    return shapes, cuts
+
+
+def reduce_kernel(count, *refs):
+    grads, outs, table = refs[:count], refs[count : 2 * count], refs[2 * count]
+    refs = list(refs[2 * count + 1 :])
+    send, recv, local = refs[-3:]
+    place = Place()
+    meet(place)
+    sems = Sems(send, recv)
+    chunks = []
+    for grad, out in zip(grads, outs):
+        rows, width = grad.shape[4:]
+        _, cuts = reduce_buffers(rows, width, grad.dtype)
+        own = refs.pop(0)
+        for half, (start, size) in enumerate(cuts):
+            first, second, third = refs.pop(0), refs.pop(0), refs.pop(0)
+            chunks.append(
+                Reduce(place, grad, own, first, second, third, out, start, size, half == 0, sems)
+            )
+    for chunk in chunks:
+        chunk.begin()
+    steps = []
+    for number, chunk in enumerate(chunks):
+        for lag, step in enumerate(
+            (chunk.add_core, chunk.add_first, chunk.add_second, chunk.finish)
+        ):
+            steps.append((number // 2 + lag, -lag, number, step))
+    for _, _, _, step in sorted(steps, key=lambda entry: entry[:3]):
+        step()
+    spread = Gather(
+        place, outs[0].at[16:24], table, slice(None), True, sems, local.at[0]
+    )
+    for step in (spread.begin, spread.second, spread.third, spread.fourth, spread.arrive, spread.settle):
+        step()
+    for chunk in chunks:
+        chunk.settle()
+
+
+def reduce_all(grads):
+    count = len(grads)
+    vmem = pl.BlockSpec(memory_space=pltpu.VMEM)
+    scratch, chunks = [], 0
+    for grad in grads:
+        shapes, cuts = reduce_buffers(grad.shape[4], grad.shape[5], grad.dtype)
+        scratch += shapes
+        chunks += len(cuts)
+    copies = REDUCE_COPIES * chunks + GATHER_COPIES
+    return pl.pallas_call(
+        partial(reduce_kernel, count),
+        out_shape=tuple(jax.ShapeDtypeStruct(grad.shape[4:], F32) for grad in grads)
+        + (jax.ShapeDtypeStruct((Z_SIZE, 2, 2, 2, 8, LANES), F32),),
+        in_specs=[vmem] * count,
+        out_specs=(vmem,) * (count + 1),
+        scratch_shapes=scratch
+        + [
+            pltpu.SemaphoreType.DMA((copies,)),
+            pltpu.SemaphoreType.DMA((copies,)),
+            pltpu.SemaphoreType.DMA((1,)),
+        ],
+        compiler_params=pltpu.CompilerParams(
+            collective_id=1, has_side_effects=True, vmem_limit_bytes=60 << 20
+        ),
+    )(*grads)
+
+
 def layer_norm(values, gain, shift):
     centred = values - jnp.mean(values, axis=-1, keepdims=True)
     inv_std = lax.rsqrt(jnp.mean(centred * centred, axis=-1, keepdims=True) + EPSILON)
@@ -242,7 +594,7 @@
     return jnp.sum(values.astype(jnp.float32), axis=0)
 
 
-def per_device(
+def per_device_native(
     tokens,
     cotangent,
     counts,
@@ -435,6 +787,219 @@
     return (output, grad_inputs) + tuple(summed) + (table_total,)
 
 
+def per_device_linked(
+    tokens,
+    cotangent,
+    counts,
+    widths,
+    norm1_gain,
+    norm1_shift,
+    w_qkv,
+    q_bias,
+    v_bias,
+    w_proj,
+    proj_bias,
+    gamma1,
+    norm2_gain,
+    norm2_shift,
+    w_fc1,
+    fc1_bias,
+    w_fc2,
+    fc2_bias,
+    gamma2,
+    bias_table,
+):
+    shard = norm1_gain.shape[0]
+    vectors = [
+        norm1_gain, norm1_shift, q_bias, v_bias, proj_bias, gamma1, norm2_gain, norm2_shift, fc2_bias, gamma2,
+    ]
+    lines = jnp.stack(vectors).astype(F32)
+    hidden_lines = fc1_bias.astype(F32).reshape(1, -1)
+    packed = jnp.concatenate(
+        [
+            jnp.pad(lines, ((0, 16 - len(vectors)), (0, LANES - shard))),
+            jnp.pad(hidden_lines, ((0, 7), (0, LANES - hidden_lines.shape[1]))),
+        ]
+    )
+    packed, qkv_weight, proj_weight, fc1_weight, fc2_weight = gather_all(
+        [packed, w_qkv, w_proj, w_fc1, w_fc2]
+    )
+    packed = packed.reshape(-1, 24, LANES)
+    (
+        gain_one, shift_one, query_bias, value_bias, proj_shift, scale_one, gain_two, shift_two, fc2_shift, scale_two,
+    ) = packed[:, : len(vectors), :shard].transpose(1, 0, 2).reshape(len(vectors), -1)
+    fc1_shift = packed[:, 16, : fc1_bias.shape[0]].reshape(-1)
+    qkv_weight, proj_weight, fc1_weight, fc2_weight = (
+        weight.reshape(-1, weight.shape[-1])
+        for weight in (qkv_weight, proj_weight, fc1_weight, fc2_weight)
+    )
+    gain_one = gain_one.astype(jnp.float32)
+    shift_one = shift_one.astype(jnp.float32)
+    proj_shift = proj_shift.astype(jnp.float32)
+    scale_one = scale_one.astype(jnp.float32)
+    gain_two = gain_two.astype(jnp.float32)
+    shift_two = shift_two.astype(jnp.float32)
+    fc1_shift = fc1_shift.astype(jnp.float32)
+    fc2_shift = fc2_shift.astype(jnp.float32)
+    scale_two = scale_two.astype(jnp.float32)
+    local_rows = tokens.shape[0]
+    width_model = tokens.shape[1]
+    seq_len = local_rows * lax.axis_size("seq")
+    offset = lax.axis_index("seq") * local_rows
+    row_span = (seq_len - 1) // (SIDE // 2) + 1
+    table_rows = bias_table.shape[0]
+    entries = -(-table_rows // (2 * LANES)) * 2 * LANES
+    table_lines = jnp.pad(
+        bias_table.T, ((0, HEAD_ROWS - HEADS), (0, entries - table_rows))
+    )
+    scalars = jnp.stack([widths[0], counts[0], offset.astype(jnp.int32)])
+    smem = pl.BlockSpec(memory_space=pltpu.SMEM)
+    vmem = pl.BlockSpec(memory_space=pltpu.VMEM)
+    params = pltpu.CompilerParams(vmem_limit_bytes=40 << 20)
+
+    inputs_f = tokens.astype(jnp.float32)
+    normed_full, normed_one, inv_std_one = layer_norm(inputs_f, gain_one, shift_one)
+    normed_low = normed_full.astype(jnp.bfloat16)
+    qkv_shift = jnp.concatenate(
+        [query_bias, jnp.zeros((width_model,), F32), value_bias]
+    ).astype(jnp.float32)
+    projected = (
+        jnp.dot(normed_low, qkv_weight, preferred_element_type=jnp.float32) + qkv_shift
+    ).astype(jnp.bfloat16)
+    queries = projected[:, :width_model]
+    key_local = projected[:, width_model:]
+    keys_all = lax.all_gather(key_local, "seq", axis=0, tiled=True)
+
+    attn_low, probs = pl.pallas_call(
+        partial(attend_kernel, row_span),
+        out_shape=(
+            jax.ShapeDtypeStruct((local_rows, width_model), BF16),
+            jax.ShapeDtypeStruct((HEADS, local_rows, seq_len), F32),
+        ),
+        in_specs=[smem, vmem, vmem, vmem],
+        out_specs=(vmem, vmem),
+        scratch_shapes=[pltpu.VMEM((HEAD_ROWS, 2 * (local_rows + seq_len)), F32)],
+        compiler_params=params,
+    )(scalars, queries, keys_all, table_lines)
+    branch_one = jnp.dot(attn_low, proj_weight, preferred_element_type=jnp.float32) + proj_shift
+    residual_one = inputs_f + scale_one * branch_one
+    normed_full_two, normed_two, inv_std_two = layer_norm(residual_one, gain_two, shift_two)
+    normed_low_two = normed_full_two.astype(jnp.bfloat16)
+    pre_act = jnp.dot(normed_low_two, fc1_weight, preferred_element_type=jnp.float32) + fc1_shift
+    activated, gelu_pull = jax.vjp(partial(jax.nn.gelu, approximate=False), pre_act)
+    hidden = activated.astype(jnp.bfloat16)
+    branch_two = jnp.dot(hidden, fc2_weight, preferred_element_type=jnp.float32) + fc2_shift
+    output = (residual_one + scale_two * branch_two).astype(jnp.bfloat16)
+    grad_out = cotangent.astype(jnp.float32)
+    grad_scale_two = jnp.sum(grad_out * branch_two, axis=0)
+    grad_branch_two = (scale_two * grad_out).astype(jnp.bfloat16)
+    grad_fc2_weight = jnp.einsum(
+        "tf,td->fd", hidden, grad_branch_two, preferred_element_type=jnp.float32
+    )
+    grad_fc2_shift = row_sum(grad_branch_two)
+    grad_hidden = jnp.einsum(
+        "td,fd->tf", grad_branch_two, fc2_weight, preferred_element_type=jnp.float32
+    )
+    grad_pre = gelu_pull(grad_hidden)[0].astype(jnp.bfloat16)
+    grad_fc1_weight = jnp.einsum(
+        "td,tf->df", normed_low_two, grad_pre, preferred_element_type=jnp.float32
+    )
+    grad_fc1_shift = row_sum(grad_pre)
+    grad_normed_two = jnp.einsum(
+        "tf,df->td", grad_pre, fc1_weight, preferred_element_type=jnp.float32
+    )
+    grad_gain_two = jnp.sum(grad_normed_two * normed_two, axis=0)
+    grad_shift_two = jnp.sum(grad_normed_two, axis=0)
+    grad_resid = grad_out + norm_back(grad_normed_two, normed_two, inv_std_two, gain_two)
+    grad_scale_one = jnp.sum(grad_resid * branch_one, axis=0)
+    grad_branch_one = (scale_one * grad_resid).astype(jnp.bfloat16)
+    grad_proj_weight = jnp.einsum(
+        "td,te->de", attn_low, grad_branch_one, preferred_element_type=jnp.float32
+    )
+    grad_proj_shift = row_sum(grad_branch_one)
+    grad_attn = jnp.einsum(
+        "te,de->td", grad_branch_one, proj_weight, preferred_element_type=jnp.float32
+    ).astype(jnp.bfloat16)
+    grad_query, key_terms, table_grad = pl.pallas_call(
+        partial(attend_back_kernel, row_span),
+        out_shape=(
+            jax.ShapeDtypeStruct((local_rows, width_model), BF16),
+            jax.ShapeDtypeStruct((seq_len, 2 * width_model), BF16),
+            jax.ShapeDtypeStruct((HEAD_ROWS, entries), F32),
+        ),
+        in_specs=[smem, vmem, vmem, vmem, vmem],
+        out_specs=(vmem, vmem, vmem),
+        scratch_shapes=[
+            pltpu.VMEM(((local_rows + seq_len) // LANES, 2 * HEAD_ROWS * 8, LANES), F32)
+        ],
+        compiler_params=params,
+    )(scalars, queries, keys_all, probs, grad_attn)
+    own_terms = lax.psum_scatter(key_terms, "seq", scatter_dimension=0, tiled=True)
+    grad_qkv = jnp.concatenate([grad_query, own_terms], axis=1)
+    grad_qkv_weight = jnp.einsum(
+        "td,te->de", normed_low, grad_qkv, preferred_element_type=jnp.float32
+    )
+    grad_query_bias = row_sum(grad_qkv[:, :width_model])
+    grad_value_bias = row_sum(grad_qkv[:, 2 * width_model :])
+    grad_normed_one = jnp.einsum(
+        "te,de->td", grad_qkv, qkv_weight, preferred_element_type=jnp.float32
+    )
+    grad_gain_one = jnp.sum(grad_normed_one * normed_one, axis=0)
+    grad_shift_one = jnp.sum(grad_normed_one, axis=0)
+    grad_inputs = (
+        grad_resid + norm_back(grad_normed_one, normed_one, inv_std_one, gain_one)
+    ).astype(jnp.bfloat16)
+    lines = jnp.stack(
+        [
+            grad_gain_one, grad_shift_one, grad_query_bias, grad_value_bias, grad_proj_shift,
+            grad_scale_one, grad_gain_two, grad_shift_two, grad_fc2_shift, grad_scale_two,
+        ]
+    )
+    devices = 8 * Z_SIZE
+    lines = lines.reshape(len(vectors), devices, shard).transpose(1, 0, 2)
+    hidden_lines = grad_fc1_shift.reshape(devices, 1, -1)
+    table_blocks = table_grad.reshape(2, 8, devices // 2, LANES).transpose(2, 0, 1, 3)
+    small = jnp.concatenate(
+        [
+            jnp.pad(lines, ((0, 0), (0, 0), (0, LANES - shard))),
+            jnp.pad(hidden_lines, ((0, 0), (0, 5), (0, LANES - hidden_lines.shape[2]))),
+            table_blocks.reshape(devices, 8, LANES),
+        ],
+        axis=1,
+    )
+
+    def slots(values):
+        return values.reshape(Z_SIZE, 2, 2, 2, -1, values.shape[-1])
+
+    small, sum_fc2, sum_fc1, sum_proj, sum_qkv, table_all = reduce_all(
+        [slots(small)]
+        + [
+            slots(grad.astype(BF16))
+            for grad in (grad_fc2_weight, grad_fc1_weight, grad_proj_weight, grad_qkv_weight)
+        ]
+    )
+    (
+        sum_gain_one, sum_shift_one, sum_query, sum_value, sum_proj_shift,
+        sum_scale_one, sum_gain_two, sum_shift_two, sum_fc2_shift, sum_scale_two,
+    ) = (small[line, :shard] for line in range(len(vectors)))
+    summed = (
+        sum_gain_one, sum_shift_one, sum_qkv, sum_query, sum_value, sum_proj, sum_proj_shift, sum_scale_one,
+        sum_gain_two, sum_shift_two, sum_fc1, small[len(vectors), : fc1_bias.shape[0]], sum_fc2, sum_fc2_shift,
+        sum_scale_two,
+    )
+    table_total = (
+        table_all.reshape(devices // 2, 2, 8, LANES).transpose(1, 2, 0, 3).reshape(HEAD_ROWS, -1)
+    )[:HEADS, :table_rows].T
+    return (output, grad_inputs) + summed + (table_total,)
+
+
+def per_device(*arrays):
+    devices = lax.axis_size("img") * lax.axis_size("seq")
+    linked = lax.axis_size("img") == 4 * Z_SIZE and lax.axis_size("seq") == 2
+    linked = linked and arrays[6].shape[0] % 8 == 0 and devices * 64 >= arrays[19].shape[0]
+    return per_device_linked(*arrays) if linked else per_device_native(*arrays)
+
+
 def solution(mesh):
     return jax.shard_map(
         per_device,

time: 947 us -> 312 us (0.33)
  waiting for transfers between devices: 745 us -> 3.79 us
  Pallas kernels: 14.2 us -> 217 us
  blocking collectives: 95.6 us -> 12.2 us
  matrix products: 45.2 us -> 32.7 us
    reduce_scatter x5 -> x1, waiting for transfers between devices: 472 us -> 3.77 us  [per_device_linked(): lax.psum_scatter(key_terms, 'seq', scatter_dimension=0, tiled=True)]
    pallas_call x2 -> x4, Pallas kernels: 14.2 us -> 217 us  [the longest x1 122 us: reduce_all(): pl.pallas_call(partial(reduce_kernel, count), out_shape=tuple((jax.ShapeD...]
    all_gather x4 -> x0, waiting for transfers between devices: 158 us -> none  [the longest x1 62.1 us: per_device(): lax.all_gather(w_fc1, ('img', 'seq'), axis=0, tiled=True)]
    psum x1 -> x0, waiting for transfers between devices: 112 us -> none  [per_device(): table_total = lax.psum(table_grad, ('img', 'seq'))[:HEADS, :table_rows].T]
    unnamed x2 -> x0, blocking collectives: 83.1 us -> none
    unnamed x111 -> x132, local copies, waits for them, and re-layouts: 18.7 us -> 4.63 us
    dot_general x12, matrix products: 45.2 us -> 32.7 us  [the longest x1 6.32 us: per_device_linked(): jnp.dot(normed_low_two, fc1_weight, preferred_element_type=jnp.float32)]
  transfers between devices with their start and end apart: 10 -> 1, of which waited for: 10 -> 1; matrix products, arithmetic and copies ran while one was open for 6% -> 5% of each run, Pallas kernels for 1% -> 0%
where the time goes in v2:
time: 312 us; the launch traced here: 311 us
  Pallas kernels  217 us (70%)
  matrix products  32.7 us (10%)
  local copies, waits for them, and re-layouts  22.9 us (7%)
  between operations  16.3 us (5%)
  blocking collectives  12.2 us (4%)
  other arithmetic  6.19 us (2%)
  waiting for transfers between devices  3.79 us (1%)
    pallas_call x1, Pallas kernels, reduce_all(): pl.pallas_call(partial(reduce_kernel, count), out_shape=tuple((jax.ShapeD...  122 us
    pallas_call x1, Pallas kernels, gather_all(): pl.pallas_call(partial(gather_kernel, count), out_shape=tuple((jax.ShapeD...  80.9 us
    all_gather x1, blocking collectives, per_device_linked(): keys_all = lax.all_gather(key_local, 'seq', axis=0, tiled=True)  12.2 us
    pallas_call x1, Pallas kernels, per_device_linked(): pl.pallas_call(partial(attend_back_kernel, row_span), out_shape=(jax.Shap...  8.38 us
    dot_general x1, matrix products, per_device_linked(): jnp.dot(normed_low_two, fc1_weight, preferred_element_type=jnp.float32)  6.32 us
  transfers between devices with their start and end apart: 1, of which 1 were waited for; matrix products, arithmetic and copies ran while one was open for 5% of the time, Pallas kernels for 0%

profile of v2, /device:TPU:0, one launch (start us, length us, event | category | flops | bytes accessed | tf_op | source)
XLA Modules:
  0.0 311.1 jit_solution(4293588129612929709)
XLA Ops:
  7.3 1.5 stack.82
  8.8 1.3 fusion.32.refs_0_
  10.0 80.9 %shard_map.331 = (f32[4,2,2,2,24,128]{5,4,3,2,1,0:T(8,128)}, bf16[4,2,2,2,24,2304]{5,4,3,2,1,0:T(8,128)(2,1)}, bf16[4,2,2,2,24,768]{5,4,3,2,1,0:T(8,128)(2,1)}, ...) custom-call(f32[24,128]{1,0:T(8,128)} %fusion.32.refs_0_, bf16[24,2304]{1,0:T(8,128)(2,1)} %refs_1_.1, ...), custom_call_target="tpu_custom_call" | custom-call | tf_op jit(solution)/shard_map/pallas_call | solution.py:397
  91.0 0.9 slice_reduce_fusion
  91.9 1.0 slice.78
  92.9 1.0 convert_reduce_fusion.1
  94.0 1.1 fusion.21
  96.0 2.7 fusion
  100.2 0.7 add.112
  101.2 0.7 add.115
  101.9 12.2 %all_gather.3.kv_ref = bf16[256,1536]{1,0:T(8,128)(2,1)S(1)} all-gather(bf16[128,1536]{1,0:T(8,128)(2,1)S(1)} %slice.80), channel_id=1, replica_groups=mesh['img'=16,'seq'=2] {'seq'}, dimensions={0}, use_global_device_ids=true | all-gather | bytes 1179648 | tf_op jit(solution)/shard_map/all_gather | solution.py:871
  114.3 5.7 %shard_map.332 = (bf16[128,768]{1,0:T(8,128)(2,1)S(1)}, f32[12,128,256]{2,1,0:T(8,128)S(1)}) custom-call(s32[3]{0:T(128)S(1)} %pad_add_fusion.scal_ref, bf16[128,768]{1,0:T(8,128)(2,1)S(1)} %slice.79.query_ref, bf16[256,1536]{1,0:T(8,128)(2,1)S(1)} %all_gather.3.kv_ref, bf16[16,2048]{1,0:T(8,128)(2,1)S(1)} %pad.24.table_ref), custom_call_target="tpu_custom_call" | custom-call | tf_op jit(solution)/shard_map/pallas_call | solution.py:873
  120.0 0.4 fusion.36
  120.8 6.3 %multiply_convert_fusion = (bf16[128,3072]{1,0:T(8,128)(2,1)S(1)}, f32[128,3072]{1,0:T(8,128)S(1)}, f32[128,3072]{1,0:T(8,128)S(1)}) fusion(f32[3072]{0:T(1024)S(1)} %copy-done.46, bf16[768,3072]{1,0:T(8,128)(2,1)} %bitcast.92, f32[128,768]{1,0:T(8,128)S(1)} %get-tuple-element.67, f32[768]{0:T(1024)S(1)} %add.109, f32[768]{0:T(1024)S(1)} %mul.180, ...), kind=kOutput, calls=%fused_computation.10 | convolution fusion | flops 630423552 | bytes 9063424 | tf_op jit(solution)/shard_map/dot_general | solution.py:888
  127.1 2.5 convert_reduce_fusion
  129.7 2.3 multiply_reduce_fusion
  132.0 2.2 fusion.23
  134.3 0.7 convert_reduce_fusion.3
  135.0 0.5 convolution_convert_fusion.4.grad_ref
  135.6 8.4 %shard_map.333 = (bf16[128,768]{1,0:T(8,128)(2,1)S(1)}, bf16[256,1536]{1,0:T(8,128)(2,1)}, f32[16,2048]{1,0:T(8,128)S(1)}) custom-call(s32[3]{0:T(128)S(1)} %pad_add_fusion.scal_ref, bf16[128,768]{1,0:T(8,128)(2,1)S(1)} %slice.79.query_ref, bf16[256,1536]{1,0:T(8,128)(2,1)S(1)} %all_gather.3.kv_ref, f32[12,128,256]{2,1,0:T(8,128)S(1)} %get-tuple-element.40.probs_ref, ...), custom_call_target="tpu_custom_call" | custom-call | tf_op jit(solution)/shard_map/pallas_call | solution.py:923
  144.1 0.7 stack.94
  144.8 0.7 stack.91
  145.5 0.7 stack.93
  146.2 0.7 stack.90
  146.9 0.7 stack.92
  147.6 0.7 pad.26
  148.2 0.7 copy.42
  148.9 0.7 stack.87
  149.6 0.7 stack.89
  150.3 0.7 constant_dynamic-update-slice_fusion.1
  151.0 1.5 convolution_convert_fusion.3
  152.5 3.6 %convolution_convert_fusion.2 = bf16[3072,768]{1,0:T(8,128)(2,1)} fusion(bf16[128,3072]{1,0:T(8,128)(2,1)S(1)} %get-tuple-element.64, bf16[128,768]{1,0:T(8,128)(2,1)S(1)} %copy-done.14, f32[768]{0:T(1024)S(1)} %mul.175), kind=kOutput, calls=%fused_computation.2 | convolution fusion | flops 606633984 | bytes 5704704 | tf_op jit(solution)/shard_map/tf,td->fd/dot_general | solution.py:896
  156.1 3.7 %convolution_convert_fusion.1 = bf16[768,3072]{1,0:T(8,128)(2,1)} fusion(bf16[128,3072]{1,0:T(8,128)(2,1)S(1)} %copy-done.11, f32[128,768]{1,0:T(8,128)S(1)} %copy-done.2, f32[768]{0:T(1024)S(1)} %add.109, f32[768]{0:T(1024)S(1)} %mul.180, f32[128]{0:T(128)S(1)} %copy-done.51, f32[128]{0:T(128)S(1)} %copy-done.44), kind=kOutput, calls=%fused_computation.1 | convolution fusion | flops 606830592 | bytes 5905408 | tf_op jit(solution)/shard_map/td,tf->df/dot_general | solution.py:904
  159.8 3.8 %reduce-scatter.2.cloned.1.call-done = bf16[128,1536]{1,0:T(8,128)(2,1)} async-done(((bf16[256,1536]{1,0:T(8,128)(2,1)}), bf16[128,1536]{1,0:T(8,128)(2,1)}) %reduce-scatter.2.cloned.1.call-update) | async-done | bytes 393232 | tf_op jit(solution)/shard_map/reduce_scatter | solution.py:937
  163.6 1.8 constant_dynamic-update-slice_fusion
  165.4 3.9 %fusion.20 = (f32[768]{0:T(1024)S(1)}, f32[128]{0:T(128)}, f32[128]{0:T(128)}, f32[768]{0:T(1024)S(1)}, f32[128,768]{1,0:T(8,128)}) fusion(bf16[128,768]{1,0:T(8,128)(2,1)} %param.20, f32[128]{0:T(128)} %copy-done.47, f32[128]{0:T(128)} %copy-done.40, f32[768]{0:T(1024)S(1)} %mul.171, bf16[128,2304]{1,0:T(8,128)(2,1)} %constant_dynamic-update-slice_fusion, ...), kind=kOutput, calls=%fused_computation.47 | convolution fusion | flops 453966080 | bytes 4729856 | tf_op jit(solution)/shard_map/te,de->td/dot_general | solution.py:944
  169.4 3.0 convolution_convert_fusion
  173.4 0.8 pad_maximum_fusion.refs_0_
  174.2 122.0 %shard_map.334 = (f32[24,128]{1,0:T(8,128)}, f32[96,768]{1,0:T(8,128)}, f32[24,3072]{1,0:T(8,128)}, f32[24,768]{1,0:T(8,128)}, f32[24,2304]{1,0:T(8,128)}, /*index=5*/f32[4,2,2,2,8,128]{5,4,3,2,1,0:T(8,128)}) custom-call(f32[4,2,2,2,24,128]{5,4,3,2,1,0:T(8,128)} %pad_maximum_fusion.refs_0_, bf16[4,2,2,2,96,768]{5,4,3,2,1,0:T(8,128)(2,1)} %bitcast.82, ...), custom_call_target="tpu_custom_call" | custom-call | tf_op jit(solution)/shard_map/pallas_call | solution.py:559
  296.2 1.3 slice_bitcast_fusion.3
  297.5 1.5 slice_bitcast_fusion.1
  299.1 0.9 copy_bitcast_fusion.1
  300.0 0.7 slice_bitcast_fusion
  300.7 0.9 fusion.19
  301.5 0.7 copy.65
  302.2 0.6 copy.66
  302.9 0.7 copy.67
  303.6 0.7 copy.68
  (163 shorter events, 2.8 us)
Async XLA Ops:
  7.2 88.8 %copy-start.3 = (bf16[128,768]{1,0:T(8,128)(2,1)S(1)}, bf16[128,768]{1,0:T(8,128)(2,1)}, u32[]{:S(2)}) copy-start(bf16[128,768]{1,0:T(8,128)(2,1)} %param.20) | copy-start | bytes 589828
  7.2 156.4 %reduce-scatter.2.cloned.1.call-start = ((), (), s32[]{:S(2)}) async-start(), calls=%async_computation.1 | async-start | bytes 1179648 | tf_op jit(solution)/shard_map/reduce_scatter | solution.py:937
  94.0 4.7 %copy-start.40 = (f32[128]{0:T(128)}, f32[128]{0:T(128)S(1)}, u32[]{:S(2)}) copy-start(f32[128]{0:T(128)S(1)} %broadcast_multiply_fusion.5) | copy-start | bytes 1540
  95.1 3.6 %copy-start.47 = (f32[128]{0:T(128)}, f32[128]{0:T(128)S(1)}, u32[]{:S(2)}) copy-start(f32[128]{0:T(128)S(1)} %add_rsqrt_fusion.1) | copy-start | bytes 1540
  98.7 15.5 %copy-start.28 = (bf16[1953,12]{0,1:T(8,128)(2,1)S(1)}, bf16[1953,12]{0,1:T(8,128)(2,1)}, u32[]{:S(2)}) copy-start(bf16[1953,12]{0,1:T(8,128)(2,1)} %param.39) | copy-start | bytes 140620
  98.7 21.3 %copy-start.6 = (bf16[4,2,2,2,24,768]{5,4,3,2,1,0:T(8,128)(2,1)S(1)}, bf16[4,2,2,2,24,768]{5,4,3,2,1,0:T(8,128)(2,1)}, u32[]{:S(2)}) copy-start(bf16[4,2,2,2,24,768]{5,4,3,2,1,0:T(8,128)(2,1)} %get-tuple-element.37) | copy-start | bytes 3538948
  101.2 19.3 %copy-start.29 = (f32[768]{0:T(1024)}, f32[768]{0:T(1024)S(1)}, u32[]{:S(2)}) copy-start(f32[768]{0:T(1024)S(1)} %mul.165) | copy-start | bytes 9220
  120.0 7.1 %slice-start = ((s8[4718592]{0:T(1024)(128)(4,1)}), s8[4194304]{0:T(1024)(128)(4,1)S(1)}, s32[]{:S(2)}) async-start(s8[4718592]{0:T(1024)(128)(4,1)} %bitcast.88), calls=%async_computation.2 | async-start | bytes 8388608
  120.0 9.6 %slice-start.2 = ((s8[4718592]{0:T(1024)(128)(4,1)}), s8[4194304]{0:T(1024)(128)(4,1)S(1)}, s32[]{:S(2)}) async-start(s8[4718592]{0:T(1024)(128)(4,1)} %bitcast.93), calls=%async_computation.4 | async-start | bytes 8388608
  120.5 11.5 %copy-start.1 = (f32[128,768]{1,0:T(8,128)}, f32[128,768]{1,0:T(8,128)S(1)}, u32[]{:S(2)}) copy-start(f32[128,768]{1,0:T(8,128)S(1)} %get-tuple-element.67) | copy-start | bytes 1179652
  120.5 11.5 %copy-start.43 = (f32[128]{0:T(128)}, f32[128]{0:T(128)S(1)}, u32[]{:S(2)}) copy-start(f32[128]{0:T(128)S(1)} %broadcast_multiply_fusion.4) | copy-start | bytes 1540
  120.7 11.3 %copy-start.50 = (f32[128]{0:T(128)}, f32[128]{0:T(128)S(1)}, u32[]{:S(2)}) copy-start(f32[128]{0:T(128)S(1)} %add_rsqrt_fusion) | copy-start | bytes 1540
  120.7 6.4 %slice-start.1 = ((s8[4718592]{0:T(1024)(128)(4,1)}), s8[524288]{0:T(1024)(128)(4,1)S(1)}, s32[]{:S(2)}) async-start(s8[4718592]{0:T(1024)(128)(4,1)} %bitcast.88), calls=%async_computation.3 | async-start | bytes 1048576
  120.7 6.4 %copy-start.14 = (bf16[128,768]{1,0:T(8,128)(2,1)S(1)}, bf16[128,768]{1,0:T(8,128)(2,1)}, u32[]{:S(2)}) copy-start(bf16[128,768]{1,0:T(8,128)(2,1)} %param.21) | copy-start | bytes 589828
  120.7 8.9 %slice-start.3 = ((s8[4718592]{0:T(1024)(128)(4,1)}), s8[524288]{0:T(1024)(128)(4,1)S(1)}, s32[]{:S(2)}) async-start(s8[4718592]{0:T(1024)(128)(4,1)} %bitcast.93), calls=%async_computation.5 | async-start | bytes 1048576
  135.5 8.5 %copy-start.45 = (f32[3072]{0:T(1024)S(1)}, f32[3072]{0:T(1024)}, u32[]{:S(2)}) copy-start(f32[3072]{0:T(1024)} %get-tuple-element.95) | copy-start | bytes 36868
  135.5 8.6 %copy-start.36 = (f32[768]{0:T(1024)S(1)}, f32[768]{0:T(1024)}, u32[]{:S(2)}) copy-start(f32[768]{0:T(1024)} %get-tuple-element.58) | copy-start | bytes 9220
  135.5 9.3 %copy-start.38 = (f32[768]{0:T(1024)S(1)}, f32[768]{0:T(1024)}, u32[]{:S(2)}) copy-start(f32[768]{0:T(1024)} %get-tuple-element.50) | copy-start | bytes 9220
  135.5 9.9 %copy-start.35 = (f32[768]{0:T(1024)S(1)}, f32[768]{0:T(1024)}, u32[]{:S(2)}) copy-start(f32[768]{0:T(1024)} %get-tuple-element.59) | copy-start | bytes 9220
  135.6 10.6 %copy-start.34 = (f32[768]{0:T(1024)S(1)}, f32[768]{0:T(1024)}, u32[]{:S(2)}) copy-start(f32[768]{0:T(1024)} %get-tuple-element.69) | copy-start | bytes 9220
  135.6 11.3 %copy-start.37 = (f32[768]{0:T(1024)S(1)}, f32[768]{0:T(1024)}, u32[]{:S(2)}) copy-start(f32[768]{0:T(1024)} %get-tuple-element.56) | copy-start | bytes 9220
  135.6 14.0 %copy-start.39 = (f32[768]{0:T(1024)S(1)}, f32[768]{0:T(1024)}, u32[]{:S(2)}) copy-start(f32[768]{0:T(1024)} %get-tuple-element.62) | copy-start | bytes 9220
  152.5 3.6 %copy-start.2 = (f32[128,768]{1,0:T(8,128)S(1)}, f32[128,768]{1,0:T(8,128)}, u32[]{:S(2)}) copy-start(f32[128,768]{1,0:T(8,128)} %copy-done.1) | copy-start | bytes 1179652
  152.5 3.6 %copy-start.11 = (bf16[128,3072]{1,0:T(8,128)(2,1)S(1)}, bf16[128,3072]{1,0:T(8,128)(2,1)}, u32[]{:S(2)}) copy-start(bf16[128,3072]{1,0:T(8,128)(2,1)} %copy-done.10) | copy-start | bytes 2359300
  152.5 3.6 %copy-start.44 = (f32[128]{0:T(128)S(1)}, f32[128]{0:T(128)}, u32[]{:S(2)}) copy-start(f32[128]{0:T(128)} %copy-done.43) | copy-start | bytes 1540
  152.5 3.6 %copy-start.51 = (f32[128]{0:T(128)S(1)}, f32[128]{0:T(128)}, u32[]{:S(2)}) copy-start(f32[128]{0:T(128)} %copy-done.50) | copy-start | bytes 1540
  156.1 9.3 %copy-start = (bf16[4,2,2,2,24,2304]{5,4,3,2,1,0:T(8,128)(2,1)S(1)}, bf16[4,2,2,2,24,2304]{5,4,3,2,1,0:T(8,128)(2,1)}, u32[]{:S(2)}) copy-start(bf16[4,2,2,2,24,2304]{5,4,3,2,1,0:T(8,128)(2,1)} %get-tuple-element.35) | copy-start | bytes 10616836
  165.4 3.9 %copy-start.4 = (bf16[128,768]{1,0:T(8,128)(2,1)S(1)}, bf16[128,768]{1,0:T(8,128)(2,1)}, u32[]{:S(2)}) copy-start(bf16[128,768]{1,0:T(8,128)(2,1)} %param.20) | copy-start | bytes 589828
  165.4 3.9 %copy-start.9 = (bf16[128,2304]{1,0:T(8,128)(2,1)S(1)}, bf16[128,2304]{1,0:T(8,128)(2,1)}, u32[]{:S(2)}) copy-start(bf16[128,2304]{1,0:T(8,128)(2,1)} %constant_dynamic-update-slice_fusion) | copy-start | bytes 1769476
  165.4 3.9 %copy-start.32 = (f32[768]{0:T(1024)S(1)}, f32[768]{0:T(1024)}, u32[]{:S(2)}) copy-start(f32[768]{0:T(1024)} %copy-done.31) | copy-start | bytes 9220
  165.4 3.9 %copy-start.41 = (f32[128]{0:T(128)S(1)}, f32[128]{0:T(128)}, u32[]{:S(2)}) copy-start(f32[128]{0:T(128)} %copy-done.40) | copy-start | bytes 1540
  165.4 3.9 %copy-start.48 = (f32[128]{0:T(128)S(1)}, f32[128]{0:T(128)}, u32[]{:S(2)}) copy-start(f32[128]{0:T(128)} %copy-done.47) | copy-start | bytes 1540
  169.3 3.5 %copy-start.25 = (f32[1,32,24]{2,1,0:T(8,128)S(1)}, f32[1,32,24]{2,1,0:T(8,128)}, u32[]{:S(2)}) copy-start(f32[1,32,24]{2,1,0:T(8,128)} %stack.90) | copy-start | bytes 9220
  169.3 3.5 %copy-start.23 = (f32[1,32,24]{2,1,0:T(8,128)S(1)}, f32[1,32,24]{2,1,0:T(8,128)}, u32[]{:S(2)}) copy-start(f32[1,32,24]{2,1,0:T(8,128)} %stack.91) | copy-start | bytes 9220
  169.3 3.5 %copy-start.24 = (f32[1,32,24]{2,1,0:T(8,128)S(1)}, f32[1,32,24]{2,1,0:T(8,128)}, u32[]{:S(2)}) copy-start(f32[1,32,24]{2,1,0:T(8,128)} %stack.92) | copy-start | bytes 9220
  169.3 3.5 %copy-start.22 = (f32[1,32,24]{2,1,0:T(8,128)S(1)}, f32[1,32,24]{2,1,0:T(8,128)}, u32[]{:S(2)}) copy-start(f32[1,32,24]{2,1,0:T(8,128)} %stack.93) | copy-start | bytes 9220
  169.3 3.5 %copy-start.21 = (f32[1,32,24]{2,1,0:T(8,128)S(1)}, f32[1,32,24]{2,1,0:T(8,128)}, u32[]{:S(2)}) copy-start(f32[1,32,24]{2,1,0:T(8,128)} %stack.94) | copy-start | bytes 9220
  174.2 124.8 %copy-start.53 = (f32[128]{0:T(128)S(1)}, f32[128]{0:T(128)}, u32[]{:S(2)}) copy-start(f32[128]{0:T(128)} %get-tuple-element.53) | copy-start | bytes 1540
  174.2 124.9 %copy-start.52 = (f32[128]{0:T(128)S(1)}, f32[128]{0:T(128)}, u32[]{:S(2)}) copy-start(f32[128]{0:T(128)} %get-tuple-element.54) | copy-start | bytes 1540
  174.2 126.5 %copy-start.5 = (bf16[128,768]{1,0:T(8,128)(2,1)S(1)}, bf16[128,768]{1,0:T(8,128)(2,1)}, u32[]{:S(2)}) copy-start(bf16[128,768]{1,0:T(8,128)(2,1)} %param.20) | copy-start | bytes 589828
  174.2 126.5 %copy-start.8 = (f32[128,768]{1,0:T(8,128)S(1)}, f32[128,768]{1,0:T(8,128)}, u32[]{:S(2)}) copy-start(f32[128,768]{1,0:T(8,128)} %copy-done.7) | copy-start | bytes 1179652
  174.2 126.5 %copy-start.12 = (f32[128,768]{1,0:T(8,128)S(1)}, f32[128,768]{1,0:T(8,128)}, u32[]{:S(2)}) copy-start(f32[128,768]{1,0:T(8,128)} %get-tuple-element.94) | copy-start | bytes 1179652
  174.2 126.5 %copy-start.42 = (f32[128]{0:T(128)S(1)}, f32[128]{0:T(128)}, u32[]{:S(2)}) copy-start(f32[128]{0:T(128)} %copy-done.40) | copy-start | bytes 1540
  174.2 126.5 %copy-start.49 = (f32[128]{0:T(128)S(1)}, f32[128]{0:T(128)}, u32[]{:S(2)}) copy-start(f32[128]{0:T(128)} %copy-done.47) | copy-start | bytes 1540
  296.2 5.3 %copy-start.19 = (f32[24,2304]{1,0:T(8,128)S(1)}, f32[24,2304]{1,0:T(8,128)}, u32[]{:S(2)}) copy-start(f32[24,2304]{1,0:T(8,128)} %get-tuple-element.121) | copy-start | bytes 663556
  296.2 6.0 %copy-start.20 = (f32[24,768]{1,0:T(8,128)S(1)}, f32[24,768]{1,0:T(8,128)}, u32[]{:S(2)}) copy-start(f32[24,768]{1,0:T(8,128)} %get-tuple-element.124) | copy-start | bytes 221188
  296.2 6.6 %copy-start.18 = (f32[24,3072]{1,0:T(8,128)S(1)}, f32[24,3072]{1,0:T(8,128)}, u32[]{:S(2)}) copy-start(f32[24,3072]{1,0:T(8,128)} %get-tuple-element.129) | copy-start | bytes 884740
  296.2 7.4 %copy-start.17 = (f32[96,768]{1,0:T(8,128)S(1)}, f32[96,768]{1,0:T(8,128)}, u32[]{:S(2)}) copy-start(f32[96,768]{1,0:T(8,128)} %get-tuple-element.131) | copy-start | bytes 884740
  (11 other events, 21.4 us)
Sparse Core Ops, SparseCore 0:
  144.1 19.4 reduce-scatter.1

commit v3 on v1

--- a/solution.py
+++ b/solution.py
@@ -20,6 +20,8 @@
 TN = (((0,), (0,)), ((), ()))
 
 
+VMEM_LIMIT = 63 << 20
+ROW_GROUP = 8
 EPSILON = 1e-06
 NEG_FILL = -1e30
 
@@ -78,7 +80,7 @@
     return jnp.where(half_mask(values.shape, half), values, jnp.zeros_like(values))
 
 
-def attend(query_ref, kv_ref, diag_ref, probs_ref, mixed_ref, width, count, offset):
+def attend(query_ref, kv_ref, diag_ref, probs_ref, mixed_ref, width, count, offset, pairs=(0, PAIRS)):
     rows, model = query_ref.shape
     keys = kv_ref.shape[0]
     span = rows + keys
@@ -111,7 +113,7 @@
         mixed_ref[:, cols] = mixed.astype(BF16)
         return carry
 
-    lax.fori_loop(0, PAIRS, one_pair, 0)
+    lax.fori_loop(*pairs, one_pair, 0)
 
 
 def fold_rows(values):
@@ -122,12 +124,11 @@
 
 
 def attend_back(
-    query_ref, kv_ref, probs_ref, grad_ref, grad_query_ref, grad_kv_ref, fold_ref, width, offset
+    query_ref, kv_ref, probs_ref, grad_ref, grad_query_ref, grad_kv_ref, fold_ref, width, offset, pairs=(0, PAIRS)
 ):
     rows, model = query_ref.shape
     keys = kv_ref.shape[0]
     same = same_side(rows, keys, width, offset)
-    fold_ref[...] = jnp.zeros_like(fold_ref)
 
     def one_pair(pair, carry):
         cols = pl.ds(pl.multiple_of(pair * PAIR, PAIR), PAIR)
@@ -164,7 +165,7 @@
         grad_kv_ref[:, value_cols] = grad_value.astype(BF16)
         return carry
 
-    lax.fori_loop(0, PAIRS, one_pair, 0)
+    lax.fori_loop(*pairs, one_pair, 0)
 
 
 def table_gradient(fold_ref, out_ref, rows, keys, row_span, width, offset):
@@ -216,10 +217,747 @@
 ):
     rows, keys = query_ref.shape[0], kv_ref.shape[0]
     width, offset = scal_ref[0], scal_ref[2]
+    fold_ref[...] = jnp.zeros_like(fold_ref)
     attend_back(
         query_ref, kv_ref, probs_ref, grad_ref, grad_query_ref, grad_kv_ref, fold_ref, width, offset
     )
     table_gradient(fold_ref, table_ref, rows, keys, row_span, width, offset)
+
+
+MESH = pl.DeviceIdType.MESH
+Z_SIZE = 4
+
+
+class Place:
+    def __init__(self):
+        img = lax.axis_index("img")
+        self.x = lax.axis_index("seq")
+        self.c = lax.rem(img, 2)
+        self.y = lax.rem(img // 2, 2)
+        self.z = img // 4
+
+    def at(self, z=None, y=None, c=None, x=None):
+        z = self.z if z is None else z
+        y = self.y if y is None else y
+        c = self.c if c is None else c
+        x = self.x if x is None else x
+        return {"img": (z * 2 + y) * 2 + c, "seq": x}
+
+    def sibling(self):
+        return self.at(c=1 - self.c)
+
+    def over_x(self):
+        return self.at(x=1 - self.x)
+
+    def over_y(self):
+        return self.at(y=1 - self.y)
+
+    def z_of(self, step):
+        return lax.rem(self.z + step, Z_SIZE)
+
+    def partners(self):
+        return [self.sibling(), self.over_x(), self.over_y()] + [
+            self.at(z=self.z_of(step)) for step in range(1, Z_SIZE)
+        ]
+
+
+def meet(place):
+    barrier = pltpu.get_barrier_semaphore()
+    partners = place.partners()
+    for partner in partners:
+        pl.semaphore_signal(barrier, inc=1, device_id=partner, device_id_type=MESH)
+    pl.semaphore_wait(barrier, len(partners))
+
+
+class Sems:
+    def __init__(self, send, recv):
+        self.send, self.recv, self.used = send, recv, 0
+
+    def copy(self, src, dst, device):
+        index = self.used
+        self.used += 1
+        return pltpu.make_async_remote_copy(
+            src_ref=src,
+            dst_ref=dst,
+            send_sem=self.send.at[index],
+            recv_sem=self.recv.at[index],
+            device_id=device,
+            device_id_type=MESH,
+        )
+
+
+GATHER_COPIES = 10
+
+
+class Gather:
+    def __init__(self, place, src, slots, cols, x_last, sems, local_sem):
+        z, y, c, x = place.z, place.y, place.c, place.x
+        groups = src.shape[0]
+        every = slice(None)
+
+        def part(a, b, e):
+            return slots.at[a, b, c, pl.ds(e * groups, groups), :, cols]
+
+        own = part(z, y, x)
+        self.local = pltpu.make_async_copy(src.at[:, :, cols], own, local_sem)
+        self.along_z = [
+            sems.copy(src.at[:, :, cols], own, place.at(z=place.z_of(step)))
+            for step in range(1, Z_SIZE)
+        ]
+        line = part(every, y, x)
+        mid_line = part(every, 1 - y, x) if x_last else part(every, y, 1 - x)
+        far_line = part(every, y, 1 - x) if x_last else part(every, 1 - y, x)
+        cross_line = part(every, 1 - y, 1 - x)
+        mid, last = place.over_y(), place.over_x()
+        if not x_last:
+            mid, last = last, mid
+        sibling = place.sibling()
+        self.line_mid = sems.copy(line, line, mid)
+        self.line_last = sems.copy(line, line, last)
+        self.line_core = sems.copy(line, line, sibling)
+        self.mid_last = sems.copy(mid_line, mid_line, last)
+        self.mid_core = sems.copy(mid_line, mid_line, sibling)
+        self.far_core = sems.copy(far_line, far_line, sibling)
+        self.cross_core = sems.copy(cross_line, cross_line, sibling)
+
+    def begin(self):
+        self.local.start()
+        for copy in self.along_z:
+            copy.start()
+
+    def second(self):
+        self.local.wait()
+        for copy in self.along_z:
+            copy.wait_recv()
+        self.line_mid.start()
+        self.line_last.start()
+        self.line_core.start()
+
+    def third(self):
+        self.line_mid.wait_recv()
+        self.mid_last.start()
+        self.mid_core.start()
+
+    def fourth(self):
+        self.line_last.wait_recv()
+        self.far_core.start()
+        self.mid_last.wait_recv()
+        self.cross_core.start()
+
+    def arrive(self):
+        for copy in (self.line_core, self.mid_core, self.far_core, self.cross_core):
+            copy.wait_recv()
+
+    def settle(self):
+        for copy in self.along_z + [
+            self.line_mid,
+            self.line_last,
+            self.line_core,
+            self.mid_last,
+            self.mid_core,
+            self.far_core,
+            self.cross_core,
+        ]:
+            copy.wait_send()
+
+
+def halves(width):
+    middle = width // 2 // LANES * LANES
+    return [(0, middle), (middle, width - middle)]
+
+
+REDUCE_COPIES = 6
+
+
+class Reduce:
+    def __init__(self, place, grad, own, first, second, third, out, start, size, x_first, sems, pieces=None):
+        rows = out.shape[0]
+
+        def flat(ref):
+            return ref.reshape(ref.shape[:-3] + (rows, ref.shape[-1]))
+
+        self.place, self.out = place, out
+        self.grad, self.own, self.first = flat(grad), flat(own), flat(first)
+        self.second, self.third = flat(second), flat(third)
+        self.pieces = pieces or [(0, start, size)]
+        self.x_first = x_first
+        z, y, c, x = place.z, place.y, place.c, place.x
+        every = slice(None)
+        cols = pl.ds(start, size)
+        self.cols = cols
+        self.to_core = sems.copy(
+            grad.at[:, :, 1 - c, :, :, :, cols], own.at[:, :, :, :, :, cols], place.sibling()
+        )
+        over_first, over_second = place.over_x(), place.over_y()
+        if x_first:
+            leaving, other = own.at[:, :, 1 - x, :, :, cols], 1 - y
+        else:
+            over_first, over_second = over_second, over_first
+            leaving, other = own.at[:, 1 - y, :, :, :, cols], 1 - x
+        self.kept = y if x_first else x
+        self.over_first = sems.copy(leaving, first, over_first)
+        self.over_second = sems.copy(first.at[:, other], second, over_second)
+        self.along_z = []
+        for step in range(1, Z_SIZE):
+            target = place.z_of(step)
+            self.along_z.append(
+                sems.copy(second.at[target], third.at[step - 1], place.at(z=target))
+            )
+
+    def begin(self):
+        self.to_core.start()
+
+    def add_core(self):
+        self.to_core.wait_recv()
+        place = self.place
+
+        def add(zy, carry):
+            z, y = zy // 2, lax.rem(zy, 2)
+            for x in range(2):
+                mine = self.grad[z, y, place.c, x, :, self.cols].astype(F32)
+                theirs = self.own[z, y, x, :, self.cols].astype(F32)
+                self.own[z, y, x, :, self.cols] = (mine + theirs).astype(self.own.dtype)
+            return carry
+
+        lax.fori_loop(0, 2 * Z_SIZE, add, 0)
+        self.over_first.start()
+
+    def add_first(self):
+        self.over_first.wait_recv()
+        place = self.place
+
+        def add(z, carry):
+            for other in range(2):
+                if self.x_first:
+                    mine = self.own[z, other, place.x, :, self.cols].astype(F32)
+                else:
+                    mine = self.own[z, place.y, other, :, self.cols].astype(F32)
+                theirs = self.first[z, other].astype(F32)
+                self.first[z, other] = (mine + theirs).astype(self.first.dtype)
+            return carry
+
+        lax.fori_loop(0, Z_SIZE, add, 0)
+        self.over_second.start()
+
+    def add_second(self):
+        self.over_second.wait_recv()
+
+        def add(z, carry):
+            mine = self.first[z, self.kept].astype(F32)
+            theirs = self.second[z].astype(F32)
+            self.second[z] = (mine + theirs).astype(self.second.dtype)
+            return carry
+
+        lax.fori_loop(0, Z_SIZE, add, 0)
+        for copy in self.along_z:
+            copy.start()
+
+    def finish(self):
+        total = self.second[self.place.z].astype(F32)
+        for step, copy in enumerate(self.along_z):
+            copy.wait_recv()
+            total = total + self.third[step].astype(F32)
+        for source, target, size in self.pieces:
+            self.out[:, target : target + size] = total[:, source : source + size]
+
+    def settle(self):
+        for copy in [self.to_core, self.over_first, self.over_second] + self.along_z:
+            copy.wait_send()
+
+
+class Names:
+    pass
+
+
+def norm_rows(values):
+    centred = values - jnp.mean(values, axis=1, keepdims=True)
+    inv_std = lax.rsqrt(jnp.mean(centred * centred, axis=1, keepdims=True) + EPSILON)
+    return centred * inv_std, inv_std
+
+
+def norm_rows_back(grad_out, normed, inv_std, gain):
+    scaled = grad_out * gain
+    return inv_std * (
+        scaled
+        - jnp.mean(scaled, axis=1, keepdims=True)
+        - normed * jnp.mean(scaled * normed, axis=1, keepdims=True)
+    )
+
+
+def sum_rows(values):
+    return jnp.sum(values.astype(F32), axis=0, keepdims=True)
+
+
+def div_const(values, divisor):
+    return jnp.floor((values.astype(F32) + 0.5) * (1.0 / divisor)).astype(jnp.int32)
+
+
+def tile(slots, start, size):
+    rows = slots.shape[3] * ROW_GROUP
+    view = slots.reshape(4 * Z_SIZE, rows, slots.shape[-1])
+    return view[:, :, pl.ds(start, size)].reshape(-1, size)
+
+
+def put_slots(slots, cols, values):
+    devices = 8 * Z_SIZE
+    view = slots.reshape(devices, slots.shape[4] * ROW_GROUP, slots.shape[-1])
+    view[:, :, cols] = values.reshape(devices, -1, values.shape[1]).astype(slots.dtype)
+
+
+def tiles(count, step):
+    def wrap(body):
+        def run(number, carry):
+            body(number, pl.multiple_of(number * step, step))
+            return carry
+
+        lax.fori_loop(0, count, run, 0)
+
+    return wrap
+
+
+LINES = 16
+SLOT_ROWS = 24
+(
+    GAIN_ONE, SHIFT_ONE, QUERY_BIAS, VALUE_BIAS, PROJ_SHIFT, SCALE_ONE, GAIN_TWO, SHIFT_TWO, FC2_SHIFT, SCALE_TWO,
+) = range(10)
+HIDDEN_LINE = 10
+
+
+def unpack_lines(packed, shard, hidden_shard, vec_ref, hidden_ref):
+    rows = packed.shape[0]
+    devices = rows // SLOT_ROWS
+    low = packed.astype(BF16)
+    width = shard * devices
+    lane = iota((LANES, width), 1)
+    spread = jnp.where(lane - div_const(lane, shard) * shard == iota((LANES, width), 0), 1.0, 0.0)
+    wide = dot(low, spread.astype(BF16))
+    owner = div_const(iota((rows, width), 0), SLOT_ROWS)
+    wide = jnp.where(owner == div_const(iota((rows, width), 1), shard), wide, 0.0).astype(BF16)
+    row = iota((LINES, rows), 1)
+    line = row - div_const(row, SLOT_ROWS) * SLOT_ROWS
+    vec_ref[...] = dot(jnp.where(line == iota((LINES, rows), 0), 1.0, 0.0).astype(BF16), wide)
+    row = iota((devices, rows), 1)
+    chosen = jnp.where(row == iota((devices, rows), 0) * SLOT_ROWS + HIDDEN_LINE, 1.0, 0.0)
+    hidden = dot(chosen.astype(BF16), low).astype(BF16)
+    step = 8 * LANES
+    for start in range(0, hidden_shard * devices, step):
+        lane = iota((LANES, step), 1) + start
+        owner = div_const(lane, hidden_shard)
+        spread = jnp.where(lane - owner * hidden_shard == iota((LANES, step), 0), 1.0, 0.0)
+        wide = dot(hidden, spread.astype(BF16))
+        owner = div_const(iota((devices, step), 1) + start, hidden_shard)
+        wide = jnp.where(owner == iota((devices, step), 0), wide, 0.0)
+        hidden_ref[:, start : start + step] = jnp.broadcast_to(sum_rows(wide), (8, step))
+
+
+def layer_kernel(names, row_span, *refs):
+    s = Names()
+    s.__dict__.update(zip(names, refs))
+    buffers = list(refs[len(names) :])
+    send, recv, local = buffers[-3:]
+    place = Place()
+    x = place.x
+    width, count, offset = s.scal[0], s.scal[1], s.scal[2]
+    rows, model = s.tokens.shape
+    keys = 2 * rows
+    hidden = s.w_fc1.shape[2]
+    shard, hidden_shard = s.w_qkv.shape[0] * ROW_GROUP, s.w_fc2.shape[0] * ROW_GROUP
+    half = model // 2
+    own_rows = pl.ds(pl.multiple_of(x * rows, rows), rows)
+    far_rows = pl.ds(pl.multiple_of((1 - x) * rows, rows), rows)
+    sems = Sems(send, recv)
+    locals_used = []
+
+    def gather(src, slots, cuts):
+        chunks = []
+        for number, (start, size) in enumerate(cuts):
+            sem = local.at[len(locals_used)]
+            locals_used.append(0)
+            chunks.append(Gather(place, src, slots, pl.ds(start, size), number == 0, sems, sem))
+        return chunks
+
+    def reduce(out, cuts, pieces):
+        chunks = []
+        grad, own = buffers.pop(0), buffers.pop(0)
+        for number, (start, size) in enumerate(cuts):
+            stages = [buffers.pop(0) for _ in range(3)]
+            chunks.append(
+                Reduce(
+                    place, grad, own, *stages, out, start, size, number == 0, sems, pieces and pieces[number],
+                )
+            )
+        return grad, chunks
+
+    def each(chunks, *steps):
+        for step in steps:
+            for chunk in chunks:
+                step(chunk)
+
+    swap = sems.copy(s.tokens, s.far_tokens, place.over_x())
+    give = sems.copy(s.give, s.take, place.over_x())
+    get_pack = gather(s.pack, s.packs, [(0, LANES)])
+    get_qkv = gather(s.w_qkv, s.wq, halves(3 * model))
+    get_proj = gather(s.w_proj, s.wp, halves(model))
+    get_fc1 = gather(s.w_fc1, s.w1, halves(hidden))
+    get_fc2 = gather(s.w_fc2, s.w2, halves(model))
+    third = 3 * half
+    qkv_pieces = [
+        [(part * half, part * model + group * half, half) for part in range(3)] for group in range(2)
+    ]
+    s.g_fc2, put_fc2 = reduce(s.o_fc2, halves(model), None)
+    s.g_fc1, put_fc1 = reduce(s.o_fc1, halves(hidden), None)
+    s.g_proj, put_proj = reduce(s.o_proj, halves(model), None)
+    s.g_qkv, put_qkv = reduce(s.o_qkv, [(0, third), (third, third)], qkv_pieces)
+    s.g_table, put_table = reduce(s.o_table, [(0, LANES)], None)
+    s.g_small, put_small = reduce(s.o_small, [(0, LANES)], None)
+    get_table = gather(s.o_table.reshape(1, 8, LANES), s.table_all, [(0, LANES)])
+
+    meet(place)
+    swap.start()
+    for chunks in (get_pack, get_qkv, get_proj, get_fc1, get_fc2):
+        each(chunks, Gather.begin)
+
+    fill_diagonals(s.table_lines, s.diag, rows, keys, row_span, width, offset)
+    inputs = s.tokens[...].astype(F32)
+    normed, inv_std = norm_rows(inputs)
+    s.n1[...] = normed
+    s.r1[...] = jnp.broadcast_to(inv_std, s.r1.shape)
+    s.fold[...] = jnp.zeros_like(s.fold)
+    s.lines[...] = jnp.zeros_like(s.lines)
+
+    each(get_pack, Gather.second, Gather.third)
+    each(get_qkv, Gather.second)
+    each(get_pack, Gather.fourth, Gather.arrive)
+    unpack_lines(tile(s.packs, 0, LANES), shard, hidden_shard, s.vec, s.b1)
+
+    def line(number):
+        return s.vec[number : number + 1, :]
+
+    def set_line(number, values):
+        s.lines[number : number + 1, :] = values
+
+    s.h1[own_rows, :] = (s.n1[...] * line(GAIN_ONE) + line(SHIFT_ONE)).astype(BF16)
+    swap.wait_recv()
+    far = norm_rows(s.far_tokens[...].astype(F32))[0]
+    s.h1[far_rows, :] = (far * line(GAIN_ONE) + line(SHIFT_ONE)).astype(BF16)
+    each(get_proj, Gather.second)
+    s.h1t[...] = s.h1[...].T
+    s.dm[...] = (line(SCALE_TWO) * s.cot[...].astype(F32)).astype(BF16)
+    set_line(FC2_SHIFT, sum_rows(s.dm[...]))
+    each(get_qkv, Gather.third)
+    each(get_fc1, Gather.second)
+    each(get_qkv, Gather.fourth)
+    each(get_proj, Gather.third)
+    each(get_qkv, Gather.arrive)
+
+    step = 2 * LANES
+
+    @tiles(model // step, step)
+    def _(number, start):
+        s.kv[:, pl.ds(start, step)] = dot(s.h1[...], tile(s.wq, model + start, step)).astype(BF16)
+        sums = dot(s.h1[...], tile(s.wq, 2 * model + start, step))
+        sums = sums + s.vec[VALUE_BIAS : VALUE_BIAS + 1, pl.ds(start, step)]
+        s.kv[:, pl.ds(model + start, step)] = sums.astype(BF16)
+
+    @tiles(model // step, step)
+    def _(number, start):
+        cols = pl.ds(start, step)
+        sums = dot(s.h1[own_rows, :], tile(s.wq, start, step))
+        s.q[:, cols] = (sums + s.vec[QUERY_BIAS : QUERY_BIAS + 1, cols]).astype(BF16)
+
+    each(get_fc1, Gather.third)
+    attend(s.q, s.kv, s.diag, s.probs, s.mixed, width, count, offset, (0, PAIRS // 2))
+    each(get_fc2, Gather.second)
+    each(get_proj, Gather.fourth)
+    attend(s.q, s.kv, s.diag, s.probs, s.mixed, width, count, offset, (PAIRS // 2, PAIRS))
+    s.mixedt[...] = s.mixed[...].T
+    each(get_fc1, Gather.fourth)
+    each(get_proj, Gather.arrive)
+
+    @tiles(model // step, step)
+    def _(number, start):
+        cols = pl.ds(start, step)
+        branch = dot(s.mixed[...], tile(s.wp, start, step)) + s.vec[PROJ_SHIFT : PROJ_SHIFT + 1, cols]
+        s.z[:, cols] = branch
+        s.x1[:, cols] = s.tokens[:, cols].astype(F32) + s.vec[SCALE_ONE : SCALE_ONE + 1, cols] * branch
+
+    normed, inv_std = norm_rows(s.x1[...])
+    s.n2[...] = normed
+    s.r2[...] = jnp.broadcast_to(inv_std, s.r2.shape)
+    s.h2[...] = (normed * line(GAIN_TWO) + line(SHIFT_TWO)).astype(BF16)
+    s.h2t[...] = s.h2[...].T
+    each(get_fc2, Gather.third)
+    each(get_fc1, Gather.arrive)
+
+    @tiles(hidden // step, step)
+    def _(number, start):
+        cols = pl.ds(start, step)
+        act = dot(s.h2[...], tile(s.w1, start, step)) + s.b1[0:1, cols]
+        gate = 0.5 * (1.0 + lax.erf(act * 0.5**0.5))
+        low = (act * gate).astype(BF16)
+        s.u[:, cols] = low
+        s.ut[cols, :] = low.T
+        s.slope[:, cols] = gate + act * jnp.exp(act * act * -0.5) * 0.3989422804014327
+
+    each(get_fc2, Gather.fourth)
+    deep = 8 * hidden_shard
+    for group in range(2):
+
+        @tiles(Z_SIZE, deep)
+        def _(number, start):
+            cols = pl.ds(group * half, half)
+            sums = dot(s.ut[pl.ds(start, deep), :], s.dm[:, cols])
+            view = s.g_fc2.reshape(Z_SIZE, 8, hidden_shard, model)
+            view[number, :, :, cols] = sums.reshape(8, hidden_shard, half).astype(BF16)
+
+        put_fc2[group].begin()
+    each(get_fc2, Gather.arrive)
+
+    @tiles(Z_SIZE, deep)
+    def _(number, start):
+        cols = pl.ds(start, deep)
+        weight = s.w2.reshape(Z_SIZE, deep, model)[number]
+        grad_hidden = dot(s.dm[...], weight, NT)
+        s.da[:, cols] = (grad_hidden * s.slope[:, cols]).astype(BF16)
+
+    each(put_fc2, Reduce.add_core)
+    for group in range(2):
+
+        @tiles(hidden // 2 // step, step)
+        def _(number, start):
+            cols = pl.ds(start + group * (hidden // 2), step)
+            sums = dot(s.h2t[...], s.da[:, cols])
+            put_slots(s.g_fc1, cols, sums)
+
+        put_fc1[group].begin()
+
+    @tiles(model // step, step)
+    def _(number, start):
+        cols = pl.ds(start, step)
+        branch = dot(s.u[...], tile(s.w2, start, step)) + s.vec[FC2_SHIFT : FC2_SHIFT + 1, cols]
+        s.out[:, cols] = (s.x1[:, cols] + s.vec[SCALE_TWO : SCALE_TWO + 1, cols] * branch).astype(BF16)
+        s.lines[SCALE_TWO : SCALE_TWO + 1, cols] = sum_rows(s.cot[:, cols].astype(F32) * branch)
+
+    s.hidden_lines[...] = jnp.broadcast_to(sum_rows(s.da[...]), s.hidden_lines.shape)
+    grad = jnp.zeros((rows, model), F32)
+    for start in range(0, hidden, model):
+        grad = grad + dot(s.da[:, start : start + model], tile(s.w1, start, model), NT)
+    set_line(GAIN_TWO, sum_rows(grad * s.n2[...]))
+    set_line(SHIFT_TWO, sum_rows(grad))
+    dx1 = s.cot[...].astype(F32) + norm_rows_back(grad, s.n2[...], s.r2[:, 0:1], line(GAIN_TWO))
+    s.dx1[...] = dx1
+    set_line(SCALE_ONE, sum_rows(dx1 * s.z[...]))
+    s.dz[...] = (line(SCALE_ONE) * dx1).astype(BF16)
+    set_line(PROJ_SHIFT, sum_rows(s.dz[...]))
+    for group in range(2):
+        cols = pl.ds(group * half, half)
+        sums = dot(s.mixedt[...], s.dz[:, cols])
+        put_slots(s.g_proj, cols, sums)
+        put_proj[group].begin()
+    s.dmixed[...] = dot(s.dz[...], tile(s.wp, 0, model), NT).astype(BF16)
+    each(put_fc1, Reduce.add_core)
+    each(put_fc2, Reduce.add_first)
+
+    def qkv_grad(group):
+        cols = pl.ds(group * half, half)
+        value_cols = pl.ds(model + group * half, half)
+        own_lines = s.h1t[:, own_rows]
+        all_lines = s.h1t[...]
+        for part, sums in enumerate(
+            (
+                dot(own_lines, s.dq[:, cols]),
+                dot(all_lines, s.dkv[:, cols]),
+                dot(all_lines, s.dkv[:, value_cols]),
+            )
+        ):
+            target = pl.ds(group * third + part * half, half)
+            put_slots(s.g_qkv, target, sums)
+        put_qkv[group].begin()
+
+    attend_back(
+        s.q, s.kv, s.probs, s.dmixed, s.dq, s.dkv, s.fold, width, offset, (0, PAIRS // 2)
+    )
+    qkv_grad(0)
+    each(put_proj, Reduce.add_core)
+    each(put_fc1, Reduce.add_first)
+    each(put_fc2, Reduce.add_second)
+    attend_back(
+        s.q, s.kv, s.probs, s.dmixed, s.dq, s.dkv, s.fold, width, offset, (PAIRS // 2, PAIRS)
+    )
+    qkv_grad(1)
+    grad_key = dot(s.dkv[:, :model], tile(s.wq, model, model), NT)
+    s.dh1[...] = grad_key + dot(s.dkv[:, model:], tile(s.wq, 2 * model, model), NT)
+    s.give[...] = s.dh1[far_rows, :].astype(BF16)
+    give.start()
+    table_gradient(s.fold, s.table_sums, rows, keys, row_span, width, offset)
+
+    @tiles(4 * Z_SIZE, LANES)
+    def _(number, start):
+        zz, yy, cc = number // 4, lax.rem(number // 2, 2), lax.rem(number, 2)
+        for xx in range(2):
+            s.g_table[zz, yy, cc, xx, 0] = s.table_sums[8 * xx : 8 * xx + 8, pl.ds(start, LANES)]
+
+    each(put_table, Reduce.begin)
+    each(put_qkv, Reduce.add_core)
+    each(put_proj, Reduce.add_first)
+    each(put_table, Reduce.add_core)
+    each(put_fc1, Reduce.add_second)
+    each(put_fc2, Reduce.finish)
+    set_line(QUERY_BIAS, sum_rows(s.dq[...]))
+    set_line(VALUE_BIAS, sum_rows(s.dkv[:, model:]))
+    grad = s.dh1[own_rows, :] + dot(s.dq[...], tile(s.wq, 0, model), NT)
+    give.wait_recv()
+    grad = grad + s.take[...].astype(F32)
+    set_line(GAIN_ONE, sum_rows(grad * s.n1[...]))
+    set_line(SHIFT_ONE, sum_rows(grad))
+    dx = s.dx1[...] + norm_rows_back(grad, s.n1[...], s.r1[:, 0:1], line(GAIN_ONE))
+    s.grad_tokens[...] = dx.astype(BF16)
+
+    @tiles(8 * Z_SIZE, 1)
+    def _(number, start):
+        zz, yy, cc, xx = number // 8, lax.rem(number // 4, 2), lax.rem(number // 2, 2), lax.rem(number, 2)
+        moved = pltpu.roll(s.lines[...], model - number * shard, 1)
+        for group in range(LINES // ROW_GROUP):
+            s.g_small[zz, yy, cc, xx, group] = moved[group * ROW_GROUP : (group + 1) * ROW_GROUP, :LANES]
+        moved = pltpu.roll(s.hidden_lines[...], hidden - number * hidden_shard, 1)
+        s.g_small[zz, yy, cc, xx, LINES // ROW_GROUP] = moved[:, :LANES]
+
+    each(put_small, Reduce.begin)
+    each(put_table, Reduce.add_first)
+    each(put_small, Reduce.add_core)
+    each(put_qkv, Reduce.add_first)
+    each(put_proj, Reduce.add_second)
+    each(put_table, Reduce.add_second)
+    each(put_small, Reduce.add_first)
+    each(put_fc1, Reduce.finish)
+    each(put_table, Reduce.finish)
+    each(get_table, Gather.begin)
+    each(put_small, Reduce.add_second)
+    each(put_qkv, Reduce.add_second)
+    each(get_table, Gather.second, Gather.third)
+    each(put_proj, Reduce.finish)
+    each(put_small, Reduce.finish)
+    each(get_table, Gather.fourth, Gather.arrive)
+    each(put_qkv, Reduce.finish)
+    swap.wait_send()
+    give.wait_send()
+    for chunks in (get_pack, get_qkv, get_proj, get_fc1, get_fc2, get_table):
+        each(chunks, Gather.settle)
+    for chunks in (put_fc2, put_fc1, put_proj, put_qkv, put_table, put_small):
+        each(chunks, Reduce.settle)
+
+
+def grouped(array):
+    return array.reshape(-1, ROW_GROUP, array.shape[-1])
+
+
+def run_layer(row_span, scalars, tokens, cotangent, packed, w_qkv, w_proj, w_fc1, w_fc2, table_lines):
+    rows, model = tokens.shape
+    keys = 2 * rows
+    shard, hidden, hidden_shard = w_qkv.shape[0], w_fc1.shape[1], w_fc2.shape[0]
+    smem = pl.BlockSpec(memory_space=pltpu.SMEM)
+    vmem = pl.BlockSpec(memory_space=pltpu.VMEM)
+    anywhere = pl.BlockSpec(memory_space=pl.ANY)
+    inputs = dict(
+        scal=(scalars, smem),
+        tokens=(tokens, vmem),
+        cot=(cotangent, vmem),
+        pack=(grouped(packed), vmem),
+        w_qkv=(grouped(w_qkv), anywhere),
+        w_proj=(grouped(w_proj), anywhere),
+        w_fc1=(grouped(w_fc1), anywhere),
+        w_fc2=(grouped(w_fc2), anywhere),
+        table_lines=(table_lines, vmem),
+    )
+    outputs = dict(
+        out=((rows, model), BF16),
+        grad_tokens=((rows, model), BF16),
+        o_small=((SLOT_ROWS, LANES), F32),
+        o_qkv=((shard, 3 * model), F32),
+        o_proj=((shard, model), F32),
+        o_fc1=((shard, hidden), F32),
+        o_fc2=((hidden_shard, model), F32),
+        table_all=((Z_SIZE, 2, 2, 2, 8, LANES), F32),
+    )
+    scratch = dict(
+        o_table=((8, LANES), F32),
+        far_tokens=((rows, model), BF16),
+        give=((rows, model), BF16),
+        take=((rows, model), BF16),
+        packs=((Z_SIZE, 2, 2, 2 * SLOT_ROWS // ROW_GROUP, ROW_GROUP, LANES), F32),
+        wq=((Z_SIZE, 2, 2, 2 * shard // ROW_GROUP, ROW_GROUP, 3 * model), BF16),
+        wp=((Z_SIZE, 2, 2, 2 * shard // ROW_GROUP, ROW_GROUP, model), BF16),
+        w1=((Z_SIZE, 2, 2, 2 * shard // ROW_GROUP, ROW_GROUP, hidden), BF16),
+        w2=((Z_SIZE, 2, 2, 2 * hidden_shard // ROW_GROUP, ROW_GROUP, model), BF16),
+        vec=((LINES, model), F32),
+        b1=((8, hidden), F32),
+        diag=((HEAD_ROWS, 2 * (rows + keys)), F32),
+        h1=((keys, model), BF16),
+        h1t=((model, keys), BF16),
+        n1=((rows, model), F32),
+        r1=((rows, LANES), F32),
+        q=((rows, model), BF16),
+        kv=((keys, 2 * model), BF16),
+        probs=((HEADS, rows, keys), F32),
+        mixed=((rows, model), BF16),
+        mixedt=((model, rows), BF16),
+        z=((rows, model), F32),
+        x1=((rows, model), F32),
+        n2=((rows, model), F32),
+        r2=((rows, LANES), F32),
+        h2=((rows, model), BF16),
+        h2t=((model, rows), BF16),
+        u=((rows, hidden), BF16),
+        ut=((hidden, rows), BF16),
+        slope=((rows, hidden), F32),
+        dm=((rows, model), BF16),
+        da=((rows, hidden), BF16),
+        dx1=((rows, model), F32),
+        dz=((rows, model), BF16),
+        dmixed=((rows, model), BF16),
+        dq=((rows, model), BF16),
+        dkv=((keys, 2 * model), BF16),
+        dh1=((keys, model), F32),
+        fold=(((rows + keys) // LANES, 2 * HEAD_ROWS * 8, LANES), F32),
+        table_sums=((HEAD_ROWS, table_lines.shape[1]), F32),
+        lines=((LINES, model), F32),
+        hidden_lines=((8, hidden), F32),
+    )
+    stages = []
+    chunks = 0
+    for slot_rows, slot_width, dtype, cuts in (
+        (hidden_shard, model, BF16, None),
+        (shard, hidden, BF16, None),
+        (shard, model, BF16, None),
+        (shard, 3 * model, BF16, [(0, 3 * model // 2)] * 2),
+        (8, LANES, F32, None),
+        (SLOT_ROWS, LANES, F32, None),
+    ):
+        cuts = cuts or ([(0, slot_width)] if slot_width <= LANES else halves(slot_width))
+        groups = slot_rows // ROW_GROUP
+        stages.append(((Z_SIZE, 2, 2, 2, groups, ROW_GROUP, slot_width), dtype))
+        stages.append(((Z_SIZE, 2, 2, groups, ROW_GROUP, slot_width), dtype))
+        for _, size in cuts:
+            for lead in ((Z_SIZE, 2), (Z_SIZE,), (Z_SIZE - 1,)):
+                stages.append((lead + (groups, ROW_GROUP, size), dtype))
+            chunks += 1
+    copies = 2 + GATHER_COPIES * 10 + REDUCE_COPIES * chunks
+    names = list(inputs) + list(outputs) + list(scratch)
+    return pl.pallas_call(
+        partial(layer_kernel, names, row_span),
+        out_shape=tuple(jax.ShapeDtypeStruct(shape, dtype) for shape, dtype in outputs.values()),
+        in_specs=[spec for _, spec in inputs.values()],
+        out_specs=(vmem,) * len(outputs),
+        scratch_shapes=[pltpu.VMEM(shape, dtype) for shape, dtype in list(scratch.values()) + stages]
+        + [
+            pltpu.SemaphoreType.DMA((copies,)),
+            pltpu.SemaphoreType.DMA((copies,)),
+            pltpu.SemaphoreType.DMA((10,)),
+        ],
+        compiler_params=pltpu.CompilerParams(
+            collective_id=0, has_side_effects=True, vmem_limit_bytes=VMEM_LIMIT
+        ),
+    )(*[array for array, _ in inputs.values()])
 
 
 def layer_norm(values, gain, shift):
@@ -242,7 +980,7 @@
     return jnp.sum(values.astype(jnp.float32), axis=0)
 
 
-def per_device(
+def per_device_native(
     tokens,
     cotangent,
     counts,
@@ -435,6 +1173,69 @@
     return (output, grad_inputs) + tuple(summed) + (table_total,)
 
 
+def per_device_linked(
+    tokens,
+    cotangent,
+    counts,
+    widths,
+    norm1_gain,
+    norm1_shift,
+    w_qkv,
+    q_bias,
+    v_bias,
+    w_proj,
+    proj_bias,
+    gamma1,
+    norm2_gain,
+    norm2_shift,
+    w_fc1,
+    fc1_bias,
+    w_fc2,
+    fc2_bias,
+    gamma2,
+    bias_table,
+):
+    local_rows = tokens.shape[0]
+    seq_len = local_rows * lax.axis_size("seq")
+    offset = lax.axis_index("seq") * local_rows
+    row_span = (seq_len - 1) // (SIDE // 2) + 1
+    table_rows = bias_table.shape[0]
+    entries = -(-table_rows // (2 * LANES)) * 2 * LANES
+    table_lines = jnp.pad(bias_table.T, ((0, HEAD_ROWS - HEADS), (0, entries - table_rows)))
+    scalars = jnp.stack([widths[0], counts[0], offset.astype(jnp.int32)])
+    shard = norm1_gain.shape[0]
+    hidden_shard = fc1_bias.shape[0]
+    vectors = [
+        norm1_gain, norm1_shift, q_bias, v_bias, proj_bias, gamma1, norm2_gain, norm2_shift, fc2_bias, gamma2,
+    ]
+    packed = jnp.concatenate(
+        [
+            jnp.pad(jnp.stack(vectors), ((0, 0), (0, LANES - shard))),
+            jnp.pad(fc1_bias.reshape(1, -1), ((0, SLOT_ROWS - len(vectors) - 1), (0, LANES - hidden_shard))),
+        ]
+    ).astype(F32)
+    output, grad_tokens, small, sum_qkv, sum_proj, sum_fc1, sum_fc2, table_all = run_layer(
+        row_span, scalars, tokens, cotangent, packed, w_qkv, w_proj, w_fc1, w_fc2, table_lines
+    )
+    sums = [small[number, :shard] for number in range(len(vectors))]
+    table_total = (
+        table_all.reshape(entries // LANES, 2, 8, LANES).transpose(1, 2, 0, 3).reshape(HEAD_ROWS, -1)
+    )[:HEADS, :table_rows].T
+    return (
+        output, grad_tokens, sums[GAIN_ONE], sums[SHIFT_ONE], sum_qkv, sums[QUERY_BIAS], sums[VALUE_BIAS],
+        sum_proj, sums[PROJ_SHIFT], sums[SCALE_ONE], sums[GAIN_TWO], sums[SHIFT_TWO], sum_fc1,
+        small[LINES, :hidden_shard], sum_fc2, sums[FC2_SHIFT], sums[SCALE_TWO], table_total,
+    )
+
+
+def per_device(*arrays):
+    tokens, bias_table = arrays[0], arrays[19]
+    linked = lax.axis_size("img") == 4 * Z_SIZE and lax.axis_size("seq") == 2
+    linked = linked and arrays[6].shape[0] % 8 == 0 and tokens.shape[0] == LANES
+    linked = linked and 15 * LANES < bias_table.shape[0] <= 4 * Z_SIZE * LANES
+    return per_device_linked(*arrays) if linked else per_device_native(*arrays)
+
+
 def solution(mesh):
     return jax.shard_map(
         per_device,

time: 947 us -> 183 us (0.19)
  waiting for transfers between devices: 745 us -> 0 us
  Pallas kernels: 14.2 us -> 167 us
  blocking collectives: 95.6 us -> 0 us
  matrix products: 45.2 us -> 0 us
  between operations: 15.9 us -> 2.02 us
  local copies, waits for them, and re-layouts: 22.2 us -> 11.8 us
    reduce_scatter x5 -> x0, waiting for transfers between devices: 472 us -> none  [the longest x1 142 us: per_device(): lax.psum_scatter(grad_fc1_weight, ('img', 'seq'), scatter_dimension=0, ti...]
    all_gather x4 -> x0, waiting for transfers between devices: 158 us -> none  [the longest x1 62.1 us: per_device(): lax.all_gather(w_fc1, ('img', 'seq'), axis=0, tiled=True)]
    pallas_call x2 -> x1, Pallas kernels: 14.2 us -> 167 us  [run_layer(): pl.pallas_call(partial(layer_kernel, names, row_span), out_shape=tuple((j...]
    psum x1 -> x0, waiting for transfers between devices: 112 us -> none  [per_device(): table_total = lax.psum(table_grad, ('img', 'seq'))[:HEADS, :table_rows].T]
    unnamed x2 -> x0, blocking collectives: 83.1 us -> none
    dot_general x12 -> x0, matrix products: 45.2 us -> none  [the longest x1 8.58 us: per_device(): jnp.dot(normed_low_two, fc1_weight, preferred_element_type=jnp.float32)]
    unnamed x111 -> x20, local copies, waits for them, and re-layouts: 18.7 us -> 5.33 us
    all_gather x1 -> x0, blocking collectives: 12.5 us -> none  [per_device(): keys_all = lax.all_gather(key_local, 'seq', axis=0, tiled=True)]
  transfers between devices with their start and end apart: 10 -> 0, of which waited for: 10 -> 0; matrix products, arithmetic and copies ran while one was open for 6% -> 0% of each run, Pallas kernels for 1% -> 0%
where the time goes in v3:
time: 183 us
  Pallas kernels  167 us (91%)
  local copies, waits for them, and re-layouts  11.8 us (6%)
  between operations  2.02 us (1%)
  other arithmetic  1.85 us (1%)
    pallas_call x1, Pallas kernels, run_layer(): pl.pallas_call(partial(layer_kernel, names, row_span), out_shape=tuple((j...  167 us
    unnamed x20, local copies, waits for them, and re-layouts  5.33 us

profile of v3, /device:TPU:0, one launch (start us, length us, event | category | flops | bytes accessed | tf_op | source)
XLA Modules:
  0.0 183.1 jit_solution(15595121068623409487)
XLA Ops:
  0.7 0.0 copy-start.6
  2.0 0.6 pad_add_fusion.refs_0_
  2.6 1.5 stack.51
  4.1 1.3 fusion.4.refs_3_
  5.3 0.0 copy-done.6
  5.3 0.6 pad.14.refs_8_
  6.0 167.4 %shard_map.331 = (bf16[128,768]{1,0:T(8,128)(2,1)}, bf16[128,768]{1,0:T(8,128)(2,1)}, f32[24,128]{1,0:T(8,128)}, f32[24,2304]{1,0:T(8,128)}, f32[24,768]{1,0:T(8...) custom-call(s32[3]{0:T(128)} %pad_add_fusion.refs_0_, bf16[128,768]{1,0:T(8,128)(2,1)} %refs_1_.1, ...), custom_call_target="tpu_custom_call" | custom-call | tf_op jit(solution)/shard_map/pallas_call | solution.py:946
  173.4 1.2 slice_bitcast_fusion.3
  174.6 1.5 slice_bitcast_fusion.1
  176.1 0.0 copy-start.4
  176.1 1.0 copy_bitcast_fusion
  177.1 0.7 slice_bitcast_fusion
  177.7 0.0 copy-done.4
  177.7 0.0 copy-start.3
  177.7 0.7 copy.48
  178.4 0.3 copy-done.3
  178.7 0.0 copy-start.2
  178.7 0.7 copy.49
  179.4 0.3 copy-done.2
  179.7 0.0 copy-start.5
  179.7 0.0 copy-start.1
  179.7 0.7 copy.50
  180.4 0.2 copy-done.5
  180.6 0.6 copy.51
  181.3 0.0 copy-done.1
  181.3 0.0 copy-start
  181.3 0.7 copy.52
  182.0 0.4 copy-done
  182.3 0.7 copy.53
Async XLA Ops:
  0.7 4.7 %copy-start.6 = (bf16[1953,12]{0,1:T(8,128)(2,1)S(1)}, bf16[1953,12]{0,1:T(8,128)(2,1)}, u32[]{:S(2)}) copy-start(bf16[1953,12]{0,1:T(8,128)(2,1)} %param.39) | copy-start | bytes 140620
  176.1 1.6 copy-start.4
  177.7 1.0 copy-start.3
  178.7 1.0 copy-start.2
  179.7 0.9 copy-start.5
  179.7 1.5 copy-start.1
  181.3 1.1 copy-start

commit v4 on v3

--- a/solution.py
+++ b/solution.py
@@ -286,7 +286,7 @@
         )
 
 
-GATHER_COPIES = 10
+GATHER_COPIES = 16
 
 
 class Gather:
@@ -298,12 +298,11 @@
         def part(a, b, e):
             return slots.at[a, b, c, pl.ds(e * groups, groups), :, cols]
 
+        mine = src.at[:, :, cols]
         own = part(z, y, x)
-        self.local = pltpu.make_async_copy(src.at[:, :, cols], own, local_sem)
-        self.along_z = [
-            sems.copy(src.at[:, :, cols], own, place.at(z=place.z_of(step)))
-            for step in range(1, Z_SIZE)
-        ]
+        self.local = pltpu.make_async_copy(mine, own, local_sem)
+        steps = range(1, Z_SIZE)
+        self.along_z = [sems.copy(mine, own, place.at(z=place.z_of(step))) for step in steps]
         line = part(every, y, x)
         mid_line = part(every, 1 - y, x) if x_last else part(every, y, 1 - x)
         far_line = part(every, y, 1 - x) if x_last else part(every, 1 - y, x)
@@ -312,34 +311,43 @@
         if not x_last:
             mid, last = last, mid
         sibling = place.sibling()
-        self.line_mid = sems.copy(line, line, mid)
-        self.line_last = sems.copy(line, line, last)
+        self.own_mid = sems.copy(mine, own, mid)
+        self.own_last = sems.copy(mine, own, last)
+        came = [part(place.z_of(Z_SIZE - step), y, x) for step in steps]
+        self.line_mid = [sems.copy(piece, piece, mid) for piece in came]
+        self.line_last = [sems.copy(piece, piece, last) for piece in came]
         self.line_core = sems.copy(line, line, sibling)
         self.mid_last = sems.copy(mid_line, mid_line, last)
         self.mid_core = sems.copy(mid_line, mid_line, sibling)
         self.far_core = sems.copy(far_line, far_line, sibling)
         self.cross_core = sems.copy(cross_line, cross_line, sibling)
 
-    def begin(self):
+    def begin_own(self):
         self.local.start()
+        self.own_mid.start()
+        self.own_last.start()
+
+    def begin_z(self):
         for copy in self.along_z:
             copy.start()
 
     def second(self):
+        for copy, onward, beyond in zip(self.along_z, self.line_mid, self.line_last):
+            copy.wait_recv()
+            onward.start()
+            beyond.start()
         self.local.wait()
-        for copy in self.along_z:
+        self.line_core.start()
+
+    def third(self):
+        for copy in [self.own_mid] + self.line_mid:
             copy.wait_recv()
-        self.line_mid.start()
-        self.line_last.start()
-        self.line_core.start()
-
-    def third(self):
-        self.line_mid.wait_recv()
         self.mid_last.start()
         self.mid_core.start()
 
     def fourth(self):
-        self.line_last.wait_recv()
+        for copy in [self.own_last] + self.line_last:
+            copy.wait_recv()
         self.far_core.start()
         self.mid_last.wait_recv()
         self.cross_core.start()
@@ -349,15 +357,13 @@
             copy.wait_recv()
 
     def settle(self):
-        for copy in self.along_z + [
-            self.line_mid,
-            self.line_last,
-            self.line_core,
-            self.mid_last,
-            self.mid_core,
-            self.far_core,
-            self.cross_core,
-        ]:
+        for copy in (
+            self.along_z
+            + [self.own_mid, self.own_last]
+            + self.line_mid
+            + self.line_last
+            + [self.line_core, self.mid_last, self.mid_core, self.far_core, self.cross_core]
+        ):
             copy.wait_send()
 
 
@@ -517,10 +523,19 @@
 
 LINES = 16
 SLOT_ROWS = 24
+QKV_COLS = 256
+
+
+def qkv_cuts(model):
+    size = 3 * QKV_COLS // 2
+    return [(start, size) for start in range(0, 3 * model, size)]
+
+
 (
     GAIN_ONE, SHIFT_ONE, QUERY_BIAS, VALUE_BIAS, PROJ_SHIFT, SCALE_ONE, GAIN_TWO, SHIFT_TWO, FC2_SHIFT, SCALE_TWO,
 ) = range(10)
 HIDDEN_LINE = 10
+LINE_NAMES = ["line" + str(number) for number in range(HIDDEN_LINE + 1)]
 
 
 def unpack_lines(packed, shard, hidden_shard, vec_ref, hidden_ref):
@@ -557,8 +572,8 @@
     send, recv, local = buffers[-3:]
     place = Place()
     x = place.x
-    width, count, offset = s.scal[0], s.scal[1], s.scal[2]
     rows, model = s.tokens.shape
+    width, count, offset = s.widths[0], s.counts[0], x * rows
     keys = 2 * rows
     hidden = s.w_fc1.shape[2]
     shard, hidden_shard = s.w_qkv.shape[0] * ROW_GROUP, s.w_fc2.shape[0] * ROW_GROUP
@@ -567,12 +582,19 @@
     far_rows = pl.ds(pl.multiple_of((1 - x) * rows, rows), rows)
     sems = Sems(send, recv)
     locals_used = []
+    outgoing = []
+
+    def move(src, dst):
+        locals_used.append(0)
+        copy = pltpu.make_async_copy(src, dst, local.at[len(locals_used) - 1])
+        copy.start()
+        return copy
 
     def gather(src, slots, cuts):
         chunks = []
         for number, (start, size) in enumerate(cuts):
-            sem = local.at[len(locals_used)]
             locals_used.append(0)
+            sem = local.at[len(locals_used) - 1]
             chunks.append(Gather(place, src, slots, pl.ds(start, size), number == 0, sems, sem))
         return chunks
 
@@ -583,7 +605,7 @@
             stages = [buffers.pop(0) for _ in range(3)]
             chunks.append(
                 Reduce(
-                    place, grad, own, *stages, out, start, size, number == 0, sems, pieces and pieces[number],
+                    place, grad, own, *stages, out, start, size, number % 2 == 0, sems, pieces and pieces[number],
                 )
             )
         return grad, chunks
@@ -593,6 +615,13 @@
             for chunk in chunks:
                 step(chunk)
 
+    line_copies = [
+        move(getattr(s, LINE_NAMES[number]), s.raw_hidden if number == HIDDEN_LINE else s.raw.at[number])
+        for number in range(HIDDEN_LINE + 1)
+    ]
+    table_copy = move(s.table, s.table_in)
+    tokens_copy = move(s.tokens, s.tokens_in)
+    cot_copy = move(s.cot, s.cot_in)
     swap = sems.copy(s.tokens, s.far_tokens, place.over_x())
     give = sems.copy(s.give, s.take, place.over_x())
     get_pack = gather(s.pack, s.packs, [(0, LANES)])
@@ -600,34 +629,52 @@
     get_proj = gather(s.w_proj, s.wp, halves(model))
     get_fc1 = gather(s.w_fc1, s.w1, halves(hidden))
     get_fc2 = gather(s.w_fc2, s.w2, halves(model))
-    third = 3 * half
-    qkv_pieces = [
-        [(part * half, part * model + group * half, half) for part in range(3)] for group in range(2)
-    ]
     s.g_fc2, put_fc2 = reduce(s.o_fc2, halves(model), None)
     s.g_fc1, put_fc1 = reduce(s.o_fc1, halves(hidden), None)
     s.g_proj, put_proj = reduce(s.o_proj, halves(model), None)
-    s.g_qkv, put_qkv = reduce(s.o_qkv, [(0, third), (third, third)], qkv_pieces)
+    wide = QKV_COLS
+    qkv_pieces = []
+    for group in range(model // wide):
+        start = group * wide
+        qkv_pieces.append([(0, start, wide), (wide, model + start, wide // 2)])
+        qkv_pieces.append(
+            [(0, model + start + wide // 2, wide // 2), (wide // 2, 2 * model + start, wide)]
+        )
+    s.g_qkv, put_qkv = reduce(s.o_qkv, qkv_cuts(model), qkv_pieces)
     s.g_table, put_table = reduce(s.o_table, [(0, LANES)], None)
     s.g_small, put_small = reduce(s.o_small, [(0, LANES)], None)
     get_table = gather(s.o_table.reshape(1, 8, LANES), s.table_all, [(0, LANES)])
 
     meet(place)
+    for copy in line_copies:
+        copy.wait()
+    s.pack[...] = jnp.zeros_like(s.pack)
+    for number in range(HIDDEN_LINE + 1):
+        source = s.raw_hidden if number == HIDDEN_LINE else s.raw.at[number]
+        s.pack[number // 8, number % 8 : number % 8 + 1, 0 : source.shape[1]] = source[...].astype(F32)
+    each(get_pack, Gather.begin_own, Gather.begin_z)
+    each(get_qkv, Gather.begin_z, Gather.begin_own)
     swap.start()
-    for chunks in (get_pack, get_qkv, get_proj, get_fc1, get_fc2):
-        each(chunks, Gather.begin)
-
+    each(get_proj, Gather.begin_own)
+    table_copy.wait()
+    s.table_lines[...] = jnp.zeros_like(s.table_lines)
+    s.table_lines[0:HEADS, 0 : s.table.shape[1]] = s.table_in[...]
     fill_diagonals(s.table_lines, s.diag, rows, keys, row_span, width, offset)
-    inputs = s.tokens[...].astype(F32)
-    normed, inv_std = norm_rows(inputs)
+    each(get_pack, Gather.second)
+    tokens_copy.wait()
+    normed, inv_std = norm_rows(s.tokens_in[...].astype(F32))
     s.n1[...] = normed
     s.r1[...] = jnp.broadcast_to(inv_std, s.r1.shape)
+    each(get_pack, Gather.third)
+    each(get_fc1, Gather.begin_own)
     s.fold[...] = jnp.zeros_like(s.fold)
     s.lines[...] = jnp.zeros_like(s.lines)
-
-    each(get_pack, Gather.second, Gather.third)
+    each(get_pack, Gather.fourth)
+    each(get_fc2, Gather.begin_own)
     each(get_qkv, Gather.second)
-    each(get_pack, Gather.fourth, Gather.arrive)
+    each(get_proj, Gather.begin_z)
+    each(get_fc1, Gather.begin_z)
+    each(get_pack, Gather.arrive)
     unpack_lines(tile(s.packs, 0, LANES), shard, hidden_shard, s.vec, s.b1)
 
     def line(number):
@@ -642,12 +689,14 @@
     s.h1[far_rows, :] = (far * line(GAIN_ONE) + line(SHIFT_ONE)).astype(BF16)
     each(get_proj, Gather.second)
     s.h1t[...] = s.h1[...].T
-    s.dm[...] = (line(SCALE_TWO) * s.cot[...].astype(F32)).astype(BF16)
+    cot_copy.wait()
+    s.dm[...] = (line(SCALE_TWO) * s.cot_in[...].astype(F32)).astype(BF16)
     set_line(FC2_SHIFT, sum_rows(s.dm[...]))
     each(get_qkv, Gather.third)
+    each(get_proj, Gather.third)
+    each(get_qkv, Gather.fourth)
     each(get_fc1, Gather.second)
-    each(get_qkv, Gather.fourth)
-    each(get_proj, Gather.third)
+    each(get_fc2, Gather.begin_z)
     each(get_qkv, Gather.arrive)
 
     step = 2 * LANES
@@ -665,13 +714,16 @@
         sums = dot(s.h1[own_rows, :], tile(s.wq, start, step))
         s.q[:, cols] = (sums + s.vec[QUERY_BIAS : QUERY_BIAS + 1, cols]).astype(BF16)
 
+    def look(first, last):
+        attend(s.q, s.kv, s.diag, s.probs, s.mixed, width, count, offset, (first, last))
+
+    each(get_proj, Gather.fourth)
+    look(0, 2)
+    look(2, 4)
     each(get_fc1, Gather.third)
-    attend(s.q, s.kv, s.diag, s.probs, s.mixed, width, count, offset, (0, PAIRS // 2))
+    look(4, PAIRS)
+    s.mixedt[...] = s.mixed[...].T
     each(get_fc2, Gather.second)
-    each(get_proj, Gather.fourth)
-    attend(s.q, s.kv, s.diag, s.probs, s.mixed, width, count, offset, (PAIRS // 2, PAIRS))
-    s.mixedt[...] = s.mixed[...].T
-    each(get_fc1, Gather.fourth)
     each(get_proj, Gather.arrive)
 
     @tiles(model // step, step)
@@ -679,15 +731,14 @@
         cols = pl.ds(start, step)
         branch = dot(s.mixed[...], tile(s.wp, start, step)) + s.vec[PROJ_SHIFT : PROJ_SHIFT + 1, cols]
         s.z[:, cols] = branch
-        s.x1[:, cols] = s.tokens[:, cols].astype(F32) + s.vec[SCALE_ONE : SCALE_ONE + 1, cols] * branch
+        s.x1[:, cols] = s.tokens_in[:, cols].astype(F32) + s.vec[SCALE_ONE : SCALE_ONE + 1, cols] * branch
 
     normed, inv_std = norm_rows(s.x1[...])
     s.n2[...] = normed
     s.r2[...] = jnp.broadcast_to(inv_std, s.r2.shape)
     s.h2[...] = (normed * line(GAIN_TWO) + line(SHIFT_TWO)).astype(BF16)
     s.h2t[...] = s.h2[...].T
-    each(get_fc2, Gather.third)
-    each(get_fc1, Gather.arrive)
+    each(get_fc1, Gather.fourth, Gather.arrive)
 
     @tiles(hidden // step, step)
     def _(number, start):
@@ -699,7 +750,7 @@
         s.ut[cols, :] = low.T
         s.slope[:, cols] = gate + act * jnp.exp(act * act * -0.5) * 0.3989422804014327
 
-    each(get_fc2, Gather.fourth)
+    each(get_fc2, Gather.third)
     deep = 8 * hidden_shard
     for group in range(2):
 
@@ -711,6 +762,8 @@
             view[number, :, :, cols] = sums.reshape(8, hidden_shard, half).astype(BF16)
 
         put_fc2[group].begin()
+    each(get_fc2, Gather.fourth)
+    each(put_fc2, Reduce.add_core)
     each(get_fc2, Gather.arrive)
 
     @tiles(Z_SIZE, deep)
@@ -720,7 +773,6 @@
         grad_hidden = dot(s.dm[...], weight, NT)
         s.da[:, cols] = (grad_hidden * s.slope[:, cols]).astype(BF16)
 
-    each(put_fc2, Reduce.add_core)
     for group in range(2):
 
         @tiles(hidden // 2 // step, step)
@@ -731,36 +783,29 @@
 
         put_fc1[group].begin()
 
-    @tiles(model // step, step)
-    def _(number, start):
-        cols = pl.ds(start, step)
-        branch = dot(s.u[...], tile(s.w2, start, step)) + s.vec[FC2_SHIFT : FC2_SHIFT + 1, cols]
-        s.out[:, cols] = (s.x1[:, cols] + s.vec[SCALE_TWO : SCALE_TWO + 1, cols] * branch).astype(BF16)
-        s.lines[SCALE_TWO : SCALE_TWO + 1, cols] = sum_rows(s.cot[:, cols].astype(F32) * branch)
-
-    s.hidden_lines[...] = jnp.broadcast_to(sum_rows(s.da[...]), s.hidden_lines.shape)
     grad = jnp.zeros((rows, model), F32)
     for start in range(0, hidden, model):
         grad = grad + dot(s.da[:, start : start + model], tile(s.w1, start, model), NT)
     set_line(GAIN_TWO, sum_rows(grad * s.n2[...]))
     set_line(SHIFT_TWO, sum_rows(grad))
-    dx1 = s.cot[...].astype(F32) + norm_rows_back(grad, s.n2[...], s.r2[:, 0:1], line(GAIN_TWO))
+    dx1 = s.cot_in[...].astype(F32) + norm_rows_back(grad, s.n2[...], s.r2[:, 0:1], line(GAIN_TWO))
     s.dx1[...] = dx1
     set_line(SCALE_ONE, sum_rows(dx1 * s.z[...]))
     s.dz[...] = (line(SCALE_ONE) * dx1).astype(BF16)
     set_line(PROJ_SHIFT, sum_rows(s.dz[...]))
+    each(put_fc1, Reduce.add_core)
     for group in range(2):
         cols = pl.ds(group * half, half)
-        sums = dot(s.mixedt[...], s.dz[:, cols])
-        put_slots(s.g_proj, cols, sums)
+        put_slots(s.g_proj, cols, dot(s.mixedt[...], s.dz[:, cols]))
         put_proj[group].begin()
     s.dmixed[...] = dot(s.dz[...], tile(s.wp, 0, model), NT).astype(BF16)
-    each(put_fc1, Reduce.add_core)
     each(put_fc2, Reduce.add_first)
 
-    def qkv_grad(group):
-        cols = pl.ds(group * half, half)
-        value_cols = pl.ds(model + group * half, half)
+    def look_back(group):
+        pairs = (group * wide // PAIR, (group + 1) * wide // PAIR)
+        attend_back(s.q, s.kv, s.probs, s.dmixed, s.dq, s.dkv, s.fold, width, offset, pairs)
+        cols = pl.ds(group * wide, wide)
+        value_cols = pl.ds(model + group * wide, wide)
         own_lines = s.h1t[:, own_rows]
         all_lines = s.h1t[...]
         for part, sums in enumerate(
@@ -770,25 +815,22 @@
                 dot(all_lines, s.dkv[:, value_cols]),
             )
         ):
-            target = pl.ds(group * third + part * half, half)
-            put_slots(s.g_qkv, target, sums)
-        put_qkv[group].begin()
-
-    attend_back(
-        s.q, s.kv, s.probs, s.dmixed, s.dq, s.dkv, s.fold, width, offset, (0, PAIRS // 2)
-    )
-    qkv_grad(0)
+            put_slots(s.g_qkv, pl.ds((3 * group + part) * wide, wide), sums)
+        each(put_qkv[2 * group : 2 * group + 2], Reduce.begin)
+
+    look_back(0)
     each(put_proj, Reduce.add_core)
+    look_back(1)
+    each(put_qkv[:2], Reduce.add_core)
     each(put_fc1, Reduce.add_first)
     each(put_fc2, Reduce.add_second)
-    attend_back(
-        s.q, s.kv, s.probs, s.dmixed, s.dq, s.dkv, s.fold, width, offset, (PAIRS // 2, PAIRS)
-    )
-    qkv_grad(1)
+    look_back(2)
     grad_key = dot(s.dkv[:, :model], tile(s.wq, model, model), NT)
     s.dh1[...] = grad_key + dot(s.dkv[:, model:], tile(s.wq, 2 * model, model), NT)
     s.give[...] = s.dh1[far_rows, :].astype(BF16)
     give.start()
+    each(put_qkv[2:4], Reduce.add_core)
+    each(put_proj, Reduce.add_first)
     table_gradient(s.fold, s.table_sums, rows, keys, row_span, width, offset)
 
     @tiles(4 * Z_SIZE, LANES)
@@ -798,20 +840,32 @@
             s.g_table[zz, yy, cc, xx, 0] = s.table_sums[8 * xx : 8 * xx + 8, pl.ds(start, LANES)]
 
     each(put_table, Reduce.begin)
-    each(put_qkv, Reduce.add_core)
-    each(put_proj, Reduce.add_first)
+    each(put_qkv[4:], Reduce.add_core)
+    each(put_qkv[:2], Reduce.add_first)
+
+    @tiles(model // step, step)
+    def _(number, start):
+        cols = pl.ds(start, step)
+        branch = dot(s.u[...], tile(s.w2, start, step)) + s.vec[FC2_SHIFT : FC2_SHIFT + 1, cols]
+        s.out_low[:, cols] = (s.x1[:, cols] + s.vec[SCALE_TWO : SCALE_TWO + 1, cols] * branch).astype(BF16)
+        s.lines[SCALE_TWO : SCALE_TWO + 1, cols] = sum_rows(s.cot_in[:, cols].astype(F32) * branch)
+
+    outgoing.append(move(s.out_low, s.out))
+    s.hidden_lines[...] = jnp.broadcast_to(sum_rows(s.da[...]), s.hidden_lines.shape)
+    set_line(QUERY_BIAS, sum_rows(s.dq[...]))
+    set_line(VALUE_BIAS, sum_rows(s.dkv[:, model:]))
     each(put_table, Reduce.add_core)
     each(put_fc1, Reduce.add_second)
     each(put_fc2, Reduce.finish)
-    set_line(QUERY_BIAS, sum_rows(s.dq[...]))
-    set_line(VALUE_BIAS, sum_rows(s.dkv[:, model:]))
+    outgoing.append(move(s.o_fc2, s.sum_fc2))
     grad = s.dh1[own_rows, :] + dot(s.dq[...], tile(s.wq, 0, model), NT)
     give.wait_recv()
     grad = grad + s.take[...].astype(F32)
     set_line(GAIN_ONE, sum_rows(grad * s.n1[...]))
     set_line(SHIFT_ONE, sum_rows(grad))
     dx = s.dx1[...] + norm_rows_back(grad, s.n1[...], s.r1[:, 0:1], line(GAIN_ONE))
-    s.grad_tokens[...] = dx.astype(BF16)
+    s.dx_low[...] = dx.astype(BF16)
+    outgoing.append(move(s.dx_low, s.grad_tokens))
 
     @tiles(8 * Z_SIZE, 1)
     def _(number, start):
@@ -824,34 +878,76 @@
 
     each(put_small, Reduce.begin)
     each(put_table, Reduce.add_first)
+    each(put_qkv[2:4], Reduce.add_first)
     each(put_small, Reduce.add_core)
-    each(put_qkv, Reduce.add_first)
     each(put_proj, Reduce.add_second)
     each(put_table, Reduce.add_second)
+    each(put_qkv[:2], Reduce.add_second)
     each(put_small, Reduce.add_first)
     each(put_fc1, Reduce.finish)
+    outgoing.append(move(s.o_fc1, s.sum_fc1))
     each(put_table, Reduce.finish)
-    each(get_table, Gather.begin)
+    each(get_table, Gather.begin_own, Gather.begin_z)
+    each(put_qkv[4:], Reduce.add_first)
+    each(put_proj, Reduce.finish)
+    outgoing.append(move(s.o_proj, s.sum_proj))
     each(put_small, Reduce.add_second)
-    each(put_qkv, Reduce.add_second)
-    each(get_table, Gather.second, Gather.third)
-    each(put_proj, Reduce.finish)
+    each(get_table, Gather.second)
+    each(put_qkv[2:4], Reduce.add_second)
+    each(get_table, Gather.third)
+    each(put_qkv[:2], Reduce.finish)
+    each(put_qkv[4:], Reduce.add_second)
     each(put_small, Reduce.finish)
-    each(get_table, Gather.fourth, Gather.arrive)
-    each(put_qkv, Reduce.finish)
+    outgoing.append(move(s.o_small, s.sum_small))
+    each(get_table, Gather.fourth)
+    each(put_qkv[2:4], Reduce.finish)
+    each(get_table, Gather.arrive)
+    for block in range(4 * Z_SIZE):
+        slots = s.table_all.at[block // 4, block // 2 % 2, block % 2]
+        start = block * LANES
+        size = min(LANES, s.o_sums.shape[1] - start)
+        s.o_sums[0:8, start : start + size] = slots[0, :, 0:size]
+        s.o_sums[8:HEADS, start : start + size] = slots[1, 0 : HEADS - 8, 0:size]
+    outgoing.append(move(s.o_sums, s.sum_table))
+    each(put_qkv[4:], Reduce.finish)
+    outgoing.append(move(s.o_qkv, s.sum_qkv))
     swap.wait_send()
     give.wait_send()
     for chunks in (get_pack, get_qkv, get_proj, get_fc1, get_fc2, get_table):
         each(chunks, Gather.settle)
     for chunks in (put_fc2, put_fc1, put_proj, put_qkv, put_table, put_small):
         each(chunks, Reduce.settle)
+    for copy in outgoing:
+        copy.wait()
+
+
+def hand_kernel(count, *refs):
+    small, arrays = refs[0], refs[1 : 1 + count]
+    outs, lines = refs[1 + count : 1 + 2 * count], refs[1 + 2 * count :]
+    for array, out in zip(arrays, outs):
+        out[...] = array[...]
+    for number, out in enumerate(lines):
+        row = number if number < HIDDEN_LINE else LINES
+        out[...] = small[row : row + 1, 0 : out.shape[1]]
+
+
+def hand_out(small, arrays, sizes):
+    vmem = pl.BlockSpec(memory_space=pltpu.VMEM)
+    count = len(arrays)
+    return pl.pallas_call(
+        partial(hand_kernel, count),
+        out_shape=tuple(jax.ShapeDtypeStruct(array.shape, array.dtype) for array in arrays)
+        + tuple(jax.ShapeDtypeStruct((1, size), F32) for size in sizes),
+        in_specs=[vmem] * (1 + count),
+        out_specs=(vmem,) * (count + len(sizes)),
+    )(small, *arrays)
 
 
 def grouped(array):
     return array.reshape(-1, ROW_GROUP, array.shape[-1])
 
 
-def run_layer(row_span, scalars, tokens, cotangent, packed, w_qkv, w_proj, w_fc1, w_fc2, table_lines):
+def run_layer(row_span, widths, counts, tokens, cotangent, vectors, w_qkv, w_proj, w_fc1, w_fc2, table):
     rows, model = tokens.shape
     keys = 2 * rows
     shard, hidden, hidden_shard = w_qkv.shape[0], w_fc1.shape[1], w_fc2.shape[0]
@@ -859,27 +955,46 @@
     vmem = pl.BlockSpec(memory_space=pltpu.VMEM)
     anywhere = pl.BlockSpec(memory_space=pl.ANY)
     inputs = dict(
-        scal=(scalars, smem),
-        tokens=(tokens, vmem),
-        cot=(cotangent, vmem),
-        pack=(grouped(packed), vmem),
+        widths=(widths, smem),
+        counts=(counts, smem),
+        tokens=(tokens, anywhere),
+        cot=(cotangent, anywhere),
         w_qkv=(grouped(w_qkv), anywhere),
         w_proj=(grouped(w_proj), anywhere),
         w_fc1=(grouped(w_fc1), anywhere),
         w_fc2=(grouped(w_fc2), anywhere),
-        table_lines=(table_lines, vmem),
-    )
+        table=(table, anywhere),
+    )
+    for name, vector in zip(LINE_NAMES, vectors):
+        inputs[name] = (vector.reshape(1, -1), anywhere)
     outputs = dict(
         out=((rows, model), BF16),
         grad_tokens=((rows, model), BF16),
+        sum_small=((SLOT_ROWS, LANES), F32),
+        sum_qkv=((shard, 3 * model), F32),
+        sum_proj=((shard, model), F32),
+        sum_fc1=((shard, hidden), F32),
+        sum_fc2=((hidden_shard, model), F32),
+        sum_table=((HEADS, table.shape[1]), F32),
+    )
+    entries = -(-table.shape[1] // (2 * LANES)) * 2 * LANES
+    scratch = dict(
+        raw=((HIDDEN_LINE, 1, shard), BF16),
+        raw_hidden=((1, hidden_shard), BF16),
+        table_in=(table.shape, BF16),
+        tokens_in=((rows, model), BF16),
+        cot_in=((rows, model), BF16),
+        out_low=((rows, model), BF16),
+        dx_low=((rows, model), BF16),
         o_small=((SLOT_ROWS, LANES), F32),
         o_qkv=((shard, 3 * model), F32),
         o_proj=((shard, model), F32),
         o_fc1=((shard, hidden), F32),
         o_fc2=((hidden_shard, model), F32),
+        o_sums=((HEADS, table.shape[1]), F32),
+        pack=((SLOT_ROWS // ROW_GROUP, ROW_GROUP, LANES), F32),
+        table_lines=((HEAD_ROWS, entries), BF16),
         table_all=((Z_SIZE, 2, 2, 2, 8, LANES), F32),
-    )
-    scratch = dict(
         o_table=((8, LANES), F32),
         far_tokens=((rows, model), BF16),
         give=((rows, model), BF16),
@@ -919,7 +1034,7 @@
         dkv=((keys, 2 * model), BF16),
         dh1=((keys, model), F32),
         fold=(((rows + keys) // LANES, 2 * HEAD_ROWS * 8, LANES), F32),
-        table_sums=((HEAD_ROWS, table_lines.shape[1]), F32),
+        table_sums=((HEAD_ROWS, entries), F32),
         lines=((LINES, model), F32),
         hidden_lines=((8, hidden), F32),
     )
@@ -929,7 +1044,7 @@
         (hidden_shard, model, BF16, None),
         (shard, hidden, BF16, None),
         (shard, model, BF16, None),
-        (shard, 3 * model, BF16, [(0, 3 * model // 2)] * 2),
+        (shard, 3 * model, BF16, qkv_cuts(model)),
         (8, LANES, F32, None),
         (SLOT_ROWS, LANES, F32, None),
     ):
@@ -947,12 +1062,12 @@
         partial(layer_kernel, names, row_span),
         out_shape=tuple(jax.ShapeDtypeStruct(shape, dtype) for shape, dtype in outputs.values()),
         in_specs=[spec for _, spec in inputs.values()],
-        out_specs=(vmem,) * len(outputs),
+        out_specs=(anywhere,) * len(outputs),
         scratch_shapes=[pltpu.VMEM(shape, dtype) for shape, dtype in list(scratch.values()) + stages]
         + [
             pltpu.SemaphoreType.DMA((copies,)),
             pltpu.SemaphoreType.DMA((copies,)),
-            pltpu.SemaphoreType.DMA((10,)),
+            pltpu.SemaphoreType.DMA((40,)),
         ],
         compiler_params=pltpu.CompilerParams(
             collective_id=0, has_side_effects=True, vmem_limit_bytes=VMEM_LIMIT
@@ -1195,36 +1310,23 @@
     gamma2,
     bias_table,
 ):
-    local_rows = tokens.shape[0]
-    seq_len = local_rows * lax.axis_size("seq")
-    offset = lax.axis_index("seq") * local_rows
+    seq_len = tokens.shape[0] * lax.axis_size("seq")
     row_span = (seq_len - 1) // (SIDE // 2) + 1
-    table_rows = bias_table.shape[0]
-    entries = -(-table_rows // (2 * LANES)) * 2 * LANES
-    table_lines = jnp.pad(bias_table.T, ((0, HEAD_ROWS - HEADS), (0, entries - table_rows)))
-    scalars = jnp.stack([widths[0], counts[0], offset.astype(jnp.int32)])
-    shard = norm1_gain.shape[0]
-    hidden_shard = fc1_bias.shape[0]
     vectors = [
-        norm1_gain, norm1_shift, q_bias, v_bias, proj_bias, gamma1, norm2_gain, norm2_shift, fc2_bias, gamma2,
+        norm1_gain, norm1_shift, q_bias, v_bias, proj_bias, gamma1, norm2_gain, norm2_shift, fc2_bias, gamma2, fc1_bias,
     ]
-    packed = jnp.concatenate(
-        [
-            jnp.pad(jnp.stack(vectors), ((0, 0), (0, LANES - shard))),
-            jnp.pad(fc1_bias.reshape(1, -1), ((0, SLOT_ROWS - len(vectors) - 1), (0, LANES - hidden_shard))),
-        ]
-    ).astype(F32)
-    output, grad_tokens, small, sum_qkv, sum_proj, sum_fc1, sum_fc2, table_all = run_layer(
-        row_span, scalars, tokens, cotangent, packed, w_qkv, w_proj, w_fc1, w_fc2, table_lines
-    )
-    sums = [small[number, :shard] for number in range(len(vectors))]
-    table_total = (
-        table_all.reshape(entries // LANES, 2, 8, LANES).transpose(1, 2, 0, 3).reshape(HEAD_ROWS, -1)
-    )[:HEADS, :table_rows].T
+    output, grad_tokens, small, *sums = run_layer(
+        row_span, widths, counts, tokens, cotangent, vectors, w_qkv, w_proj, w_fc1, w_fc2, bias_table.T
+    )
+    sizes = [vector.shape[0] for vector in vectors]
+    output, grad_tokens, sum_qkv, sum_proj, sum_fc1, sum_fc2, table_total, *lines = hand_out(
+        small, [output, grad_tokens, *sums], sizes
+    )
+    lines = [line.reshape(-1) for line in lines]
     return (
-        output, grad_tokens, sums[GAIN_ONE], sums[SHIFT_ONE], sum_qkv, sums[QUERY_BIAS], sums[VALUE_BIAS],
-        sum_proj, sums[PROJ_SHIFT], sums[SCALE_ONE], sums[GAIN_TWO], sums[SHIFT_TWO], sum_fc1,
-        small[LINES, :hidden_shard], sum_fc2, sums[FC2_SHIFT], sums[SCALE_TWO], table_total,
+        output, grad_tokens, lines[GAIN_ONE], lines[SHIFT_ONE], sum_qkv, lines[QUERY_BIAS], lines[VALUE_BIAS],
+        sum_proj, lines[PROJ_SHIFT], lines[SCALE_ONE], lines[GAIN_TWO], lines[SHIFT_TWO], sum_fc1,
+        lines[HIDDEN_LINE], sum_fc2, lines[FC2_SHIFT], lines[SCALE_TWO], table_total.T,
     )
 
 

time: 183 us -> 162 us (0.89)
  local copies, waits for them, and re-layouts: 11.8 us -> 0 us
  Pallas kernels: 167 us -> 159 us
  other arithmetic: 1.85 us -> 0 us
    pallas_call x1, Pallas kernels: 167 us -> 156 us  [run_layer(): pl.pallas_call(partial(layer_kernel, names, row_span), out_shape=tuple((j...]
    unnamed x20 -> x0, local copies, waits for them, and re-layouts: 5.33 us -> none
    squeeze x2 -> x0, local copies, waits for them, and re-layouts: 2.7 us -> none  [the longest x1 1.52 us: per_device_linked(): sums = [small[number, :shard] for number in range(len(vectors))]]
    pallas_call x0 -> x1, Pallas kernels: none -> 2.53 us  [hand_out(): pl.pallas_call(partial(hand_kernel, count), out_shape=tuple((jax.ShapeDty...]
where the time goes in v4:
time: 162 us; the launch traced here: 161 us
  Pallas kernels  159 us (98%)
  between operations  2.12 us (1%)
    pallas_call x1, Pallas kernels, run_layer(): pl.pallas_call(partial(layer_kernel, names, row_span), out_shape=tuple((j...  156 us

profile of v4, /device:TPU:0, one launch (start us, length us, event | category | flops | bytes accessed | tf_op | source)
XLA Modules:
  0.0 160.9 jit_solution(11994511840754546319)
XLA Ops:
  2.0 156.2 %shard_map.331 = (bf16[128,768]{1,0:T(8,128)(2,1)}, bf16[128,768]{1,0:T(8,128)(2,1)}, f32[24,128]{1,0:T(8,128)}, f32[24,2304]{1,0:T(8,128)}, f32[24,768]{1,0:T(8...) custom-call(s32[1]{0:T(128)S(6)} %copy.39.refs_0_, s32[1]{0:T(128)S(6)} %copy.38.refs_1_, ...), custom_call_target="tpu_custom_call" | custom-call | tf_op jit(solution)/shard_map/pallas_call | solution.py:1061
  158.2 2.5 %shard_map.332 = (bf16[128,768]{1,0:T(8,128)(2,1)}, bf16[128,768]{1,0:T(8,128)(2,1)}, f32[24,2304]{1,0:T(8,128)}, f32[24,768]{1,0:T(8,128)}, f32[24,3072]{1,0:T(...) custom-call(f32[24,128]{1,0:T(8,128)} %get-tuple-element.44.refs_0_,, ...), custom_call_target="tpu_custom_call" | custom-call | tf_op jit(solution)/shard_map/pallas_call | solution.py:937

commit v5 on v4

--- a/solution.py
+++ b/solution.py
@@ -270,23 +270,37 @@
 
 
 class Sems:
-    def __init__(self, send, recv):
-        self.send, self.recv, self.used = send, recv, 0
-
-    def copy(self, src, dst, device):
-        index = self.used
-        self.used += 1
+    def __init__(self, send, recv, place):
+        self.send, self.recv, self.place = send, recv, place
+        self.sends = self.recvs = 0
+
+    def take_send(self):
+        self.sends += 1
+        return self.send.at[self.sends - 1]
+
+    def take_recv(self):
+        self.recvs += 1
+        return self.recv.at[self.recvs - 1]
+
+    def copy(self, src, dst, device, sent=None, came=None):
         return pltpu.make_async_remote_copy(
             src_ref=src,
             dst_ref=dst,
-            send_sem=self.send.at[index],
-            recv_sem=self.recv.at[index],
+            send_sem=self.take_send() if sent is None else sent,
+            recv_sem=self.take_recv() if came is None else came,
             device_id=device,
             device_id_type=MESH,
         )
 
-
-GATHER_COPIES = 16
+    def total(self, ref, sem):
+        return pltpu.make_async_remote_copy(
+            src_ref=ref,
+            dst_ref=ref,
+            send_sem=sem,
+            recv_sem=sem,
+            device_id=self.place.sibling(),
+            device_id_type=MESH,
+        )
 
 
 class Gather:
@@ -300,9 +314,17 @@
 
         mine = src.at[:, :, cols]
         own = part(z, y, x)
+        self.z = z
         self.local = pltpu.make_async_copy(mine, own, local_sem)
-        steps = range(1, Z_SIZE)
-        self.along_z = [sems.copy(mine, own, place.at(z=place.z_of(step))) for step in steps]
+        sent = sems.take_send()
+        came = [sems.take_recv() for _ in range(1, Z_SIZE)]
+        self.along_z = [
+            sems.copy(mine, own, place.at(z=place.z_of(step)), sent, came[step - 1])
+            for step in range(1, Z_SIZE)
+        ]
+        last_z = Z_SIZE - 1
+        self.relay_up = sems.copy(part(0, y, x), part(0, y, x), place.at(z=last_z), sent, came[last_z - 1])
+        self.relay_down = sems.copy(part(last_z, y, x), part(last_z, y, x), place.at(z=0), sent, came[0])
         line = part(every, y, x)
         mid_line = part(every, 1 - y, x) if x_last else part(every, y, 1 - x)
         far_line = part(every, y, 1 - x) if x_last else part(every, 1 - y, x)
@@ -311,16 +333,23 @@
         if not x_last:
             mid, last = last, mid
         sibling = place.sibling()
-        self.own_mid = sems.copy(mine, own, mid)
-        self.own_last = sems.copy(mine, own, last)
-        came = [part(place.z_of(Z_SIZE - step), y, x) for step in steps]
-        self.line_mid = [sems.copy(piece, piece, mid) for piece in came]
-        self.line_last = [sems.copy(piece, piece, last) for piece in came]
-        self.line_core = sems.copy(line, line, sibling)
-        self.mid_last = sems.copy(mid_line, mid_line, last)
-        self.mid_core = sems.copy(mid_line, mid_line, sibling)
-        self.far_core = sems.copy(far_line, far_line, sibling)
-        self.cross_core = sems.copy(cross_line, cross_line, sibling)
+        mid_came, last_came, core_came = sems.take_recv(), sems.take_recv(), sems.take_recv()
+        self.own_mid = sems.copy(mine, own, mid, sent, mid_came)
+        self.own_last = sems.copy(mine, own, last, sent, last_came)
+        pieces = [part(place.z_of(Z_SIZE - step), y, x) for step in range(1, Z_SIZE)]
+        self.line_mid = [sems.copy(piece, piece, mid, sent, mid_came) for piece in pieces]
+        self.line_last = [sems.copy(piece, piece, last, sent, last_came) for piece in pieces]
+        self.line_core = sems.copy(line, line, sibling, sent, core_came)
+        self.mid_last = sems.copy(mid_line, mid_line, last, sent)
+        self.mid_core = sems.copy(mid_line, mid_line, sibling, sent, core_came)
+        self.far_core = sems.copy(far_line, far_line, sibling, sent, core_came)
+        self.cross_core = sems.copy(cross_line, cross_line, sibling, sent, core_came)
+        self.all_mid = sems.total(mid_line, mid_came)
+        self.all_last = sems.total(far_line, last_came)
+        self.all_core = sems.total(slots.at[:, :, 1 - c, :, :, cols], core_came)
+        flat = slots.reshape((8 * Z_SIZE * groups,) + slots.shape[4:])
+        self.outer_sent = sems.total(flat.at[pl.ds(0, (8 * Z_SIZE - 2) * groups), :, cols], sent)
+        self.inner_sent = sems.total(flat.at[:, :, cols], sent)
 
     def begin_own(self):
         self.local.start()
@@ -328,51 +357,143 @@
         self.own_last.start()
 
     def begin_z(self):
-        for copy in self.along_z:
-            copy.start()
+        up, across, down = self.along_z
+
+        @pl.when(self.z != Z_SIZE - 1)
+        def _():
+            up.start()
+
+        @pl.when(self.z != 0)
+        def _():
+            down.start()
+
+        across.start()
+
+    def pass_on(self, number):
+        self.line_mid[number].start()
+        self.line_last[number].start()
 
     def second(self):
-        for copy, onward, beyond in zip(self.along_z, self.line_mid, self.line_last):
-            copy.wait_recv()
-            onward.start()
-            beyond.start()
+        up, across, down = self.along_z
+        across.wait_recv()
+
+        @pl.when(self.z == Z_SIZE - 2)
+        def _():
+            self.relay_up.start()
+
+        @pl.when(self.z == 1)
+        def _():
+            self.relay_down.start()
+
+        self.pass_on(1)
+
+        @pl.when(self.z >= Z_SIZE // 2)
+        def _():
+            up.wait_recv()
+            self.pass_on(0)
+            down.wait_recv()
+            self.pass_on(2)
+
+        @pl.when(self.z < Z_SIZE // 2)
+        def _():
+            down.wait_recv()
+            self.pass_on(2)
+            up.wait_recv()
+            self.pass_on(0)
+
         self.local.wait()
         self.line_core.start()
 
     def third(self):
-        for copy in [self.own_mid] + self.line_mid:
-            copy.wait_recv()
+        self.all_mid.wait_recv()
         self.mid_last.start()
         self.mid_core.start()
 
     def fourth(self):
-        for copy in [self.own_last] + self.line_last:
-            copy.wait_recv()
+        self.all_last.wait_recv()
         self.far_core.start()
         self.mid_last.wait_recv()
         self.cross_core.start()
 
     def arrive(self):
-        for copy in (self.line_core, self.mid_core, self.far_core, self.cross_core):
+        self.all_core.wait_recv()
+
+    def settle(self):
+        inner = (self.z - 1) * (Z_SIZE - 2 - self.z) >= 0
+
+        @pl.when(inner)
+        def _():
+            self.inner_sent.wait_send()
+
+        @pl.when(jnp.logical_not(inner))
+        def _():
+            self.outer_sent.wait_send()
+
+
+class GatherLate(Gather):
+    def __init__(self, place, src, slots, cols, x_last, sems, local_sem):
+        z, y, c, x = place.z, place.y, place.c, place.x
+        groups = src.shape[0]
+        sibling = place.sibling()
+
+        def plane(a):
+            return slots.at[a, :, c, :, :, cols]
+
+        def part(b, e):
+            return slots.at[z, b, c, pl.ds(e * groups, groups), :, cols]
+
+        mine = src.at[:, :, cols]
+        own = part(y, x)
+        self.local = pltpu.make_async_copy(mine, own, local_sem)
+        sent = sems.take_send()
+        near, last = place.over_x(), place.over_y()
+        piece = part(y, 1 - x)
+        if not x_last:
+            near, last = last, near
+            piece = part(1 - y, x)
+        self.own_near = sems.copy(mine, own, near, sent)
+        self.own_last = sems.copy(mine, own, last, sent)
+        self.near_last = sems.copy(piece, piece, last, sent)
+        self.along_z = [
+            sems.copy(plane(z), plane(z), place.at(z=place.z_of(step)), sent) for step in range(1, Z_SIZE)
+        ]
+        core_came = sems.take_recv()
+        self.line_core = sems.copy(plane(z), plane(z), sibling, sent, core_came)
+        self.far_core = []
+        for step in range(1, Z_SIZE):
+            far = plane(place.z_of(Z_SIZE - step))
+            self.far_core.append(sems.copy(far, far, sibling, sent, core_came))
+        self.all_core = sems.total(slots.at[:, :, 1 - c, :, :, cols], core_came)
+        flat = slots.reshape((8 * Z_SIZE * groups,) + slots.shape[4:])
+        self.all_sent = sems.total(flat.at[pl.ds(0, (8 * Z_SIZE - 1) * groups), :, cols], sent)
+
+    def begin_own(self):
+        self.local.start()
+        self.own_near.start()
+        self.own_last.start()
+
+    def begin_z(self):
+        self.own_near.wait_recv()
+        self.near_last.start()
+
+    def second(self):
+        self.own_last.wait_recv()
+        self.near_last.wait_recv()
+        self.local.wait()
+        for copy in self.along_z:
+            copy.start()
+        self.line_core.start()
+
+    def third(self):
+        pass
+
+    def fourth(self):
+        for copy, onward in zip(self.along_z, self.far_core):
             copy.wait_recv()
+            onward.start()
 
     def settle(self):
-        for copy in (
-            self.along_z
-            + [self.own_mid, self.own_last]
-            + self.line_mid
-            + self.line_last
-            + [self.line_core, self.mid_last, self.mid_core, self.far_core, self.cross_core]
-        ):
-            copy.wait_send()
-
-
-def halves(width):
-    middle = width // 2 // LANES * LANES
-    return [(0, middle), (middle, width - middle)]
-
-
-REDUCE_COPIES = 6
+        self.all_sent.wait_send()
 
 
 class Reduce:
@@ -391,8 +512,9 @@
         every = slice(None)
         cols = pl.ds(start, size)
         self.cols = cols
+        sent = sems.take_send()
         self.to_core = sems.copy(
-            grad.at[:, :, 1 - c, :, :, :, cols], own.at[:, :, :, :, :, cols], place.sibling()
+            grad.at[:, :, 1 - c, :, :, :, cols], own.at[:, :, :, :, :, cols], place.sibling(), sent
         )
         over_first, over_second = place.over_x(), place.over_y()
         if x_first:
@@ -401,14 +523,18 @@
             over_first, over_second = over_second, over_first
             leaving, other = own.at[:, 1 - y, :, :, :, cols], 1 - x
         self.kept = y if x_first else x
-        self.over_first = sems.copy(leaving, first, over_first)
-        self.over_second = sems.copy(first.at[:, other], second, over_second)
+        self.over_first = sems.copy(leaving, first, over_first, sent)
+        self.over_second = sems.copy(first.at[:, other], second, over_second, sent)
+        came = sems.take_recv()
         self.along_z = []
         for step in range(1, Z_SIZE):
             target = place.z_of(step)
             self.along_z.append(
-                sems.copy(second.at[target], third.at[step - 1], place.at(z=target))
+                sems.copy(second.at[target], third.at[step - 1], place.at(z=target), sent, came)
             )
+        self.all_z = sems.total(third, came)
+        slots = grad.reshape((8 * Z_SIZE,) + grad.shape[4:])
+        self.all_sent = sems.total(slots.at[pl.ds(0, 8 * Z_SIZE - 1), :, :, cols], sent)
 
     def begin(self):
         self.to_core.start()
@@ -426,6 +552,9 @@
             return carry
 
         lax.fori_loop(0, 2 * Z_SIZE, add, 0)
+        self.send_core()
+
+    def send_core(self):
         self.over_first.start()
 
     def add_first(self):
@@ -460,15 +589,87 @@
 
     def finish(self):
         total = self.second[self.place.z].astype(F32)
-        for step, copy in enumerate(self.along_z):
-            copy.wait_recv()
+        self.all_z.wait_recv()
+        for step in range(Z_SIZE - 1):
             total = total + self.third[step].astype(F32)
         for source, target, size in self.pieces:
             self.out[:, target : target + size] = total[:, source : source + size]
 
     def settle(self):
-        for copy in [self.to_core, self.over_first, self.over_second] + self.along_z:
-            copy.wait_send()
+        self.all_sent.wait_send()
+
+
+class ReduceEarly(Reduce):
+    def __init__(self, place, grad, own, by_z, plane, first, second, out, start, size, x_first, sems, pieces=None):
+        self.pieces = pieces or [(0, start, size)]
+        self.x_first = x_first
+        rows = out.shape[0]
+
+        def flat(ref):
+            return ref.reshape(ref.shape[:-3] + (rows, ref.shape[-1]))
+
+        self.place, self.out = place, out
+        self.grad, self.own, self.by_z = flat(grad), flat(own), flat(by_z)
+        self.plane, self.first, self.second = flat(plane), flat(first), flat(second)
+        c, x, y = place.c, place.x, place.y
+        cols = pl.ds(start, size)
+        self.cols = cols
+        sent = sems.take_send()
+        self.to_core = sems.copy(
+            grad.at[:, :, 1 - c, :, :, :, cols], own.at[:, :, :, :, :, cols], place.sibling(), sent
+        )
+        came = sems.take_recv()
+        self.along_z = []
+        for step in range(1, Z_SIZE):
+            target = place.z_of(step)
+            self.along_z.append(
+                sems.copy(
+                    own.at[target, :, :, :, :, cols], by_z.at[step - 1], place.at(z=target), sent, came
+                )
+            )
+        self.all_z = sems.total(by_z, came)
+        over_first, over_second = place.over_x(), place.over_y()
+        if x_first:
+            leaving, other = plane.at[:, 1 - x], 1 - y
+        else:
+            over_first, over_second = over_second, over_first
+            leaving, other = plane.at[1 - y], 1 - x
+        self.kept = y if x_first else x
+        self.over_first = sems.copy(leaving, first, over_first, sent)
+        self.over_second = sems.copy(first.at[other], second, over_second, sent)
+        slots = grad.reshape((8 * Z_SIZE,) + grad.shape[4:])
+        self.all_sent = sems.total(slots.at[pl.ds(0, 8 * Z_SIZE - 1), :, :, cols], sent)
+
+    def send_core(self):
+        for copy in self.along_z:
+            copy.start()
+
+    def add_first(self):
+        self.all_z.wait_recv()
+        z = self.place.z
+        for y in range(2):
+            for x in range(2):
+                total = self.own[z, y, x, :, self.cols].astype(F32)
+                for step in range(Z_SIZE - 1):
+                    total = total + self.by_z[step, y, x].astype(F32)
+                self.plane[y, x] = total.astype(self.plane.dtype)
+        self.over_first.start()
+
+    def add_second(self):
+        self.over_first.wait_recv()
+        for other in range(2):
+            if self.x_first:
+                mine = self.plane[other, self.place.x].astype(F32)
+            else:
+                mine = self.plane[self.place.y, other].astype(F32)
+            self.first[other] = (mine + self.first[other].astype(F32)).astype(self.first.dtype)
+        self.over_second.start()
+
+    def finish(self):
+        self.over_second.wait_recv()
+        total = self.first[self.kept].astype(F32) + self.second[...].astype(F32)
+        for source, target, size in self.pieces:
+            self.out[:, target : target + size] = total[:, source : source + size]
 
 
 class Names:
@@ -526,9 +727,26 @@
 QKV_COLS = 256
 
 
+def quarters(width):
+    large = -(-width // 4 // LANES) * LANES
+    small = width // 2 - large
+    cuts = [(0, large), (large, large), (2 * large, small), (2 * large + small, small)]
+    return [(start, size, False) for start, size in cuts]
+
+
+def halves(width, turned):
+    middle = width // 2 // LANES * LANES
+    return [(0, middle, turned), (middle, width - middle, turned)]
+
+
+def fc2_cuts(width):
+    part = width // 3
+    return [(0, part, False), (part, part, False), (2 * part, width - 2 * part, True)]
+
+
 def qkv_cuts(model):
     size = 3 * QKV_COLS // 2
-    return [(start, size) for start in range(0, 3 * model, size)]
+    return [(start, size, False) for start in range(0, 3 * model, size)]
 
 
 (
@@ -580,7 +798,7 @@
     half = model // 2
     own_rows = pl.ds(pl.multiple_of(x * rows, rows), rows)
     far_rows = pl.ds(pl.multiple_of((1 - x) * rows, rows), rows)
-    sems = Sems(send, recv)
+    sems = Sems(send, recv, place)
     locals_used = []
     outgoing = []
 
@@ -590,21 +808,28 @@
         copy.start()
         return copy
 
+    def hand(src, dst):
+        copy = pltpu.make_async_copy(src, dst, local.at[len(outgoing)])
+        copy.start()
+        outgoing.append(copy)
+
     def gather(src, slots, cuts):
         chunks = []
-        for number, (start, size) in enumerate(cuts):
+        for number, (start, size, late) in enumerate(cuts):
             locals_used.append(0)
             sem = local.at[len(locals_used) - 1]
-            chunks.append(Gather(place, src, slots, pl.ds(start, size), number == 0, sems, sem))
+            kind = GatherLate if late else Gather
+            chunks.append(kind(place, src, slots, pl.ds(start, size), number % 2 == 0, sems, sem))
         return chunks
 
     def reduce(out, cuts, pieces):
         chunks = []
         grad, own = buffers.pop(0), buffers.pop(0)
-        for number, (start, size) in enumerate(cuts):
-            stages = [buffers.pop(0) for _ in range(3)]
+        for number, (start, size, early) in enumerate(cuts):
+            stages = [buffers.pop(0) for _ in range(4 if early else 3)]
+            kind = ReduceEarly if early else Reduce
             chunks.append(
-                Reduce(
+                kind(
                     place, grad, own, *stages, out, start, size, number % 2 == 0, sems, pieces and pieces[number],
                 )
             )
@@ -613,7 +838,7 @@
     def each(chunks, *steps):
         for step in steps:
             for chunk in chunks:
-                step(chunk)
+                getattr(chunk, step.__name__)()
 
     line_copies = [
         move(getattr(s, LINE_NAMES[number]), s.raw_hidden if number == HIDDEN_LINE else s.raw.at[number])
@@ -624,14 +849,14 @@
     cot_copy = move(s.cot, s.cot_in)
     swap = sems.copy(s.tokens, s.far_tokens, place.over_x())
     give = sems.copy(s.give, s.take, place.over_x())
-    get_pack = gather(s.pack, s.packs, [(0, LANES)])
-    get_qkv = gather(s.w_qkv, s.wq, halves(3 * model))
-    get_proj = gather(s.w_proj, s.wp, halves(model))
-    get_fc1 = gather(s.w_fc1, s.w1, halves(hidden))
-    get_fc2 = gather(s.w_fc2, s.w2, halves(model))
-    s.g_fc2, put_fc2 = reduce(s.o_fc2, halves(model), None)
-    s.g_fc1, put_fc1 = reduce(s.o_fc1, halves(hidden), None)
-    s.g_proj, put_proj = reduce(s.o_proj, halves(model), None)
+    get_pack = gather(s.pack, s.packs, [(0, LANES, False)])
+    get_qkv = gather(s.w_qkv, s.wq, halves(3 * model, False))
+    get_proj = gather(s.w_proj, s.wp, halves(model, False))
+    get_fc1 = gather(s.w_fc1, s.w1, quarters(hidden))
+    get_fc2 = gather(s.w_fc2, s.w2, fc2_cuts(model))
+    s.g_fc2, put_fc2 = reduce(s.o_fc2, fc2_cuts(model), None)
+    s.g_fc1, put_fc1 = reduce(s.o_fc1, quarters(hidden), None)
+    s.g_proj, put_proj = reduce(s.o_proj, halves(model, False), None)
     wide = QKV_COLS
     qkv_pieces = []
     for group in range(model // wide):
@@ -641,9 +866,9 @@
             [(0, model + start + wide // 2, wide // 2), (wide // 2, 2 * model + start, wide)]
         )
     s.g_qkv, put_qkv = reduce(s.o_qkv, qkv_cuts(model), qkv_pieces)
-    s.g_table, put_table = reduce(s.o_table, [(0, LANES)], None)
-    s.g_small, put_small = reduce(s.o_small, [(0, LANES)], None)
-    get_table = gather(s.o_table.reshape(1, 8, LANES), s.table_all, [(0, LANES)])
+    s.g_table, put_table = reduce(s.o_table, [(0, LANES, False)], None)
+    s.g_small, put_small = reduce(s.o_small, [(0, LANES, False)], None)
+    get_table = gather(s.o_table.reshape(1, 8, LANES), s.table_all, [(0, LANES, False)])
 
     meet(place)
     for copy in line_copies:
@@ -666,14 +891,15 @@
     s.n1[...] = normed
     s.r1[...] = jnp.broadcast_to(inv_std, s.r1.shape)
     each(get_pack, Gather.third)
+    each(get_proj, Gather.begin_z)
+    each(get_fc1[:2], Gather.begin_z)
     each(get_fc1, Gather.begin_own)
     s.fold[...] = jnp.zeros_like(s.fold)
     s.lines[...] = jnp.zeros_like(s.lines)
     each(get_pack, Gather.fourth)
     each(get_fc2, Gather.begin_own)
     each(get_qkv, Gather.second)
-    each(get_proj, Gather.begin_z)
-    each(get_fc1, Gather.begin_z)
+    each(get_fc1[2:], Gather.begin_z)
     each(get_pack, Gather.arrive)
     unpack_lines(tile(s.packs, 0, LANES), shard, hidden_shard, s.vec, s.b1)
 
@@ -692,11 +918,15 @@
     cot_copy.wait()
     s.dm[...] = (line(SCALE_TWO) * s.cot_in[...].astype(F32)).astype(BF16)
     set_line(FC2_SHIFT, sum_rows(s.dm[...]))
+    each(get_fc1[:2], Gather.second)
+    each(get_fc2, Gather.begin_z)
+    each(get_fc2[2:], Gather.second)
     each(get_qkv, Gather.third)
     each(get_proj, Gather.third)
+    each(get_fc1[2:], Gather.second)
     each(get_qkv, Gather.fourth)
-    each(get_fc1, Gather.second)
-    each(get_fc2, Gather.begin_z)
+    each(get_fc1[:2], Gather.third)
+    each(get_fc2[:2], Gather.second)
     each(get_qkv, Gather.arrive)
 
     step = 2 * LANES
@@ -719,11 +949,12 @@
 
     each(get_proj, Gather.fourth)
     look(0, 2)
+    each(get_fc1[2:], Gather.third)
     look(2, 4)
-    each(get_fc1, Gather.third)
+    each(get_fc1[:2], Gather.fourth)
     look(4, PAIRS)
+    each(get_fc2[:2], Gather.third)
     s.mixedt[...] = s.mixed[...].T
-    each(get_fc2, Gather.second)
     each(get_proj, Gather.arrive)
 
     @tiles(model // step, step)
@@ -738,7 +969,8 @@
     s.r2[...] = jnp.broadcast_to(inv_std, s.r2.shape)
     s.h2[...] = (normed * line(GAIN_TWO) + line(SHIFT_TWO)).astype(BF16)
     s.h2t[...] = s.h2[...].T
-    each(get_fc1, Gather.fourth, Gather.arrive)
+    each(get_fc1[2:], Gather.fourth)
+    each(get_fc1, Gather.arrive)
 
     @tiles(hidden // step, step)
     def _(number, start):
@@ -750,18 +982,17 @@
         s.ut[cols, :] = low.T
         s.slope[:, cols] = gate + act * jnp.exp(act * act * -0.5) * 0.3989422804014327
 
-    each(get_fc2, Gather.third)
     deep = 8 * hidden_shard
-    for group in range(2):
+    for chunk, (first, size, _) in zip(put_fc2, fc2_cuts(model)):
 
         @tiles(Z_SIZE, deep)
         def _(number, start):
-            cols = pl.ds(group * half, half)
+            cols = pl.ds(first, size)
             sums = dot(s.ut[pl.ds(start, deep), :], s.dm[:, cols])
             view = s.g_fc2.reshape(Z_SIZE, 8, hidden_shard, model)
-            view[number, :, :, cols] = sums.reshape(8, hidden_shard, half).astype(BF16)
-
-        put_fc2[group].begin()
+            view[number, :, :, cols] = sums.reshape(8, hidden_shard, size).astype(BF16)
+
+        chunk.begin()
     each(get_fc2, Gather.fourth)
     each(put_fc2, Reduce.add_core)
     each(get_fc2, Gather.arrive)
@@ -773,19 +1004,22 @@
         grad_hidden = dot(s.dm[...], weight, NT)
         s.da[:, cols] = (grad_hidden * s.slope[:, cols]).astype(BF16)
 
-    for group in range(2):
-
-        @tiles(hidden // 2 // step, step)
+    for chunk, (first, size, _) in zip(put_fc1, quarters(hidden)):
+
+        @tiles(size // step, step)
         def _(number, start):
-            cols = pl.ds(start + group * (hidden // 2), step)
-            sums = dot(s.h2t[...], s.da[:, cols])
-            put_slots(s.g_fc1, cols, sums)
-
-        put_fc1[group].begin()
+            cols = pl.ds(start + first, step)
+            put_slots(s.g_fc1, cols, dot(s.h2t[...], s.da[:, cols]))
+
+        chunk.begin()
 
     grad = jnp.zeros((rows, model), F32)
     for start in range(0, hidden, model):
         grad = grad + dot(s.da[:, start : start + model], tile(s.w1, start, model), NT)
+    s.dh2[...] = grad
+    each(put_fc2[:2], Reduce.add_first)
+    each(put_fc1, Reduce.add_core)
+    grad = s.dh2[...]
     set_line(GAIN_TWO, sum_rows(grad * s.n2[...]))
     set_line(SHIFT_TWO, sum_rows(grad))
     dx1 = s.cot_in[...].astype(F32) + norm_rows_back(grad, s.n2[...], s.r2[:, 0:1], line(GAIN_TWO))
@@ -793,13 +1027,11 @@
     set_line(SCALE_ONE, sum_rows(dx1 * s.z[...]))
     s.dz[...] = (line(SCALE_ONE) * dx1).astype(BF16)
     set_line(PROJ_SHIFT, sum_rows(s.dz[...]))
-    each(put_fc1, Reduce.add_core)
     for group in range(2):
         cols = pl.ds(group * half, half)
         put_slots(s.g_proj, cols, dot(s.mixedt[...], s.dz[:, cols]))
         put_proj[group].begin()
     s.dmixed[...] = dot(s.dz[...], tile(s.wp, 0, model), NT).astype(BF16)
-    each(put_fc2, Reduce.add_first)
 
     def look_back(group):
         pairs = (group * wide // PAIR, (group + 1) * wide // PAIR)
@@ -821,16 +1053,12 @@
     look_back(0)
     each(put_proj, Reduce.add_core)
     look_back(1)
-    each(put_qkv[:2], Reduce.add_core)
-    each(put_fc1, Reduce.add_first)
-    each(put_fc2, Reduce.add_second)
+    each(put_fc2[:2], Reduce.add_second)
     look_back(2)
     grad_key = dot(s.dkv[:, :model], tile(s.wq, model, model), NT)
     s.dh1[...] = grad_key + dot(s.dkv[:, model:], tile(s.wq, 2 * model, model), NT)
     s.give[...] = s.dh1[far_rows, :].astype(BF16)
     give.start()
-    each(put_qkv[2:4], Reduce.add_core)
-    each(put_proj, Reduce.add_first)
     table_gradient(s.fold, s.table_sums, rows, keys, row_span, width, offset)
 
     @tiles(4 * Z_SIZE, LANES)
@@ -840,9 +1068,11 @@
             s.g_table[zz, yy, cc, xx, 0] = s.table_sums[8 * xx : 8 * xx + 8, pl.ds(start, LANES)]
 
     each(put_table, Reduce.begin)
-    each(put_qkv[4:], Reduce.add_core)
-    each(put_qkv[:2], Reduce.add_first)
-
+    each(put_fc2[2:], Reduce.add_first)
+    each(put_fc1[:2], Reduce.add_first)
+    each(put_table, Reduce.add_core)
+    each(put_fc1[2:], Reduce.add_first)
+    each(put_qkv, Reduce.add_core)
     @tiles(model // step, step)
     def _(number, start):
         cols = pl.ds(start, step)
@@ -850,14 +1080,10 @@
         s.out_low[:, cols] = (s.x1[:, cols] + s.vec[SCALE_TWO : SCALE_TWO + 1, cols] * branch).astype(BF16)
         s.lines[SCALE_TWO : SCALE_TWO + 1, cols] = sum_rows(s.cot_in[:, cols].astype(F32) * branch)
 
-    outgoing.append(move(s.out_low, s.out))
+    hand(s.out_low, s.out)
     s.hidden_lines[...] = jnp.broadcast_to(sum_rows(s.da[...]), s.hidden_lines.shape)
     set_line(QUERY_BIAS, sum_rows(s.dq[...]))
     set_line(VALUE_BIAS, sum_rows(s.dkv[:, model:]))
-    each(put_table, Reduce.add_core)
-    each(put_fc1, Reduce.add_second)
-    each(put_fc2, Reduce.finish)
-    outgoing.append(move(s.o_fc2, s.sum_fc2))
     grad = s.dh1[own_rows, :] + dot(s.dq[...], tile(s.wq, 0, model), NT)
     give.wait_recv()
     grad = grad + s.take[...].astype(F32)
@@ -865,7 +1091,7 @@
     set_line(SHIFT_ONE, sum_rows(grad))
     dx = s.dx1[...] + norm_rows_back(grad, s.n1[...], s.r1[:, 0:1], line(GAIN_ONE))
     s.dx_low[...] = dx.astype(BF16)
-    outgoing.append(move(s.dx_low, s.grad_tokens))
+    hand(s.dx_low, s.grad_tokens)
 
     @tiles(8 * Z_SIZE, 1)
     def _(number, start):
@@ -877,30 +1103,36 @@
         s.g_small[zz, yy, cc, xx, LINES // ROW_GROUP] = moved[:, :LANES]
 
     each(put_small, Reduce.begin)
+    each(put_fc1[:2], Reduce.add_second)
     each(put_table, Reduce.add_first)
+    each(put_fc1[2:], Reduce.add_second)
+    each(put_small, Reduce.add_core)
+    each(put_proj, Reduce.add_first)
+    each(put_fc2[2:], Reduce.add_second)
+    each(put_table, Reduce.add_second)
+    each(put_qkv[:2], Reduce.add_first)
     each(put_qkv[2:4], Reduce.add_first)
-    each(put_small, Reduce.add_core)
+    each(put_small, Reduce.add_first)
+    each(put_qkv[4:], Reduce.add_first)
     each(put_proj, Reduce.add_second)
-    each(put_table, Reduce.add_second)
-    each(put_qkv[:2], Reduce.add_second)
-    each(put_small, Reduce.add_first)
-    each(put_fc1, Reduce.finish)
-    outgoing.append(move(s.o_fc1, s.sum_fc1))
     each(put_table, Reduce.finish)
     each(get_table, Gather.begin_own, Gather.begin_z)
-    each(put_qkv[4:], Reduce.add_first)
+    each(put_qkv[:2], Reduce.add_second)
+    each(put_small, Reduce.add_second)
+    each(put_qkv[2:4], Reduce.add_second)
+    each(put_fc2, Reduce.finish)
+    hand(s.o_fc2, s.sum_fc2)
+    each(put_qkv[4:], Reduce.add_second)
+    each(get_table, Gather.second)
+    each(put_fc1, Reduce.finish)
+    hand(s.o_fc1, s.sum_fc1)
+    each(get_table, Gather.third)
     each(put_proj, Reduce.finish)
-    outgoing.append(move(s.o_proj, s.sum_proj))
-    each(put_small, Reduce.add_second)
-    each(get_table, Gather.second)
-    each(put_qkv[2:4], Reduce.add_second)
-    each(get_table, Gather.third)
-    each(put_qkv[:2], Reduce.finish)
-    each(put_qkv[4:], Reduce.add_second)
+    hand(s.o_proj, s.sum_proj)
+    each(get_table, Gather.fourth)
     each(put_small, Reduce.finish)
-    outgoing.append(move(s.o_small, s.sum_small))
-    each(get_table, Gather.fourth)
-    each(put_qkv[2:4], Reduce.finish)
+    hand(s.o_small, s.sum_small)
+    each(put_qkv[:4], Reduce.finish)
     each(get_table, Gather.arrive)
     for block in range(4 * Z_SIZE):
         slots = s.table_all.at[block // 4, block // 2 % 2, block % 2]
@@ -908,9 +1140,9 @@
         size = min(LANES, s.o_sums.shape[1] - start)
         s.o_sums[0:8, start : start + size] = slots[0, :, 0:size]
         s.o_sums[8:HEADS, start : start + size] = slots[1, 0 : HEADS - 8, 0:size]
-    outgoing.append(move(s.o_sums, s.sum_table))
+    hand(s.o_sums, s.sum_table)
     each(put_qkv[4:], Reduce.finish)
-    outgoing.append(move(s.o_qkv, s.sum_qkv))
+    hand(s.o_qkv, s.sum_qkv)
     swap.wait_send()
     give.wait_send()
     for chunks in (get_pack, get_qkv, get_proj, get_fc1, get_fc2, get_table):
@@ -1033,6 +1265,7 @@
         dq=((rows, model), BF16),
         dkv=((keys, 2 * model), BF16),
         dh1=((keys, model), F32),
+        dh2=((rows, model), F32),
         fold=(((rows + keys) // LANES, 2 * HEAD_ROWS * 8, LANES), F32),
         table_sums=((HEAD_ROWS, entries), F32),
         lines=((LINES, model), F32),
@@ -1041,22 +1274,25 @@
     stages = []
     chunks = 0
     for slot_rows, slot_width, dtype, cuts in (
-        (hidden_shard, model, BF16, None),
-        (shard, hidden, BF16, None),
-        (shard, model, BF16, None),
+        (hidden_shard, model, BF16, fc2_cuts(model)),
+        (shard, hidden, BF16, quarters(hidden)),
+        (shard, model, BF16, halves(model, False)),
         (shard, 3 * model, BF16, qkv_cuts(model)),
-        (8, LANES, F32, None),
-        (SLOT_ROWS, LANES, F32, None),
+        (8, LANES, F32, [(0, LANES, False)]),
+        (SLOT_ROWS, LANES, F32, [(0, LANES, False)]),
     ):
-        cuts = cuts or ([(0, slot_width)] if slot_width <= LANES else halves(slot_width))
         groups = slot_rows // ROW_GROUP
         stages.append(((Z_SIZE, 2, 2, 2, groups, ROW_GROUP, slot_width), dtype))
         stages.append(((Z_SIZE, 2, 2, groups, ROW_GROUP, slot_width), dtype))
-        for _, size in cuts:
-            for lead in ((Z_SIZE, 2), (Z_SIZE,), (Z_SIZE - 1,)):
+        for _, size, early in cuts:
+            leads = ((Z_SIZE, 2), (Z_SIZE,), (Z_SIZE - 1,))
+            if early:
+                leads = ((Z_SIZE - 1, 2, 2), (2, 2), (2,), ())
+            for lead in leads:
                 stages.append((lead + (groups, ROW_GROUP, size), dtype))
             chunks += 1
-    copies = 2 + GATHER_COPIES * 10 + REDUCE_COPIES * chunks
+    gathers = 13
+    sends, recvs = 2 + gathers + chunks, 2 + 7 * gathers + 4 * chunks
     names = list(inputs) + list(outputs) + list(scratch)
     return pl.pallas_call(
         partial(layer_kernel, names, row_span),
@@ -1065,9 +1301,9 @@
         out_specs=(anywhere,) * len(outputs),
         scratch_shapes=[pltpu.VMEM(shape, dtype) for shape, dtype in list(scratch.values()) + stages]
         + [
-            pltpu.SemaphoreType.DMA((copies,)),
-            pltpu.SemaphoreType.DMA((copies,)),
-            pltpu.SemaphoreType.DMA((40,)),
+            pltpu.SemaphoreType.DMA((sends,)),
+            pltpu.SemaphoreType.DMA((recvs,)),
+            pltpu.SemaphoreType.DMA((HIDDEN_LINE + 4 + gathers,)),
         ],
         compiler_params=pltpu.CompilerParams(
             collective_id=0, has_side_effects=True, vmem_limit_bytes=VMEM_LIMIT

time: 162 us -> 154 us (0.951)
  Pallas kernels: 159 us -> 150 us
    pallas_call x1, Pallas kernels: 156 us -> 148 us  [run_layer(): pl.pallas_call(partial(layer_kernel, names, row_span), out_shape=tuple((j...]
where the time goes in v5:
time: 154 us; the launch traced here: 152 us
  Pallas kernels  150 us (97%)
  between operations  2.12 us (1%)
    pallas_call x1, Pallas kernels, run_layer(): pl.pallas_call(partial(layer_kernel, names, row_span), out_shape=tuple((j...  148 us

profile of v5, /device:TPU:0, one launch (start us, length us, event | category | flops | bytes accessed | tf_op | source)
XLA Modules:
  0.0 152.4 jit_solution(12980488828396278634)
XLA Ops:
  2.0 147.8 %shard_map.331 = (bf16[128,768]{1,0:T(8,128)(2,1)}, bf16[128,768]{1,0:T(8,128)(2,1)}, f32[24,128]{1,0:T(8,128)}, f32[24,2304]{1,0:T(8,128)}, f32[24,768]{1,0:T(8...) custom-call(s32[1]{0:T(128)S(6)} %copy.39.refs_0_, s32[1]{0:T(128)S(6)} %copy.38.refs_1_, ...), custom_call_target="tpu_custom_call" | custom-call | tf_op jit(solution)/shard_map/pallas_call | solution.py:1297
  149.7 2.5 %shard_map.332 = (bf16[128,768]{1,0:T(8,128)(2,1)}, bf16[128,768]{1,0:T(8,128)(2,1)}, f32[24,2304]{1,0:T(8,128)}, f32[24,768]{1,0:T(8,128)}, f32[24,3072]{1,0:T(...) custom-call(f32[24,128]{1,0:T(8,128)} %get-tuple-element.44.refs_0_,, ...), custom_call_target="tpu_custom_call" | custom-call | tf_op jit(solution)/shard_map/pallas_call | solution.py:1169

commit v6 on v5

--- a/solution.py
+++ b/solution.py
@@ -322,9 +322,6 @@
             sems.copy(mine, own, place.at(z=place.z_of(step)), sent, came[step - 1])
             for step in range(1, Z_SIZE)
         ]
-        last_z = Z_SIZE - 1
-        self.relay_up = sems.copy(part(0, y, x), part(0, y, x), place.at(z=last_z), sent, came[last_z - 1])
-        self.relay_down = sems.copy(part(last_z, y, x), part(last_z, y, x), place.at(z=0), sent, came[0])
         line = part(every, y, x)
         mid_line = part(every, 1 - y, x) if x_last else part(every, y, 1 - x)
         far_line = part(every, y, 1 - x) if x_last else part(every, 1 - y, x)
@@ -348,8 +345,7 @@
         self.all_last = sems.total(far_line, last_came)
         self.all_core = sems.total(slots.at[:, :, 1 - c, :, :, cols], core_came)
         flat = slots.reshape((8 * Z_SIZE * groups,) + slots.shape[4:])
-        self.outer_sent = sems.total(flat.at[pl.ds(0, (8 * Z_SIZE - 2) * groups), :, cols], sent)
-        self.inner_sent = sems.total(flat.at[:, :, cols], sent)
+        self.all_sent = sems.total(flat.at[pl.ds(0, (8 * Z_SIZE - 1) * groups), :, cols], sent)
 
     def begin_own(self):
         self.local.start()
@@ -357,49 +353,28 @@
         self.own_last.start()
 
     def begin_z(self):
-        up, across, down = self.along_z
-
-        @pl.when(self.z != Z_SIZE - 1)
-        def _():
-            up.start()
-
-        @pl.when(self.z != 0)
-        def _():
-            down.start()
-
-        across.start()
+        for copy in self.along_z:
+            copy.start()
 
     def pass_on(self, number):
         self.line_mid[number].start()
         self.line_last[number].start()
 
     def second(self):
-        up, across, down = self.along_z
-        across.wait_recv()
-
-        @pl.when(self.z == Z_SIZE - 2)
-        def _():
-            self.relay_up.start()
-
-        @pl.when(self.z == 1)
-        def _():
-            self.relay_down.start()
-
-        self.pass_on(1)
+
+        def take(number):
+            self.along_z[number].wait_recv()
+            self.pass_on(number)
 
         @pl.when(self.z >= Z_SIZE // 2)
         def _():
-            up.wait_recv()
-            self.pass_on(0)
-            down.wait_recv()
-            self.pass_on(2)
+            for number in range(Z_SIZE - 1):
+                take(number)
 
         @pl.when(self.z < Z_SIZE // 2)
         def _():
-            down.wait_recv()
-            self.pass_on(2)
-            up.wait_recv()
-            self.pass_on(0)
+            for number in reversed(range(Z_SIZE - 1)):
+                take(number)
 
         self.local.wait()
         self.line_core.start()
@@ -419,15 +394,7 @@
         self.all_core.wait_recv()
 
     def settle(self):
-        inner = (self.z - 1) * (Z_SIZE - 2 - self.z) >= 0
-
-        @pl.when(inner)
-        def _():
-            self.inner_sent.wait_send()
-
-        @pl.when(jnp.logical_not(inner))
-        def _():
-            self.outer_sent.wait_send()
+        self.all_sent.wait_send()
 
 
 class GatherLate(Gather):
@@ -926,7 +893,6 @@
     each(get_fc1[2:], Gather.second)
     each(get_qkv, Gather.fourth)
     each(get_fc1[:2], Gather.third)
-    each(get_fc2[:2], Gather.second)
     each(get_qkv, Gather.arrive)
 
     step = 2 * LANES
@@ -947,13 +913,13 @@
     def look(first, last):
         attend(s.q, s.kv, s.diag, s.probs, s.mixed, width, count, offset, (first, last))
 
+    each(get_fc1[2:], Gather.third)
+    each(get_fc2[:2], Gather.second)
     each(get_proj, Gather.fourth)
     look(0, 2)
-    each(get_fc1[2:], Gather.third)
     look(2, 4)
     each(get_fc1[:2], Gather.fourth)
     look(4, PAIRS)
-    each(get_fc2[:2], Gather.third)
     s.mixedt[...] = s.mixed[...].T
     each(get_proj, Gather.arrive)
 
@@ -969,6 +935,7 @@
     s.r2[...] = jnp.broadcast_to(inv_std, s.r2.shape)
     s.h2[...] = (normed * line(GAIN_TWO) + line(SHIFT_TWO)).astype(BF16)
     s.h2t[...] = s.h2[...].T
+    each(get_fc2[:2], Gather.third)
     each(get_fc1[2:], Gather.fourth)
     each(get_fc1, Gather.arrive)
 
@@ -982,6 +949,7 @@
         s.ut[cols, :] = low.T
         s.slope[:, cols] = gate + act * jnp.exp(act * act * -0.5) * 0.3989422804014327
 
+    each(get_fc2, Gather.fourth)
     deep = 8 * hidden_shard
     for chunk, (first, size, _) in zip(put_fc2, fc2_cuts(model)):
 
@@ -993,7 +961,6 @@
             view[number, :, :, cols] = sums.reshape(8, hidden_shard, size).astype(BF16)
 
         chunk.begin()
-    each(get_fc2, Gather.fourth)
     each(put_fc2, Reduce.add_core)
     each(get_fc2, Gather.arrive)
 

time: 154 us -> 150 us (0.974); the launches traced: 152 us -> 150 us
  Pallas kernels: 150 us -> 148 us
    pallas_call x1, Pallas kernels: 148 us -> 146 us  [run_layer(): pl.pallas_call(partial(layer_kernel, names, row_span), out_shape=tuple((j...]
where the time goes in v6:
time: 150 us
  Pallas kernels  148 us (99%)
  between operations  2.12 us (1%)
    pallas_call x1, Pallas kernels, run_layer(): pl.pallas_call(partial(layer_kernel, names, row_span), out_shape=tuple((j...  146 us

profile of v6, /device:TPU:0, one launch (start us, length us, event | category | flops | bytes accessed | tf_op | source)
XLA Modules:
  0.0 150.2 jit_solution(6552023832597795249)
XLA Ops:
  2.0 145.5 %shard_map.331 = (bf16[128,768]{1,0:T(8,128)(2,1)}, bf16[128,768]{1,0:T(8,128)(2,1)}, f32[24,128]{1,0:T(8,128)}, f32[24,2304]{1,0:T(8,128)}, f32[24,768]{1,0:T(8...) custom-call(s32[1]{0:T(128)S(6)} %copy.39.refs_0_, s32[1]{0:T(128)S(6)} %copy.38.refs_1_, ...), custom_call_target="tpu_custom_call" | custom-call | tf_op jit(solution)/shard_map/pallas_call | solution.py:1264
  147.5 2.5 %shard_map.332 = (bf16[128,768]{1,0:T(8,128)(2,1)}, bf16[128,768]{1,0:T(8,128)(2,1)}, f32[24,2304]{1,0:T(8,128)}, f32[24,768]{1,0:T(8,128)}, f32[24,3072]{1,0:T(...) custom-call(f32[24,128]{1,0:T(8,128)} %get-tuple-element.44.refs_0_,, ...), custom_call_target="tpu_custom_call" | custom-call | tf_op jit(solution)/shard_map/pallas_call | solution.py:1136

commit v7 on v6

--- a/solution.py
+++ b/solution.py
@@ -706,6 +706,13 @@
     return [(0, middle, turned), (middle, width - middle, turned)]
 
 
+def fc1_sum_cuts(width):
+    large, small = width // 4, width // 6
+    cuts = [(0, large), (large, large), (2 * large, small), (2 * large + small, small)]
+    cuts = [(start, size, False) for start, size in cuts]
+    return cuts + [(2 * large + 2 * small, width - 2 * large - 2 * small, True)]
+
+
 def fc2_cuts(width):
     part = width // 3
     return [(0, part, False), (part, part, False), (2 * part, width - 2 * part, True)]
@@ -820,9 +827,9 @@
     get_qkv = gather(s.w_qkv, s.wq, halves(3 * model, False))
     get_proj = gather(s.w_proj, s.wp, halves(model, False))
     get_fc1 = gather(s.w_fc1, s.w1, quarters(hidden))
-    get_fc2 = gather(s.w_fc2, s.w2, fc2_cuts(model))
+    get_fc2 = gather(s.w_fc2, s.w2, [(0, LANES, False), (LANES, 2 * LANES, False), (3 * LANES, model - 3 * LANES, True)])
     s.g_fc2, put_fc2 = reduce(s.o_fc2, fc2_cuts(model), None)
-    s.g_fc1, put_fc1 = reduce(s.o_fc1, quarters(hidden), None)
+    s.g_fc1, put_fc1 = reduce(s.o_fc1, fc1_sum_cuts(hidden), None)
     s.g_proj, put_proj = reduce(s.o_proj, halves(model, False), None)
     wide = QKV_COLS
     qkv_pieces = []
@@ -971,7 +978,7 @@
         grad_hidden = dot(s.dm[...], weight, NT)
         s.da[:, cols] = (grad_hidden * s.slope[:, cols]).astype(BF16)
 
-    for chunk, (first, size, _) in zip(put_fc1, quarters(hidden)):
+    for chunk, (first, size, _) in zip(put_fc1, fc1_sum_cuts(hidden)):
 
         @tiles(size // step, step)
         def _(number, start):
@@ -1242,7 +1249,7 @@
     chunks = 0
     for slot_rows, slot_width, dtype, cuts in (
         (hidden_shard, model, BF16, fc2_cuts(model)),
-        (shard, hidden, BF16, quarters(hidden)),
+        (shard, hidden, BF16, fc1_sum_cuts(hidden)),
         (shard, model, BF16, halves(model, False)),
         (shard, 3 * model, BF16, qkv_cuts(model)),
         (8, LANES, F32, [(0, LANES, False)]),

time: 150 us -> 148 us (0.987)
  Pallas kernels: 148 us -> 145 us
    pallas_call x1, Pallas kernels: 146 us -> 143 us  [run_layer(): pl.pallas_call(partial(layer_kernel, names, row_span), out_shape=tuple((j...]
where the time goes in v7:
time: 148 us; the launch traced here: 147 us
  Pallas kernels  145 us (98%)
  between operations  2.12 us (1%)
    pallas_call x1, Pallas kernels, run_layer(): pl.pallas_call(partial(layer_kernel, names, row_span), out_shape=tuple((j...  143 us

profile of v7, /device:TPU:0, one launch (start us, length us, event | category | flops | bytes accessed | tf_op | source)
XLA Modules:
  0.0 147.4 jit_solution(18153379031442842279)
XLA Ops:
  2.0 142.7 %shard_map.331 = (bf16[128,768]{1,0:T(8,128)(2,1)}, bf16[128,768]{1,0:T(8,128)(2,1)}, f32[24,128]{1,0:T(8,128)}, f32[24,2304]{1,0:T(8,128)}, f32[24,768]{1,0:T(8...) custom-call(s32[1]{0:T(128)S(6)} %copy.39.refs_0_, s32[1]{0:T(128)S(6)} %copy.38.refs_1_, ...), custom_call_target="tpu_custom_call" | custom-call | tf_op jit(solution)/shard_map/pallas_call | solution.py:1271
  144.7 2.5 %shard_map.332 = (bf16[128,768]{1,0:T(8,128)(2,1)}, bf16[128,768]{1,0:T(8,128)(2,1)}, f32[24,2304]{1,0:T(8,128)}, f32[24,768]{1,0:T(8,128)}, f32[24,3072]{1,0:T(...) custom-call(f32[24,128]{1,0:T(8,128)} %get-tuple-element.44.refs_0_,, ...), custom_call_target="tpu_custom_call" | custom-call | tf_op jit(solution)/shard_map/pallas_call | solution.py:1143
